TPU v7x, 32 devices: a whole 2x2x4 slice. The times are simulated.
32 devices in a mesh: dp: 8 (over y, x, core), tensor: 4 (over z).
Axes of the slice: x: 2, y: 2, z: 4, core: 2. Of those that a mesh axis runs over, the one named last changes fastest.
Arguments:
- hidden_in: bfloat16 [8192, 768], P(('dp', 'tensor')), may hold values from -6 to 6
- prev_logits: float32 [8192, 12], P('dp'), may hold values from -6 to 6
- routes: int32 [2, 8192, 2], P(None, 'dp'), may hold values from 0 to 11, all different within a row; in each aligned block of 1024 rows (0 to 1023, 1024 to 2047, ..., all dimensions but the last counted through in order) at most 256 rows name the same one
- span_starts: int32 [8, 2], P('dp'), may hold values from 0 to 768, as said below
- attn_norm: bfloat16 [2, 768], P(None, ('dp', 'tensor')), may hold values from 0.5 to 1.5
- qkv_weight: bfloat16 [2, 768, 3, 768], P(None, 'dp', None, 'tensor'), may hold values from -0.21875 to 0.21875
- out_weight: bfloat16 [2, 768, 768], P(None, 'tensor', 'dp'), may hold values from -0.875 to 0.875
- moe_norm: bfloat16 [2, 768], P(None, ('dp', 'tensor')), may hold values from 0.5 to 1.5
- router: bfloat16 [2, 768, 12], P(None, ('dp', 'tensor')), may hold values from -0.109375 to 0.109375
- gate_mix: bfloat16 [2, 12, 12], replicated, may hold values from -0.875 to 0.875
- const_vec: bfloat16 [2, 2, 768], P(None, None, ('dp', 'tensor')), may hold values from -6 to 6
- const_mix: bfloat16 [2, 2, 768, 2], P(None, None, ('dp', 'tensor')), may hold values from -0.21875 to 0.21875
- up_weight: bfloat16 [2, 8, 768, 2, 2048], P(None, None, 'dp', None, 'tensor'), may hold values from -0.21875 to 0.21875
- down_weight: bfloat16 [2, 8, 2048, 768], P(None, None, 'tensor', 'dp'), may hold values from -0.25 to 0.25
- out_grad: bfloat16 [8192, 768], P(('dp', 'tensor')), may hold values from -6 to 6
Outputs:
- hidden_out: float32 [8192, 768], P(('dp', 'tensor'))
- in_grad: float32 [8192, 768], P(('dp', 'tensor'))
- attn_norm_grad: float32 [2, 768], P(None, ('dp', 'tensor'))
- qkv_grad: float32 [2, 768, 3, 768], P(None, 'dp', None, 'tensor')
- out_weight_grad: float32 [2, 768, 768], P(None, 'tensor', 'dp')
- moe_norm_grad: float32 [2, 768], P(None, ('dp', 'tensor'))
- router_grad: float32 [2, 768, 12], P(None, ('dp', 'tensor'))
- gate_mix_grad: float32 [2, 12, 12], replicated
- const_vec_grad: float32 [2, 2, 768], P(None, None, ('dp', 'tensor'))
- const_mix_grad: float32 [2, 2, 768, 2], P(None, None, ('dp', 'tensor'))
- up_grad: float32 [2, 8, 768, 2, 2048], P(None, None, 'dp', None, 'tensor')
- down_grad: float32 [2, 8, 2048, 768], P(None, None, 'tensor', 'dp')
Inputs may be any that keep to these rules, and one draw needn't show every extreme that they name: `routes`: numbers below 8 are feed-forward experts, 8 the zero expert, 9 the copy expert, 10 and 11 the constant experts. A token's two numbers differ, and in every layer no number is named by more than 256 tokens of one sequence. Span k of a sequence covers positions span_starts to span_starts + 255, all within positions k * 512 to (k + 1) * 512 - 1.
All inputs are finite; a program needn't handle non-finite values.
Results may differ from a plain program's by a relative error of at most 0.035.
Values may be sent and summed in bfloat16 or wider, within the bound.
A program may use at most 384 MiB of HBM per device.

v0:
```python
import jax
import jax.numpy as jnp
from jax import lax
from jax.sharding import PartitionSpec as P

HEAD = 64
EXPERTS = 8
NEXP = 12
TOPK = 2
PIC = 256


EPS = 1e-06
HIGH = lax.Precision.HIGHEST


def span_marks(starts, seq_len):
    places = jnp.arange(seq_len, dtype=jnp.int32)
    inside = (places[:, None] >= starts[None, :]) & (places[:, None] < starts[None, :] + PIC)
    labels = jnp.arange(1, starts.shape[0] + 1, dtype=jnp.int32)
    return jnp.sum(jnp.where(inside, labels[None, :], 0), axis=1, dtype=jnp.int32)


def allowed_keys(start_row, span_ids, block_rows):
    places = jnp.arange(span_ids.shape[0], dtype=jnp.int32)
    query_pos = start_row + jnp.arange(block_rows, dtype=jnp.int32)
    query_ids = lax.dynamic_slice_in_dim(span_ids, start_row, block_rows, 0)
    causal = places[None, :] <= query_pos[:, None]
    picture = (query_ids[:, None] == span_ids[None, :]) & (query_ids[:, None] > 0)
    return causal | picture


def block_scores(block_q, key_rows, start_row, span_ids, block_rows, factor):
    scores = (
        jnp.einsum("qhe,khe->hqk", block_q, key_rows, preferred_element_type=jnp.float32) * factor
    )
    return jnp.where(allowed_keys(start_row, span_ids, block_rows)[None], scores, -1e30)


def attend_forward(triple, span_ids, block_rows):
    queries, key_rows, value_rows = (triple[0], triple[1], triple[2])
    factor = queries.shape[2] ** (-0.5)

    def one_block(block_at):
        start_row = block_at * block_rows
        block_q = lax.dynamic_slice_in_dim(queries, start_row, block_rows, 0)
        scores = block_scores(block_q, key_rows, start_row, span_ids, block_rows, factor)
        row_max = jnp.max(scores, axis=-1, keepdims=True)
        exp_rows = jnp.exp(scores - row_max)
        row_sum = jnp.sum(exp_rows, axis=-1, keepdims=True)
        attn_probs = (exp_rows / row_sum).astype(jnp.bfloat16)
        attended = jnp.einsum(
            "hqk,khe->qhe", attn_probs, value_rows, preferred_element_type=jnp.float32
        )
        return (attended.astype(jnp.bfloat16), (row_max + jnp.log(row_sum))[:, :, 0])

    outputs, log_sums = lax.map(
        one_block, jnp.arange(queries.shape[0] // block_rows, dtype=jnp.int32)
    )
    return (outputs.reshape(queries.shape[0], -1), log_sums)


def attend_backward(triple, span_ids, block_rows, log_sums, grad_att):
    queries, key_rows, value_rows = (triple[0], triple[1], triple[2])
    factor = queries.shape[2] ** (-0.5)

    def one_step(carry, block_at):
        grad_keys, grad_values = carry
        start_row = block_at * block_rows
        block_q = lax.dynamic_slice_in_dim(queries, start_row, block_rows, 0)
        block_g = lax.dynamic_slice_in_dim(grad_att, start_row, block_rows, 0)
        scores = block_scores(block_q, key_rows, start_row, span_ids, block_rows, factor)
        attn_probs = jnp.exp(scores - log_sums[block_at][:, :, None])
        low_probs = attn_probs.astype(jnp.bfloat16)
        grad_values = grad_values + jnp.einsum(
            "hqk,qhe->khe", low_probs, block_g, preferred_element_type=jnp.float32
        )
        grad_probs = jnp.einsum(
            "qhe,khe->hqk", block_g, value_rows, preferred_element_type=jnp.float32
        )
        inner_sum = jnp.sum(attn_probs * grad_probs, axis=-1, keepdims=True)
        grad_scores = (attn_probs * (grad_probs - inner_sum)).astype(jnp.bfloat16)
        grad_q = (
            jnp.einsum("hqk,khe->qhe", grad_scores, key_rows, preferred_element_type=jnp.float32)
            * factor
        )
        grad_keys = (
            grad_keys
            + jnp.einsum("hqk,qhe->khe", grad_scores, block_q, preferred_element_type=jnp.float32)
            * factor
        )
        return ((grad_keys, grad_values), grad_q)

    zero_rows = jnp.zeros(queries.shape, jnp.float32)
    carried, grad_qs = lax.scan(
        one_step,
        (zero_rows, zero_rows),
        jnp.arange(queries.shape[0] // block_rows, dtype=jnp.int32),
    )
    return jnp.stack([grad_qs.reshape(queries.shape), carried[0], carried[1]]).astype(jnp.bfloat16)


def dispatch(route_ids, capacity):
    flat_ids = route_ids.reshape(-1)
    hit_table = (flat_ids[:, None] == jnp.arange(NEXP, dtype=jnp.int32)[None, :]).astype(jnp.int32)
    slots = jnp.sum(
        (jnp.cumsum(hit_table, axis=0, dtype=jnp.int32) - 1) * hit_table, axis=1, dtype=jnp.int32
    )
    is_ffn = flat_ids < EXPERTS
    target = jnp.where(is_ffn, flat_ids * capacity + slots, EXPERTS * capacity)
    pick_ids = jnp.arange(flat_ids.shape[0], dtype=jnp.int32)
    owner_ids = jnp.zeros((EXPERTS * capacity,), jnp.int32).at[target].set(pick_ids, mode="drop")
    filled = jnp.zeros((EXPERTS * capacity,), jnp.float32).at[target].set(1.0, mode="drop")
    return (is_ffn, target, owner_ids, filled)


def norm_rows(values, gain):
    scale_rows = lax.rsqrt(jnp.mean(values * values, axis=-1, keepdims=True) + EPS)
    return (values * scale_rows * gain, scale_rows)


def norm_back(values, scale_rows, gain, grad_top):
    unit_rows = values * scale_rows
    grad_gain = jnp.sum(grad_top * unit_rows, axis=0)
    grad_unit = grad_top * gain
    grad_below = scale_rows * (
        grad_unit - unit_rows * jnp.mean(grad_unit * unit_rows, axis=-1, keepdims=True)
    )
    return (grad_below, grad_gain)


def spread_rows(values):
    return lax.all_gather(values, "tensor", axis=0, tiled=True)


def spread_grads(values):
    return lax.all_gather(values, "tensor", axis=0, tiled=True)


def collect_rows(values):
    return lax.psum_scatter(
        values.astype(jnp.bfloat16), "tensor", scatter_dimension=0, tiled=True
    ).astype(jnp.float32)


def collect_grads(values):
    return lax.psum_scatter(
        values.astype(jnp.bfloat16), "tensor", scatter_dimension=0, tiled=True
    ).astype(jnp.float32)


def layer_weights(qkv_weight, out_weight, up_weight, down_weight, layer_at):
    return (
        lax.all_gather(qkv_weight[layer_at], "dp", axis=0, tiled=True),
        lax.all_gather(out_weight[layer_at], "dp", axis=1, tiled=True),
        lax.all_gather(up_weight[layer_at], "dp", axis=1, tiled=True),
        lax.all_gather(down_weight[layer_at], "dp", axis=2, tiled=True),
    )


def weights_again(qkv_weight, out_weight, up_weight, down_weight, layer_at):
    return (
        lax.all_gather(qkv_weight[layer_at], "dp", axis=0, tiled=True),
        lax.all_gather(out_weight[layer_at], "dp", axis=1, tiled=True),
        lax.all_gather(up_weight[layer_at], "dp", axis=1, tiled=True),
        lax.all_gather(down_weight[layer_at], "dp", axis=2, tiled=True),
    )


def shards(
    hidden_in,
    prev_logits,
    routes,
    span_starts,
    attn_norm,
    qkv_weight,
    out_weight,
    moe_norm,
    router,
    gate_mix,
    const_vec,
    const_mix,
    up_weight,
    down_weight,
    out_grad,
):
    layers = qkv_weight.shape[0]
    own_rows = hidden_in.shape[0]
    seq_len = own_rows * lax.axis_size("tensor")
    offset = lax.axis_index("tensor") * own_rows
    block_rows = min(512, seq_len)
    capacity = seq_len // 4
    heads_local = qkv_weight.shape[3] // HEAD
    attn_gains, moe_gains, router_full, const_vecs, const_mixes = (
        lax.all_gather(attn_norm, ("dp", "tensor"), axis=1, tiled=True),
        lax.all_gather(moe_norm, ("dp", "tensor"), axis=1, tiled=True),
        lax.all_gather(router, ("dp", "tensor"), axis=1, tiled=True),
        lax.all_gather(const_vec, ("dp", "tensor"), axis=2, tiled=True),
        lax.all_gather(const_mix, ("dp", "tensor"), axis=2, tiled=True),
    )
    attn_gains = attn_gains.astype(jnp.float32)
    moe_gains = moe_gains.astype(jnp.float32)
    const_vecs = const_vecs.astype(jnp.float32)
    span_ids = span_marks(span_starts[0], seq_len)
    hidden = hidden_in.astype(jnp.float32)
    previous = prev_logits
    stored = []
    for layer_at in range(layers):
        triple_w, w_out, w_up, w_down = layer_weights(
            qkv_weight, out_weight, up_weight, down_weight, layer_at
        )
        normed, attn_scale = norm_rows(hidden, attn_gains[layer_at])
        attn_in = spread_rows(normed.astype(jnp.bfloat16))
        triple = jnp.einsum(
            "sd,dcf->csf", attn_in, triple_w, preferred_element_type=jnp.float32
        ).astype(jnp.bfloat16)
        triple = triple.reshape(3, seq_len, heads_local, HEAD)
        attended, log_sums = attend_forward(triple, span_ids, block_rows)
        attn_done = hidden + collect_rows(
            jnp.dot(attended, w_out, preferred_element_type=jnp.float32)
        )
        moe_pre, moe_scale = norm_rows(attn_done, moe_gains[layer_at])
        moe_low = moe_pre.astype(jnp.bfloat16)
        moe_all = spread_rows(moe_low)
        w_mix = gate_mix[layer_at].astype(jnp.float32)
        logits = jnp.dot(
            moe_all, router_full[layer_at], preferred_element_type=jnp.float32
        ) + jnp.dot(previous, w_mix, precision=HIGH)
        route_ids = routes[layer_at]
        gate_pair = jax.nn.softmax(jnp.take_along_axis(logits, route_ids, axis=1), axis=1)
        is_ffn, target, owner_ids, filled = dispatch(route_ids, capacity)
        expert_in = moe_all[owner_ids // 2].reshape(EXPERTS, capacity, -1)
        gate_up = jnp.einsum("ecd,edgf->ecgf", expert_in, w_up, preferred_element_type=jnp.float32)
        swiglu = (jax.nn.silu(gate_up[:, :, 0]) * gate_up[:, :, 1]).astype(jnp.bfloat16)
        expert_rows = jnp.einsum(
            "ecf,efd->ecd", swiglu, w_down, preferred_element_type=jnp.float32
        ).reshape(EXPERTS * capacity, -1)
        picked = expert_rows[jnp.where(is_ffn, target, 0)].reshape(seq_len, TOPK, -1)
        ffn_mask = is_ffn.reshape(seq_len, TOPK)
        routed = collect_rows(jnp.sum((gate_pair * ffn_mask)[:, :, None] * picked, axis=1))
        own_gates = lax.dynamic_slice_in_dim(gate_pair, offset, own_rows, 0)
        own_route = lax.dynamic_slice_in_dim(route_ids, offset, own_rows, 0)
        moe_own = moe_low.astype(jnp.float32)
        copy_gate = jnp.sum(own_gates * (own_route == EXPERTS + 1), axis=1)
        side_sum = copy_gate[:, None] * moe_own
        const_parts = []
        for const_at in range(2):
            const_gate = jnp.sum(own_gates * (own_route == EXPERTS + 2 + const_at), axis=1)
            const_alpha = jax.nn.softmax(
                jnp.dot(
                    moe_low, const_mixes[layer_at, const_at], preferred_element_type=jnp.float32
                ),
                axis=1,
            )
            const_out = (
                const_alpha[:, 0:1] * moe_own
                + const_alpha[:, 1:2] * const_vecs[layer_at, const_at][None, :]
            )
            side_sum = side_sum + const_gate[:, None] * const_out
            const_parts.append((const_gate, const_alpha, const_out))
        stored.append(
            {
                "weights": (triple_w, w_out, w_up, w_down),
                "hidden": hidden,
                "attn_scale": attn_scale,
                "attn_in": attn_in,
                "triple": triple,
                "attended": attended,
                "log_sums": log_sums,
                "attn_done": attn_done,
                "moe_scale": moe_scale,
                "moe_all": moe_all,
                "moe_own": moe_own,
                "previous": previous,
                "route_ids": route_ids,
                "gate_pair": gate_pair,
                "target": target,
                "owner_ids": owner_ids,
                "filled": filled,
                "ffn_mask": ffn_mask,
                "expert_in": expert_in,
                "gate_up": gate_up,
                "swiglu": swiglu,
                "picked": picked,
                "own_route": own_route,
                "copy_gate": copy_gate,
                "const_parts": const_parts,
                "w_mix": w_mix,
            }
        )
        hidden = attn_done + routed + side_sum
        previous = logits
    grad_hidden = out_grad.astype(jnp.float32)
    grad_prev = jnp.zeros((seq_len, NEXP), jnp.float32)
    big_parts = [None] * layers
    gain_attn = [None] * layers
    gain_moe = [None] * layers
    router_parts = [None] * layers
    cvec_parts = [None] * layers
    cmix_parts = [None] * layers
    mix_parts = [None] * layers
    for layer_at in reversed(range(layers)):
        saved = stored[layer_at]
        triple_w, w_out, w_up, w_down = weights_again(
            qkv_weight, out_weight, up_weight, down_weight, layer_at
        )
        gate_pair = saved["gate_pair"]
        owner_ids = saved["owner_ids"]
        grad_out_all = spread_grads(grad_hidden.astype(jnp.bfloat16))
        slot_gate = gate_pair.reshape(-1)[owner_ids] * saved["filled"]
        grad_expert = (
            (slot_gate[:, None] * grad_out_all[owner_ids // 2])
            .astype(jnp.bfloat16)
            .reshape(EXPERTS, capacity, -1)
        )
        grad_inner = jnp.einsum(
            "ecd,efd->ecf", grad_expert, w_down, preferred_element_type=jnp.float32
        )
        grad_down = jnp.einsum(
            "ecf,ecd->efd", saved["swiglu"], grad_expert, preferred_element_type=jnp.float32
        )
        gate_part = saved["gate_up"][:, :, 0]
        up_part = saved["gate_up"][:, :, 1]
        sig_gate = jax.nn.sigmoid(gate_part)
        grad_gate = grad_inner * up_part * sig_gate * (1.0 + gate_part * (1.0 - sig_gate))
        grad_upv = grad_inner * gate_part * sig_gate
        grad_both = jnp.stack([grad_gate, grad_upv], axis=2).astype(jnp.bfloat16)
        grad_in_exp = jnp.einsum(
            "ecgf,edgf->ecd", grad_both, w_up, preferred_element_type=jnp.float32
        )
        grad_upw = jnp.einsum(
            "ecd,ecgf->edgf", saved["expert_in"], grad_both, preferred_element_type=jnp.float32
        )
        grad_mixed = (
            jnp.zeros((seq_len, grad_in_exp.shape[2]), jnp.float32)
            .at[owner_ids // 2]
            .add(grad_in_exp.reshape(EXPERTS * capacity, -1))
        )
        grad_gates = (
            jnp.sum(saved["picked"] * grad_out_all[:, None, :], axis=-1) * saved["ffn_mask"]
        )
        moe_own = saved["moe_own"]
        own_route = saved["own_route"]
        own_gate_grad = (own_route == EXPERTS + 1) * jnp.sum(
            grad_hidden * moe_own, axis=1, keepdims=True
        )
        grad_own_mixed = saved["copy_gate"][:, None] * grad_hidden
        cvec_list = []
        cmix_list = []
        for const_at in range(2):
            const_gate, const_alpha, const_out = saved["const_parts"][const_at]
            own_gate_grad = own_gate_grad + (own_route == EXPERTS + 2 + const_at) * jnp.sum(
                grad_hidden * const_out, axis=1, keepdims=True
            )
            weighted = const_gate[:, None] * grad_hidden
            grad_own_mixed = grad_own_mixed + const_alpha[:, 0:1] * weighted
            grad_alpha = jnp.stack(
                [
                    jnp.sum(weighted * moe_own, axis=1),
                    jnp.sum(weighted * const_vecs[layer_at, const_at][None, :], axis=1),
                ],
                axis=1,
            )
            grad_logit = const_alpha * (
                grad_alpha - jnp.sum(const_alpha * grad_alpha, axis=1, keepdims=True)
            )
            cmix_list.append(jnp.dot(moe_own.T, grad_logit, precision=HIGH))
            grad_own_mixed = grad_own_mixed + jnp.dot(
                grad_logit, const_mixes[layer_at, const_at].astype(jnp.float32).T, precision=HIGH
            )
            cvec_list.append(jnp.sum(weighted * const_alpha[:, 1:2], axis=0))
        merged = lax.dynamic_slice_in_dim(grad_gates, offset, own_rows, 0) + own_gate_grad
        grad_gates = lax.dynamic_update_slice_in_dim(grad_gates, merged, offset, 0)
        grad_pair = gate_pair * (
            grad_gates - jnp.sum(gate_pair * grad_gates, axis=1, keepdims=True)
        )
        expert_codes = jnp.arange(NEXP, dtype=jnp.int32)
        grad_logits = (
            jnp.sum(
                (saved["route_ids"][:, :, None] == expert_codes[None, None, :])
                * grad_pair[:, :, None],
                axis=1,
            )
            + grad_prev
        )
        router_parts[layer_at] = jnp.dot(saved["moe_all"].T, grad_logits, precision=HIGH)
        mix_parts[layer_at] = jnp.dot(saved["previous"].T, grad_logits, precision=HIGH)
        grad_prev = jnp.dot(grad_logits, saved["w_mix"].T, precision=HIGH)
        grad_mixed = grad_mixed + jnp.dot(
            grad_logits, router_full[layer_at].astype(jnp.float32).T, precision=HIGH
        )
        grad_moe_in = collect_grads(grad_mixed) + grad_own_mixed
        grad_mid, gain_moe[layer_at] = norm_back(
            saved["attn_done"], saved["moe_scale"], moe_gains[layer_at], grad_moe_in
        )
        grad_mid = grad_mid + grad_hidden
        cvec_parts[layer_at] = jnp.stack(cvec_list)
        cmix_parts[layer_at] = jnp.stack(cmix_list)
        grad_att_all = spread_grads(grad_mid.astype(jnp.bfloat16))
        grad_att = jnp.einsum(
            "sd,fd->sf", grad_att_all, w_out, preferred_element_type=jnp.float32
        ).astype(jnp.bfloat16)
        grad_outw = jnp.einsum(
            "sf,sd->fd", saved["attended"], grad_att_all, preferred_element_type=jnp.float32
        )
        grad_triple = attend_backward(
            saved["triple"],
            span_ids,
            block_rows,
            saved["log_sums"],
            grad_att.reshape(seq_len, heads_local, HEAD),
        ).reshape(3, seq_len, -1)
        grad_attn_in = collect_grads(
            jnp.einsum("csf,dcf->sd", grad_triple, triple_w, preferred_element_type=jnp.float32)
        )
        grad_qkvw = jnp.einsum(
            "sd,csf->dcf", saved["attn_in"], grad_triple, preferred_element_type=jnp.float32
        )
        grad_before, gain_attn[layer_at] = norm_back(
            saved["hidden"], saved["attn_scale"], attn_gains[layer_at], grad_attn_in
        )
        grad_hidden = grad_before + grad_mid
        big_parts[layer_at] = (grad_qkvw, grad_outw, grad_upw, grad_down)
    qkv_stack = jnp.stack([item[0] for item in big_parts])
    outw_stack = jnp.stack([item[1] for item in big_parts])
    up_stack = jnp.stack([item[2] for item in big_parts])
    down_stack = jnp.stack([item[3] for item in big_parts])
    qkv_stack, outw_stack, up_stack, down_stack = (
        lax.psum_scatter(qkv_stack, "dp", scatter_dimension=1, tiled=True),
        lax.psum_scatter(outw_stack, "dp", scatter_dimension=2, tiled=True),
        lax.psum_scatter(up_stack, "dp", scatter_dimension=2, tiled=True),
        lax.psum_scatter(down_stack, "dp", scatter_dimension=3, tiled=True),
    )
    small_sums = (
        lax.psum_scatter(jnp.stack(gain_attn), ("dp", "tensor"), scatter_dimension=1, tiled=True),
        lax.psum_scatter(jnp.stack(gain_moe), ("dp", "tensor"), scatter_dimension=1, tiled=True),
        lax.psum_scatter(
            jnp.stack(router_parts), ("dp", "tensor"), scatter_dimension=1, tiled=True
        ),
        lax.psum_scatter(jnp.stack(cvec_parts), ("dp", "tensor"), scatter_dimension=2, tiled=True),
        lax.psum_scatter(jnp.stack(cmix_parts), ("dp", "tensor"), scatter_dimension=2, tiled=True),
    )
    mix_total = lax.psum(jnp.stack(mix_parts), ("dp", "tensor"))
    return (
        hidden,
        grad_hidden,
        small_sums[0],
        qkv_stack,
        outw_stack,
        small_sums[1],
        small_sums[2],
        mix_total,
        small_sums[3],
        small_sums[4],
        up_stack,
        down_stack,
    )


def solution(mesh):
    return jax.shard_map(
        shards,
        mesh=mesh,
        in_specs=(
            P(("dp", "tensor"), None),
            P("dp", None),
            P(None, "dp", None),
            P("dp", None),
            P(None, ("dp", "tensor")),
            P(None, "dp", None, "tensor"),
            P(None, "tensor", "dp"),
            P(None, ("dp", "tensor")),
            P(None, ("dp", "tensor"), None),
            P(),
            P(None, None, ("dp", "tensor")),
            P(None, None, ("dp", "tensor"), None),
            P(None, None, "dp", None, "tensor"),
            P(None, None, "tensor", "dp"),
            P(("dp", "tensor"), None),
        ),
        out_specs=(
            P(("dp", "tensor"), None),
            P(("dp", "tensor"), None),
            P(None, ("dp", "tensor")),
            P(None, "dp", None, "tensor"),
            P(None, "tensor", "dp"),
            P(None, ("dp", "tensor")),
            P(None, ("dp", "tensor"), None),
            P(),
            P(None, None, ("dp", "tensor")),
            P(None, None, ("dp", "tensor"), None),
            P(None, None, "dp", None, "tensor"),
            P(None, None, "tensor", "dp"),
        ),
        check_vma=False,
    )
```

profile of v0, /device:TPU:0, one launch (start us, length us, event | category | flops | bytes accessed | tf_op | source)
XLA Modules:
  0.0 2093.2 jit_solution(1854615634681716348)
XLA Ops:
  8.4 70.0 %all-gather.8 = bf16[32,24,2]{1,2,0:T(2,128)(2,1)S(1)} all-gather(bf16[1,24,2]{1,2,0:T(2,128)(2,1)} %bitcast.663), channel_id=1, replica_groups=mesh['dp'=8,'tensor'=4] {'dp','tensor'}, dimensions={0}, use_global_device_ids=true | all-gather | bytes 3168 | tf_op jit(solution)/shard_map/all_gather | solution.py:195
  119.6 22.6 %while.54 = (s32[]{:T(128)}, bf16[2,512,3,64]{1,3,2,0:T(8,128)(2,1)S(1)}, f32[2,3,512]{2,1,0:T(4,128)}, s32[2]{0:T(128)S(1)}, s32[1024]{0:T(1024)}, /*index=5*/b...) while((s32[]{:T(128)}, ...), condition=%wide.region_5.6_spmd, body=%wide.region_2.5_spmd.sunk | while | flops 423722496 | bytes 22222028 | solution.py:57
  145.3 67.1 %all-gather.9 = bf16[32,24,2]{1,2,0:T(2,128)(2,1)S(1)} all-gather(bf16[1,24,2]{1,2,0:T(2,128)(2,1)S(1)} %bitcast.664), channel_id=1, replica_groups=mesh['dp'=8,'tensor'=4] {'dp','tensor'}, dimensions={0}, use_global_device_ids=true | all-gather | bytes 3168 | tf_op jit(solution)/shard_map/all_gather | solution.py:196
  227.7 70.0 %all_gather.77 = bf16[2,768,12]{2,0,1:T(2,128)(2,1)S(1)} all-gather(bf16[2,24,12]{2,0,1:T(2,128)(2,1)S(1)} %copy.253), channel_id=1, replica_groups=mesh['dp'=8,'tensor'=4] {'dp','tensor'}, dimensions={1}, use_global_device_ids=true | all-gather | bytes 38016 | tf_op jit(solution)/shard_map/all_gather | solution.py:197
  425.2 74.0 %all_gather.81 = bf16[2,2,768]{1,0,2:T(2,128)(2,1)S(1)} all-gather(bf16[2,2,24]{1,0,2:T(2,128)(2,1)S(1)} %copy.262), channel_id=1, replica_groups=mesh['dp'=8,'tensor'=4] {'dp','tensor'}, dimensions={2}, use_global_device_ids=true | all-gather | bytes 6336 | tf_op jit(solution)/shard_map/all_gather | solution.py:198
  499.5 79.7 %all_gather.80 = bf16[2,2,768,2]{3,1,0,2:T(2,128)(2,1)S(1)} all-gather(bf16[2,2,24,2]{3,1,0,2:T(2,128)(2,1)S(1)} %copy.260), channel_id=1, replica_groups=mesh['dp'=8,'tensor'=4] {'dp','tensor'}, dimensions={2}, use_global_device_ids=true | all-gather | bytes 12672 | tf_op jit(solution)/shard_map/all_gather | solution.py:199
  662.3 32.3 %reduce-scatter.26.cloned.1.call-done = bf16[256,768]{1,0:T(8,128)(2,1)} async-done(((bf16[1024,768]{1,0:T(8,128)(2,1)}), bf16[256,768]{1,0:T(8,128)(2,1)}) %reduce-scatter.26.cloned.1.call-update) | async-done | bytes 393232 | tf_op jit(solution)/shard_map/reduce_scatter | solution.py:141
  745.1 33.6 %all-gather.45.cloned.1.call-done = bf16[1,8,512,768]{2,1,0,3:T(8,128)(2,1)} async-done(((bf16[1,8,512,96]{2,1,0,3:T(8,128)(2,1)}), bf16[1,8,512,768]{2,1,0,3:T(8,128)(2,1)}) %all-gather.45.cloned.1.call-update) | async-done | bytes 6291472 | tf_op jit(solution)/shard_map/all_gather | solution.py:157
  789.6 27.8 %all-gather.29.cloned.1.call-done = bf16[1024,768]{1,0:T(8,128)(2,1)} async-done(((bf16[256,768]{1,0:T(8,128)(2,1)}), bf16[1024,768]{1,0:T(8,128)(2,1)}) %all-gather.29.cloned.1.call-update) | async-done | bytes 1572880 | tf_op jit(solution)/shard_map/all_gather | solution.py:133
  860.2 29.8 %all-gather.43.cloned.1.call-done = bf16[1,8,768,2,512]{4,2,3,1,0:T(8,128)(2,1)} async-done(((bf16[1,8,96,2,512]{4,2,3,1,0:T(8,128)(2,1)}), bf16[1,8,768,2,512]{4,2,3,1,0:T(8,128)(2,1)}) %all-gather.43.cloned.1.call-update) | async-done | bytes 12582928 | tf_op jit(solution)/shard_map/all_gather | solution.py:156
  995.5 33.1 %reduce-scatter.30.cloned.1.call-done = bf16[256,768]{1,0:T(8,128)(2,1)} async-done(((bf16[1024,768]{1,0:T(8,128)(2,1)}), bf16[256,768]{1,0:T(8,128)(2,1)}) %reduce-scatter.30.cloned.1.call-update) | async-done | bytes 393232 | tf_op jit(solution)/shard_map/reduce_scatter | solution.py:147
  1031.9 33.2 %reduce-scatter.28.cloned.1.call-done = bf16[256,768]{1,0:T(8,128)(2,1)} async-done(((bf16[1024,768]{1,0:T(8,128)(2,1)}), bf16[256,768]{1,0:T(8,128)(2,1)}) %reduce-scatter.28.cloned.1.call-update) | async-done | bytes 393232 | tf_op jit(solution)/shard_map/reduce_scatter | solution.py:141
  1068.1 36.0 %all-gather.33.cloned.1.call-done = bf16[1024,768]{1,0:T(8,128)(2,1)} async-done(((bf16[256,768]{1,0:T(8,128)(2,1)}), bf16[1024,768]{1,0:T(8,128)(2,1)}) %all-gather.33.cloned.1.call-update) | async-done | bytes 1572880 | tf_op jit(solution)/shard_map/all_gather | solution.py:137
  1107.7 30.9 %while.56 = (s32[]{:T(128)}, f32[1024,3,64]{0,2,1:T(8,128)S(1)}, f32[1024,3,64]{0,2,1:T(8,128)}, bf16[2,512,3,64]{1,3,2,0:T(8,128)(2,1)}, s32[2]{0:T(128)S(1)}, ...) while((s32[]{:T(128)}, f32[1024,3,64]{0,2,1:T(8,128)S(1)}, ...), condition=%wide.region_63.65_spmd.clone, body=%wide.region_61.64_spmd.clone.sunk | while | flops 1033403904 | bytes 65861036 | solution.py:95
  1146.4 34.4 %reduce-scatter.32.cloned.1.call-done = bf16[256,768]{1,0:T(8,128)(2,1)} async-done(((bf16[1024,768]{1,0:T(8,128)(2,1)}), bf16[256,768]{1,0:T(8,128)(2,1)}) %reduce-scatter.32.cloned.1.call-update) | async-done | bytes 393232 | tf_op jit(solution)/shard_map/reduce_scatter | solution.py:147
  1297.6 32.3 %reduce-scatter.34.cloned.1.call-done = bf16[256,768]{1,0:T(8,128)(2,1)} async-done(((bf16[1024,768]{1,0:T(8,128)(2,1)}), bf16[256,768]{1,0:T(8,128)(2,1)}) %reduce-scatter.34.cloned.1.call-update) | async-done | bytes 393232 | tf_op jit(solution)/shard_map/reduce_scatter | solution.py:147
  1340.2 31.7 %all-gather.37.cloned.1.call-done = bf16[1024,768]{1,0:T(8,128)(2,1)} async-done(((bf16[256,768]{1,0:T(8,128)(2,1)}), bf16[1024,768]{1,0:T(8,128)(2,1)}) %all-gather.37.cloned.1.call-update) | async-done | bytes 1572880 | tf_op jit(solution)/shard_map/all_gather | solution.py:137
  1382.0 37.0 %while.57 = (s32[]{:T(128)}, f32[1024,3,64]{0,2,1:T(8,128)S(1)}, f32[1024,3,64]{0,2,1:T(8,128)}, bf16[2,512,3,64]{1,3,2,0:T(8,128)(2,1)S(1)}, s32[2]{0:T(128)S(1...) while((s32[]{:T(128)}, f32[1024,3,64]{0,2,1:T(8,128)S(1)}, ...), condition=%wide.region_84.86_spmd.clone, body=%wide.region_82.85_spmd.clone.sunk | while | flops 1033403904 | bytes 61142360 | solution.py:95
  1462.0 25.1 %copy.294 = f32[2,8,512,768]{2,1,0,3:T(8,128)} copy(f32[2,8,512,768]{3,2,1,0:T(8,128)} %pad_maximum_fusion.1) | data formatting | bytes 50331648 | tf_op jit(solution)/shard_map/stack | solution.py:427
  1517.2 35.1 %pad_maximum_fusion = f32[2,8,768,2,512]{4,2,3,1,0:T(8,128)} fusion(f32[1,8,768,2,512]{4,2,3,1,0:T(8,128)} %convolution_bitcast_fusion, f32[1,8,768,2,512]{4,2,3,1,0:T(8,128)} %convolution_bitcast_fusion.1), kind=kLoop, calls=%fused_computation.116 | loop fusion | flops 12582912 | bytes 100663296 | tf_op jit(solution)/shard_map/stack | solution.py:426
  1558.6 19.5 reduce-scatter.36.cloned.1.call-done
  1579.5 40.2 %all-reduce.5 = (f32[2,768]{1,0:T(2,128)S(1)}, f32[2,768]{1,0:T(2,128)S(1)}, f32[2,12,12]{1,2,0:T(8,128)S(1)}, f32[2,2,768]{2,1,0:T(2,128)S(1)}, f32[2,2,768,2]{2,3,1,0:T(2,128)S(1)}) all-reduce(f32[2,768]{1,0:T(2,128)S(1)} %get-tuple-element.587, ...), channel_id=18, replica_groups=mesh['dp'=8,'tensor'=4] {'dp','tensor'}, use_global_device_ids=true, to_apply=%region_89.91.clone | all-reduce | flops 12576 | bytes 100608
  1631.1 157.2 %reduce-scatter.40.cloned.1.call-done = f32[2,8,512,96]{2,1,0,3:T(8,128)} async-done(((f32[2,8,512,768]{2,1,0,3:T(8,128)}), f32[2,8,512,96]{2,1,0,3:T(8,128)}) %reduce-scatter.40.cloned.1.call-update) | async-done | bytes 3145744 | tf_op jit(solution)/shard_map/reduce_scatter | solution.py:432
  1793.7 282.4 %reduce-scatter.38.cloned.1.call-done = f32[2,8,96,2,512]{4,2,3,1,0:T(8,128)} async-done(((f32[2,8,768,2,512]{4,2,3,1,0:T(8,128)}), f32[2,8,96,2,512]{4,2,3,1,0:T(8,128)}) %reduce-scatter.38.cloned.1.call-update) | async-done | bytes 6291472 | tf_op jit(solution)/shard_map/reduce_scatter | solution.py:431
  (941 shorter events, 835.9 us)
Async XLA Ops:
  7.2 108.0 %all-gather.23.cloned.1.call-start = ((), (), s32[]{:S(2)}) async-start(), calls=%async_computation.12 | async-start | bytes 1966080 | tf_op jit(solution)/shard_map/all_gather | solution.py:133
  81.8 131.5 %reduce-scatter.22.cloned.1.call-start = ((), (), s32[]{:S(2)}) async-start(), calls=%async_computation.13 | async-start | bytes 1966080 | tf_op jit(solution)/shard_map/reduce_scatter | solution.py:141
  145.2 169.7 %all-gather.25.cloned.1.call-start = ((), (), s32[]{:S(2)}) async-start(), calls=%async_computation.14 | async-start | bytes 1966080 | tf_op jit(solution)/shard_map/all_gather | solution.py:133
  217.0 130.4 %all-gather.41.cloned.1.call-start = ((), (), s32[]{:S(2)}) async-start(), calls=%async_computation.31 | async-start | bytes 7077888 | tf_op jit(solution)/shard_map/all_gather | solution.py:157
  219.4 155.4 %all-gather.39.cloned.1.call-start = ((), (), s32[]{:S(2)}) async-start(), calls=%async_computation.30 | async-start | bytes 14155776 | tf_op jit(solution)/shard_map/all_gather | solution.py:156
  225.9 370.4 %reduce-scatter.24.cloned.1.call-start = ((), (), s32[]{:S(2)}) async-start(), calls=%async_computation.15 | async-start | bytes 1966080 | tf_op jit(solution)/shard_map/reduce_scatter | solution.py:141
  425.0 208.8 %all-gather.27.cloned.1.call-start = ((), (), s32[]{:S(2)}) async-start(), calls=%async_computation.16 | async-start | bytes 1966080 | tf_op jit(solution)/shard_map/all_gather | solution.py:133
  599.1 95.5 %reduce-scatter.26.cloned.1.call-start = ((), (), s32[]{:S(2)}) async-start(), calls=%async_computation.17 | async-start | bytes 1966080 | tf_op jit(solution)/shard_map/reduce_scatter | solution.py:141
  660.9 117.8 %all-gather.45.cloned.1.call-start = ((), (), s32[]{:S(2)}) async-start(), calls=%async_computation.33 | async-start | bytes 7077888 | tf_op jit(solution)/shard_map/all_gather | solution.py:157
  662.3 155.1 %all-gather.29.cloned.1.call-start = ((), (), s32[]{:S(2)}) async-start(), calls=%async_computation.18 | async-start | bytes 1966080 | tf_op jit(solution)/shard_map/all_gather | solution.py:133
  697.8 192.2 %all-gather.43.cloned.1.call-start = ((), (), s32[]{:S(2)}) async-start(), calls=%async_computation.32 | async-start | bytes 14155776 | tf_op jit(solution)/shard_map/all_gather | solution.py:156
  700.8 327.8 %reduce-scatter.30.cloned.1.call-start = ((), (), s32[]{:S(2)}) async-start(), calls=%async_computation.21 | async-start | bytes 1966080 | tf_op jit(solution)/shard_map/reduce_scatter | solution.py:147
  993.0 72.1 %reduce-scatter.28.cloned.1.call-start = ((), (), s32[]{:S(2)}) async-start(), calls=%async_computation.19 | async-start | bytes 1966080 | tf_op jit(solution)/shard_map/reduce_scatter | solution.py:141
  993.5 110.5 %all-gather.33.cloned.1.call-start = ((), (), s32[]{:S(2)}) async-start(), calls=%async_computation.22 | async-start | bytes 1966080 | tf_op jit(solution)/shard_map/all_gather | solution.py:137
  1068.0 112.8 %reduce-scatter.32.cloned.1.call-start = ((), (), s32[]{:S(2)}) async-start(), calls=%async_computation.23 | async-start | bytes 1966080 | tf_op jit(solution)/shard_map/reduce_scatter | solution.py:147
  1146.3 75.0 %all-gather.35.cloned.1.call-start = ((), (), s32[]{:S(2)}) async-start(), calls=%async_computation.24 | async-start | bytes 1966080 | tf_op jit(solution)/shard_map/all_gather | solution.py:137
  1185.4 144.5 %reduce-scatter.34.cloned.1.call-start = ((), (), s32[]{:S(2)}) async-start(), calls=%async_computation.25 | async-start | bytes 1966080 | tf_op jit(solution)/shard_map/reduce_scatter | solution.py:147
  1295.4 76.5 %all-gather.37.cloned.1.call-start = ((), (), s32[]{:S(2)}) async-start(), calls=%async_computation.26 | async-start | bytes 1966080 | tf_op jit(solution)/shard_map/all_gather | solution.py:137
  1335.9 219.3 %all-reduce.8.cloned.1.call-start = ((), (), s32[]{:S(2)}) async-start(), calls=%async_computation.36 | async-start | bytes 196608
  1340.2 216.5 %reduce-scatter.44.cloned.1.call-start = ((), (), s32[]{:S(2)}) async-start(), calls=%async_computation.35 | async-start | bytes 1327104
  1379.8 198.2 %reduce-scatter.36.cloned.1.call-start = ((), (), s32[]{:S(2)}) async-start(), calls=%async_computation.27 | async-start | bytes 1966080 | tf_op jit(solution)/shard_map/reduce_scatter | solution.py:147
  1423.6 204.9 %reduce-scatter.42.cloned.1.call-start = ((), (), s32[]{:S(2)}) async-start(), calls=%async_computation.34 | async-start | bytes 3981312
  1444.7 343.6 %reduce-scatter.40.cloned.1.call-start = ((), (), s32[]{:S(2)}) async-start(), calls=%async_computation.29 | async-start | bytes 28311552 | tf_op jit(solution)/shard_map/reduce_scatter | solution.py:432
  1487.1 589.0 %reduce-scatter.38.cloned.1.call-start = ((), (), s32[]{:S(2)}) async-start(), calls=%async_computation.28 | async-start | bytes 56623104 | tf_op jit(solution)/shard_map/reduce_scatter | solution.py:431
  (251 other events, 7051.3 us)
Sparse Core Ops, SparseCore 0:
  145.3 34.4 reduce-scatter.21
  217.1 36.1 all-gather.24
  255.6 45.4 all-gather.40
  302.8 71.9 all-gather.38
  425.1 39.1 reduce-scatter.23
  599.2 34.4 all-gather.26
  660.3 34.3 reduce-scatter.25
  696.2 35.8 all-gather.30
  734.4 44.2 all-gather.44
  780.3 37.0 all-gather.28
  819.1 70.7 all-gather.42
  993.1 35.4 reduce-scatter.29
  1030.8 34.2 reduce-scatter.27
  1068.2 35.8 all-gather.32
  1146.5 34.3 reduce-scatter.31
  1185.5 35.8 all-gather.34
  1295.5 34.3 reduce-scatter.33
  1336.0 35.8 all-gather.36
  1377.9 121.4 all-reduce.7
  1502.7 37.5 reduce-scatter.43
  1542.6 35.4 reduce-scatter.35
  1581.5 46.9 reduce-scatter.41
  1632.0 156.2 reduce-scatter.39
  1792.0 284.1 reduce-scatter.37
  (1 shorter events, 33.2 us)
where the time goes:
time: 2100 us; the launch traced here: 2090 us
  waiting for transfers between devices  837 us (40%)
  blocking collectives  447 us (21%)
  local copies, waits for them, and re-layouts  341 us (16%)
  other arithmetic  218 us (10%)
  matrix products  216 us (10%)
    reduce_scatter x1, waiting for transfers between devices, shards(): lax.psum_scatter(up_stack, 'dp', scatter_dimension=2, tiled=True)  282 us
    reduce_scatter x1, waiting for transfers between devices, shards(): lax.psum_scatter(down_stack, 'dp', scatter_dimension=3, tiled=True)  157 us
    reduce_scatter x4, waiting for transfers between devices, collect_grads(): lax.psum_scatter(values.astype(jnp.bfloat16), 'tensor', scatter_dimension...  119 us
    all_gather x4, waiting for transfers between devices, spread_grads(): return lax.all_gather(values, 'tensor', axis=0, tiled=True)  86.3 us
    all_gather x1, blocking collectives, shards(): lax.all_gather(const_mix, ('dp', 'tensor'), axis=2, tiled=True)  79.7 us
    all_gather x1, blocking collectives, shards(): lax.all_gather(const_vec, ('dp', 'tensor'), axis=2, tiled=True)  74 us
    all_gather x1, blocking collectives, shards(): lax.all_gather(router, ('dp', 'tensor'), axis=1, tiled=True)  70 us
    all_gather x1, blocking collectives, shards(): lax.all_gather(attn_norm, ('dp', 'tensor'), axis=1, tiled=True)  70 us
  transfers between devices with their start and end apart: 25, of which 19 were waited for; matrix products, arithmetic and copies ran while one was open for 20% of the time, Pallas kernels for 0%

commit v1 on v0

v1 whole, which is shorter than its diff:
```python
import functools

import jax
import jax.numpy as jnp
from jax import lax
from jax.experimental import pallas as pl
from jax.experimental.pallas import tpu as pltpu
from jax.sharding import PartitionSpec as P

HEAD = 64
EXPERTS = 8
NEXP = 12
TOPK = 2
PIC = 256
LANES = 128

EPS = 1e-06
HIGH = lax.Precision.HIGHEST
MESH = pl.DeviceIdType.MESH
F32 = jnp.float32
BF16 = jnp.bfloat16
VMEM_SPEC = pl.BlockSpec(memory_space=pltpu.VMEM)
VMEM_LIMIT = 60 * 1024 * 1024


def dot(a, b):
    return jnp.dot(a, b, preferred_element_type=F32)


def dot_nt(a, b):
    return lax.dot_general(a, b, (((1,), (1,)), ((), ())), preferred_element_type=F32)


def dot_tn(a, b):
    return lax.dot_general(a, b, (((0,), (0,)), ((), ())), preferred_element_type=F32)


def everyone_kernel(count, inner, reduce, x_ref, out_ref, *scratch):
    if reduce:
        land, send_sems, recv_sems = scratch
    else:
        land, (send_sems, recv_sems) = out_ref, scratch
    me = lax.axis_index("dp") * inner + lax.axis_index("tensor")

    def place(other):
        return (lax.div(other, inner), lax.rem(other, inner))

    barrier = pltpu.get_barrier_semaphore()

    def greet(step, carry):
        other = lax.rem(me + step, count)
        pl.semaphore_signal(barrier, inc=1, device_id=place(other), device_id_type=MESH)
        return carry

    lax.fori_loop(1, count, greet, 0)
    pl.semaphore_wait(barrier, count - 1)

    def copy_to(other):
        return pltpu.make_async_remote_copy(
            src_ref=x_ref.at[other] if reduce else x_ref,
            dst_ref=land.at[me],
            send_sem=send_sems.at[other],
            recv_sem=recv_sems.at[me],
            device_id=place(other),
            device_id_type=MESH,
        )

    def send(step, carry):
        copy_to(lax.rem(me + step, count)).start()
        return carry

    lax.fori_loop(1, count, send, 0)
    land[me] = x_ref[me] if reduce else x_ref[...]

    def finish(step, carry):
        other = lax.rem(me + count - step, count)
        pltpu.make_async_remote_copy(
            src_ref=x_ref.at[other] if reduce else x_ref,
            dst_ref=land.at[other],
            send_sem=send_sems.at[other],
            recv_sem=recv_sems.at[other],
            device_id=place(other),
            device_id_type=MESH,
        ).wait()
        return carry

    lax.fori_loop(1, count, finish, 0)
    if reduce:
        out_ref[...] = jnp.sum(land[...], axis=0)


def everyone(values, reduce, collective_id):
    inner = lax.axis_size("tensor")
    count = lax.axis_size("dp") * inner
    tail = values.shape[1:] if reduce else values.shape
    scratch = [pltpu.SemaphoreType.DMA((count,)), pltpu.SemaphoreType.DMA((count,))]
    if reduce:
        scratch = [pltpu.VMEM((count,) + tail, values.dtype)] + scratch
    return pl.pallas_call(
        functools.partial(everyone_kernel, count, inner, reduce),
        out_shape=jax.ShapeDtypeStruct(tail if reduce else (count,) + tail, values.dtype),
        in_specs=[VMEM_SPEC],
        out_specs=VMEM_SPEC,
        scratch_shapes=scratch,
        compiler_params=pltpu.CompilerParams(
            collective_id=collective_id, has_side_effects=True, vmem_limit_bytes=VMEM_LIMIT
        ),
        name="everyone",
    )(values)


def normed(values, gain):
    return values * lax.rsqrt(jnp.mean(values * values, axis=-1, keepdims=True) + EPS) * gain


def line_kernel(kind, nt, chunks, extra, *refs):
    refs = list(refs)
    has_sum = kind != "start"
    has_gather = kind != "end"
    part = refs.pop(0) if has_sum else None
    if kind == "start":
        x_ref, gain_ref = refs.pop(0), refs.pop(0)
    elif kind == "fwd":
        extra_ref, gain_ref = refs.pop(0), refs.pop(0)
    elif kind == "last":
        extra_ref, og_ref = refs.pop(0), refs.pop(0)
    else:
        extra_ref = refs.pop(0) if extra else None
        base_ref, skip_ref, gain_ref = refs.pop(0), refs.pop(0), refs.pop(0)
    own_ref = refs.pop(0) if has_sum else None
    gg_ref = refs.pop(0) if kind in ("bwd", "end") else None
    all_ref = refs.pop(0) if has_gather else None
    if has_sum:
        from_left, from_right, tx, acc, rs_send, rl_sem, rr_sem = refs[:7]
        refs = refs[7:]
    if has_gather:
        ag_right, ag_left, ag_recv = refs[:3]

    me = lax.axis_index("tensor")
    has_l, has_r = me > 0, me < nt - 1
    left, right = jnp.maximum(me - 1, 0), jnp.minimum(me + 1, nt - 1)

    barrier = pltpu.get_barrier_semaphore()

    @pl.when(has_l)
    def _():
        pl.semaphore_signal(barrier, inc=1, device_id={"tensor": left}, device_id_type=MESH)

    @pl.when(has_r)
    def _():
        pl.semaphore_signal(barrier, inc=1, device_id={"tensor": right}, device_id_type=MESH)

    pl.semaphore_wait(barrier, has_l.astype(jnp.int32) + has_r.astype(jnp.int32))

    def copy(src, dst, send_sem, recv_sem, to):
        return pltpu.make_async_remote_copy(
            src_ref=src,
            dst_ref=dst,
            send_sem=send_sem,
            recv_sem=recv_sem,
            device_id={"tensor": to},
            device_id_type=MESH,
        )

    def sum_right(j, c, src):
        return copy(src, from_left.at[j, c], rs_send.at[j, c], rl_sem.at[j, c], right)

    def sum_left(j, c, src):
        return copy(src, from_right.at[j, c], rs_send.at[j, c], rr_sem.at[j, c], left)

    def spread_right(j, c):
        block = all_ref.at[j, c]
        return copy(block, block, ag_right.at[j, c], ag_recv.at[j, c], right)

    def spread_left(j, c):
        block = all_ref.at[j, c]
        return copy(block, block, ag_left.at[j, c], ag_recv.at[j, c], left)

    def offer(c):
        @pl.when(has_r)
        def _():
            spread_right(me, c).start()

        @pl.when(has_l)
        def _():
            spread_left(me, c).start()

    def pass_on(c, d):
        @pl.when(me - d >= 0)
        def _():
            j = me - d
            spread_right(j, c).wait_recv()

            @pl.when(has_r)
            def _():
                spread_right(j, c).start()

        @pl.when(me + d < nt)
        def _():
            j = me + d
            spread_left(j, c).wait_recv()

            @pl.when(has_l)
            def _():
                spread_left(j, c).start()

    def relay(c, t):
        j_up, j_down = nt - 1 - t, t

        @pl.when(has_l & (me < j_up))
        def _():
            sum_right(j_up, c, tx.at[j_up, c]).wait_recv()
            tx[j_up, c] = (part[j_up, c].astype(F32) + from_left[j_up, c].astype(F32)).astype(BF16)
            sum_right(j_up, c, tx.at[j_up, c]).start()

        @pl.when(has_r & (me > j_down))
        def _():
            sum_left(j_down, c, tx.at[j_down, c]).wait_recv()
            tx[j_down, c] = (
                part[j_down, c].astype(F32) + from_right[j_down, c].astype(F32)
            ).astype(BF16)
            sum_left(j_down, c, tx.at[j_down, c]).start()

    def own_rows(c):
        acc[...] = part[me, c].astype(F32)

        @pl.when(has_l)
        def _():
            sum_right(me, c, tx.at[me, c]).wait_recv()
            acc[...] += from_left[me, c].astype(F32)

        @pl.when(has_r)
        def _():
            sum_left(me, c, tx.at[me, c]).wait_recv()
            acc[...] += from_right[me, c].astype(F32)

        total = acc[...]
        if kind == "fwd":
            total = total + extra_ref[c]
            all_ref[me, c] = normed(total, gain_ref[...]).astype(BF16)
            own_ref[c] = total
        elif kind == "last":
            own_ref[c] = total + extra_ref[c]
        else:
            if extra:
                total = total + extra_ref[c]
            base = base_ref[c]
            scale = lax.rsqrt(jnp.mean(base * base, axis=-1, keepdims=True) + EPS)
            unit = base * scale
            grad_unit = total * gain_ref[...]
            below = scale * (grad_unit - unit * jnp.mean(grad_unit * unit, axis=-1, keepdims=True))
            result = below + skip_ref[c]
            if has_gather:
                all_ref[me, c] = result.astype(BF16)
            own_ref[c] = result
            gg = jnp.sum(total * unit, axis=0, keepdims=True)
            if c == 0:
                gg_ref[...] = gg
            else:
                gg_ref[...] += gg
        if kind in ("fwd", "bwd"):
            offer(c)

    if kind == "start":
        for c in range(chunks):
            all_ref[me, c] = normed(x_ref[c].astype(F32), gain_ref[...]).astype(BF16)
            offer(c)
        for c in range(chunks):
            for d in range(1, nt):
                pass_on(c, d)
    else:

        @pl.when(jnp.logical_not(has_l))
        def _():
            for c in range(chunks):
                for j in range(nt - 1, 0, -1):
                    sum_right(j, c, part.at[j, c]).start()

        @pl.when(jnp.logical_not(has_r))
        def _():
            for c in range(chunks):
                for j in range(nt - 1):
                    sum_left(j, c, part.at[j, c]).start()

        if kind == "last":
            for c in range(chunks):
                all_ref[me, c] = og_ref[c]
            for c in range(chunks):
                offer(c)
        for c in range(chunks + (1 if has_gather and kind != "last" else 0)):
            for t in range(nt - 1):
                if c < chunks:
                    relay(c, t)
                if kind == "last":
                    pass_on(c, t + 1)
                elif has_gather and c >= 1:
                    pass_on(c - 1, t + 1)
            if c < chunks:
                own_rows(c)

    for c in range(chunks):
        for j in range(nt):
            if has_sum:

                @pl.when(me < j)
                def _():
                    sum_right(j, c, tx.at[j, c]).wait_send()

                @pl.when(me > j)
                def _():
                    sum_left(j, c, tx.at[j, c]).wait_send()

            if has_gather:

                @pl.when(has_r & (j <= me))
                def _():
                    spread_right(j, c).wait_send()

                @pl.when(has_l & (j >= me))
                def _():
                    spread_left(j, c).wait_send()


def line_exchange(kind, args, rows, width, collective_id, extra=False, chunks=2):
    nt = lax.axis_size("tensor")
    has_sum = kind != "start"
    has_gather = kind != "end"
    piece = rows // chunks
    split = []
    for item in args:
        if item.shape[0] == nt * rows:
            split.append(item.reshape(nt, chunks, piece, width))
        elif item.shape[0] == rows:
            split.append(item.reshape(chunks, piece, width))
        else:
            split.append(item)
    outs = []
    if has_sum:
        outs.append(jax.ShapeDtypeStruct((chunks, piece, width), F32))
    if kind in ("bwd", "end"):
        outs.append(jax.ShapeDtypeStruct((1, width), F32))
    if has_gather:
        outs.append(jax.ShapeDtypeStruct((nt, chunks, piece, width), BF16))
    scratch = []
    sems = pltpu.SemaphoreType.DMA((nt, chunks))
    if has_sum:
        buf = pltpu.VMEM((nt, chunks, piece, width), BF16)
        scratch += [buf, buf, buf, pltpu.VMEM((piece, width), F32), sems, sems, sems]
    if has_gather:
        scratch += [sems, sems, sems]
    results = pl.pallas_call(
        functools.partial(line_kernel, kind, nt, chunks, extra),
        out_shape=outs,
        in_specs=[VMEM_SPEC] * len(split),
        out_specs=[VMEM_SPEC] * len(outs),
        scratch_shapes=scratch,
        compiler_params=pltpu.CompilerParams(
            collective_id=collective_id, has_side_effects=True, vmem_limit_bytes=VMEM_LIMIT
        ),
        cost_estimate=pl.CostEstimate(
            flops=10 * nt * rows * width, bytes_accessed=100 * rows * width * nt, transcendentals=0
        ),
        name="line_" + kind,
    )(*split)
    results = list(results)
    if has_sum:
        results[0] = results[0].reshape(rows, width)
    if has_gather:
        results[-1] = results[-1].reshape(nt * rows, width)
    return results


def span_mask(starts_ref, row_at, rows, cols, spans):
    row = row_at + lax.broadcasted_iota(jnp.int32, (rows, cols), 0)
    col = lax.broadcasted_iota(jnp.int32, (rows, cols), 1)
    seen = col <= row
    for k in range(spans):
        begin = starts_ref[0, k]
        seen = seen | (
            (row >= begin) & (row < begin + PIC) & (col >= begin) & (col < begin + PIC)
        )
    return seen


def key_extent(row_at, seq_len, spans):
    segment = seq_len // spans
    return (row_at // segment + 1) * segment


def attend_kernel(heads, spans, block, starts_ref, a_ref, w_ref, qkv_ref, o_ref, lse_ref, out_ref):
    seq_len = a_ref.shape[0]
    wide = heads * HEAD
    factor = HEAD ** (-0.5)
    qkv_ref[...] = dot(a_ref[...], w_ref[:, : 3 * wide]).astype(BF16)
    for at in range(0, seq_len, block):
        reach = key_extent(at, seq_len, spans)
        seen = span_mask(starts_ref, at, block, reach, spans)
        for h in range(heads):
            q = qkv_ref[at : at + block, h * HEAD : (h + 1) * HEAD]
            k = qkv_ref[:reach, wide + h * HEAD : wide + (h + 1) * HEAD]
            v = qkv_ref[:reach, 2 * wide + h * HEAD : 2 * wide + (h + 1) * HEAD]
            s = jnp.where(seen, dot_nt(q, k) * factor, -1e30)
            top = jnp.max(s, axis=-1, keepdims=True)
            e = jnp.exp(s - top)
            total = jnp.sum(e, axis=-1, keepdims=True)
            probs = (e * (1.0 / total)).astype(BF16)
            o_ref[at : at + block, h * HEAD : (h + 1) * HEAD] = dot(probs, v).astype(BF16)
            lse_ref[at : at + block, h : h + 1] = top + jnp.log(total)
    out_ref[...] = dot_nt(o_ref[...], w_ref[:, 3 * wide :]).astype(BF16)


def attend_forward(starts, a_all, w_attn, heads):
    seq_len, width = a_all.shape
    wide = heads * HEAD
    spans = starts.shape[1]
    return pl.pallas_call(
        functools.partial(attend_kernel, heads, spans, PIC),
        out_shape=[
            jax.ShapeDtypeStruct((seq_len, 3 * wide), BF16),
            jax.ShapeDtypeStruct((seq_len, wide), BF16),
            jax.ShapeDtypeStruct((seq_len, heads), F32),
            jax.ShapeDtypeStruct((seq_len, width), BF16),
        ],
        in_specs=[pl.BlockSpec(memory_space=pltpu.SMEM), VMEM_SPEC, VMEM_SPEC],
        out_specs=[VMEM_SPEC] * 4,
        compiler_params=pltpu.CompilerParams(vmem_limit_bytes=VMEM_LIMIT),
        cost_estimate=pl.CostEstimate(
            flops=8 * seq_len * width * wide + 4 * heads * seq_len * seq_len * HEAD,
            bytes_accessed=6 * seq_len * width,
            transcendentals=heads * seq_len * seq_len,
        ),
        name="attend_forward",
    )(starts, a_all, w_attn)


def attend_back_kernel(
    heads, spans, block, starts_ref, g_ref, w_ref, a_ref, qkv_ref, o_ref, lse_ref,
    ga_ref, gw_ref, go_scr, gq_scr, gk_acc, gv_acc,
):
    seq_len = a_ref.shape[0]
    wide = heads * HEAD
    factor = HEAD ** (-0.5)
    go_scr[...] = dot(g_ref[...], w_ref[:, 3 * wide :]).astype(BF16)
    gw_ref[:, 3 * wide :] = dot_tn(g_ref[...], o_ref[...]).astype(BF16)
    gk_acc[...] = jnp.zeros_like(gk_acc)
    gv_acc[...] = jnp.zeros_like(gv_acc)
    for at in range(0, seq_len, block):
        reach = key_extent(at, seq_len, spans)
        seen = span_mask(starts_ref, at, block, reach, spans)
        for h in range(heads):
            own = slice(h * HEAD, (h + 1) * HEAD)
            q = qkv_ref[at : at + block, own]
            k = qkv_ref[:reach, wide + h * HEAD : wide + (h + 1) * HEAD]
            v = qkv_ref[:reach, 2 * wide + h * HEAD : 2 * wide + (h + 1) * HEAD]
            go = go_scr[at : at + block, own]
            s = jnp.where(seen, dot_nt(q, k) * factor, -1e30)
            probs = jnp.exp(s - lse_ref[at : at + block, h : h + 1])
            gp = dot_nt(go, v)
            inner = jnp.sum(probs * gp, axis=-1, keepdims=True)
            gs = (probs * (gp - inner)).astype(BF16)
            gq_scr[at : at + block, own] = (dot(gs, k) * factor).astype(BF16)
            gk_acc[:reach, own] += dot_tn(gs, q) * factor
            gv_acc[:reach, own] += dot_tn(probs.astype(BF16), go)
    gq_scr[:, wide : 2 * wide] = gk_acc[...].astype(BF16)
    gq_scr[:, 2 * wide :] = gv_acc[...].astype(BF16)
    gw_ref[:, : 3 * wide] = dot_tn(a_ref[...], gq_scr[...]).astype(BF16)
    ga_ref[...] = dot_nt(gq_scr[...], w_ref[:, : 3 * wide]).astype(BF16)


def attend_backward(starts, g_all, w_attn, a_all, qkv, o, lse, heads):
    seq_len, width = a_all.shape
    wide = heads * HEAD
    spans = starts.shape[1]
    return pl.pallas_call(
        functools.partial(attend_back_kernel, heads, spans, PIC),
        out_shape=[
            jax.ShapeDtypeStruct((seq_len, width), BF16),
            jax.ShapeDtypeStruct((width, 4 * wide), BF16),
        ],
        in_specs=[pl.BlockSpec(memory_space=pltpu.SMEM)] + [VMEM_SPEC] * 6,
        out_specs=[VMEM_SPEC] * 2,
        scratch_shapes=[
            pltpu.VMEM((seq_len, wide), BF16),
            pltpu.VMEM((seq_len, 3 * wide), BF16),
            pltpu.VMEM((seq_len, wide), F32),
            pltpu.VMEM((seq_len, wide), F32),
        ],
        compiler_params=pltpu.CompilerParams(vmem_limit_bytes=VMEM_LIMIT),
        cost_estimate=pl.CostEstimate(
            flops=16 * seq_len * width * wide + 10 * heads * seq_len * seq_len * HEAD,
            bytes_accessed=12 * seq_len * width,
            transcendentals=heads * seq_len * seq_len,
        ),
        name="attend_backward",
    )(starts, g_all, w_attn, a_all, qkv, o, lse)


def lane_column(values, at):
    lane = lax.broadcasted_iota(jnp.int32, values.shape, 1)
    return jnp.sum(jnp.where(lane == at, values, 0), axis=1, keepdims=True)


def two_parts(values):
    high = values.astype(BF16)
    return high, (values - high.astype(F32)).astype(BF16)


def experts_kernel(
    cap, b_ref, w_ref, rowpos_ref, pos_ref, router_ref, zterm_ref,
    x_ref, gu_ref, z_ref, wd_ref, f_ref, pick_scr, y_scr,
):
    e = pl.program_id(0)
    seq_len, width = b_ref.shape
    half = gu_ref.shape[2] // 2

    @pl.when(e == 0)
    def _():
        z = dot(b_ref[...], router_ref[...]) + zterm_ref[...]
        z_ref[...] = z
        hit = pos_ref[...] >= 0
        top = jnp.max(jnp.where(hit, z, -3e38), axis=1, keepdims=True)
        ez = jnp.where(hit, jnp.exp(jnp.where(hit, z - top, 0.0)), 0.0)
        wd_ref[...] = ez / jnp.sum(ez, axis=1, keepdims=True)

    w = w_ref[...].reshape(width, 3 * half)
    take = (
        lax.broadcasted_iota(jnp.int32, (cap, seq_len), 0) == rowpos_ref[0]
    ).astype(F32).astype(BF16)
    x = dot(take, b_ref[...]).astype(BF16)
    x_ref[0] = x
    gu = dot(x, w[:, : 2 * half])
    gu_ref[0] = gu.astype(BF16)
    g, u = gu[:, :half], gu[:, half:]
    h = (g * jax.nn.sigmoid(g) * u).astype(BF16)
    y = dot_nt(h, w[:, 2 * half :])
    y_scr[pl.ds(pl.multiple_of(e * cap, cap), cap), :] = y.astype(BF16)
    column = lane_column(pos_ref[...], e)
    weight = lane_column(wd_ref[...], e)
    put = jnp.where(
        lax.broadcasted_iota(jnp.int32, (seq_len, cap), 1) == column, weight, 0.0
    ).astype(BF16)
    pick_scr[:, pl.ds(pl.multiple_of(e * cap, cap), cap)] = put

    @pl.when(e == pl.num_programs(0) - 1)
    def _():
        f_ref[...] = dot(pick_scr[...], y_scr[...]).astype(BF16)


def whole(shape):
    return pl.BlockSpec(shape, lambda e: (0,) * len(shape))


def experts_forward(b_all, w_exp, rowpos, pos, router, zterm, cap):
    seq_len, width = b_all.shape
    shards_dp, count, rows, wide3 = w_exp.shape
    half = wide3 // 3
    return pl.pallas_call(
        functools.partial(experts_kernel, cap),
        grid=(count,),
        out_shape=[
            jax.ShapeDtypeStruct((count, cap, width), BF16),
            jax.ShapeDtypeStruct((count, cap, 2 * half), BF16),
            jax.ShapeDtypeStruct((seq_len, LANES), F32),
            jax.ShapeDtypeStruct((seq_len, LANES), F32),
            jax.ShapeDtypeStruct((seq_len, width), BF16),
        ],
        in_specs=[
            whole((seq_len, width)),
            pl.BlockSpec((shards_dp, 1, rows, wide3), lambda e: (0, e, 0, 0)),
            pl.BlockSpec((1, 1, seq_len), lambda e: (e, 0, 0)),
            whole((seq_len, LANES)),
            whole((width, LANES)),
            whole((seq_len, LANES)),
        ],
        out_specs=[
            pl.BlockSpec((1, cap, width), lambda e: (e, 0, 0)),
            pl.BlockSpec((1, cap, 2 * half), lambda e: (e, 0, 0)),
            whole((seq_len, LANES)),
            whole((seq_len, LANES)),
            whole((seq_len, width)),
        ],
        scratch_shapes=[
            pltpu.VMEM((seq_len, count * cap), BF16),
            pltpu.VMEM((count * cap, width), BF16),
        ],
        compiler_params=pltpu.CompilerParams(vmem_limit_bytes=VMEM_LIMIT),
        cost_estimate=pl.CostEstimate(
            flops=count * (4 * cap * seq_len * width + 6 * cap * width * half),
            bytes_accessed=2 * count * width * wide3,
            transcendentals=0,
        ),
        name="experts_forward",
    )(b_all, w_exp, rowpos, pos, router, zterm)


def experts_back_kernel(
    cap, g_ref, w_ref, x_ref, gu_ref, rowpos_ref, pos_ref, wd_ref, gwown_ref, gprev_ref, rt_ref,
    gw_ref, gz_ref, gb_ref, pick_scr, gx_scr, gg_scr,
):
    e = pl.program_id(0)
    seq_len, width = g_ref.shape
    shards_dp, _, rows, wide3 = w_ref.shape
    half = wide3 // 3
    w = w_ref[...].reshape(width, wide3)
    take = (
        lax.broadcasted_iota(jnp.int32, (cap, seq_len), 0) == rowpos_ref[0]
    ).astype(F32).astype(BF16)
    w_high, w_low = two_parts(wd_ref[...])
    weight = lane_column(dot(take, w_high) + dot(take, w_low), e)
    gf = dot(take, g_ref[...])
    gh = dot(gf.astype(BF16), w[:, 2 * half :])
    gu = gu_ref[0].astype(F32)
    g, u = gu[:, :half], gu[:, half:]
    sig = jax.nn.sigmoid(g)
    h = (g * sig * u).astype(BF16)
    slot_grad = jnp.sum(h.astype(F32) * gh, axis=1, keepdims=True)
    gh = gh * weight
    gg = gh * u * sig * (1.0 + g * (1.0 - sig))
    gup = gh * g * sig
    both = jnp.concatenate([gg.astype(BF16), gup.astype(BF16)], axis=1)
    gy = (gf * weight).astype(BF16)
    gw_ref[:, 0, :, : 2 * half] = dot_tn(x_ref[0], both).astype(BF16).reshape(
        shards_dp, rows, 2 * half
    )
    gw_ref[:, 0, :, 2 * half :] = dot_tn(gy, h).astype(BF16).reshape(shards_dp, rows, half)
    here = pl.ds(pl.multiple_of(e * cap, cap), cap)
    gx_scr[here, :] = dot_nt(both, w[:, : 2 * half]).astype(BF16)
    s_high, s_low = two_parts(slot_grad)
    lane = lax.broadcasted_iota(jnp.int32, (cap, LANES), 1)
    gg_scr[here, :LANES] = jnp.where(lane == e, s_high.astype(F32), 0.0).astype(BF16)
    gg_scr[here, LANES:] = jnp.where(lane == e, s_low.astype(F32), 0.0).astype(BF16)
    column = lane_column(pos_ref[...], e)
    pick_scr[:, here] = (
        lax.broadcasted_iota(jnp.int32, (seq_len, cap), 1) == column
    ).astype(F32).astype(BF16)

    @pl.when(e == pl.num_programs(0) - 1)
    def _():
        slots = dot(pick_scr[...], gg_scr[...])
        gw = slots[:, :LANES] + slots[:, LANES:] + gwown_ref[...]
        wd = wd_ref[...]
        gz = wd * (gw - jnp.sum(wd * gw, axis=1, keepdims=True)) + gprev_ref[...]
        gz_ref[...] = gz
        z_high, z_low = two_parts(gz)
        gb = dot(pick_scr[...], gx_scr[...]) + dot(z_high, rt_ref[...]) + dot(z_low, rt_ref[...])
        gb_ref[...] = gb.astype(BF16)


def experts_backward(g_all, w_exp, x, gu, rowpos, pos, wd, gw_own, grad_prev, router_t, cap):
    seq_len, width = g_all.shape
    shards_dp, count, rows, wide3 = w_exp.shape
    half = wide3 // 3
    weight_spec = pl.BlockSpec((shards_dp, 1, rows, wide3), lambda e: (0, e, 0, 0))
    return pl.pallas_call(
        functools.partial(experts_back_kernel, cap),
        grid=(count,),
        out_shape=[
            jax.ShapeDtypeStruct(w_exp.shape, BF16),
            jax.ShapeDtypeStruct((seq_len, LANES), F32),
            jax.ShapeDtypeStruct((seq_len, width), BF16),
        ],
        in_specs=[
            whole((seq_len, width)),
            weight_spec,
            pl.BlockSpec((1, cap, width), lambda e: (e, 0, 0)),
            pl.BlockSpec((1, cap, 2 * half), lambda e: (e, 0, 0)),
            pl.BlockSpec((1, 1, seq_len), lambda e: (e, 0, 0)),
            whole((seq_len, LANES)),
            whole((seq_len, LANES)),
            whole((seq_len, LANES)),
            whole((seq_len, LANES)),
            whole((LANES, width)),
        ],
        out_specs=[weight_spec, whole((seq_len, LANES)), whole((seq_len, width))],
        scratch_shapes=[
            pltpu.VMEM((seq_len, count * cap), BF16),
            pltpu.VMEM((count * cap, width), BF16),
            pltpu.VMEM((count * cap, 2 * LANES), BF16),
        ],
        compiler_params=pltpu.CompilerParams(vmem_limit_bytes=VMEM_LIMIT),
        cost_estimate=pl.CostEstimate(
            flops=count * (4 * cap * seq_len * width + 12 * cap * width * half),
            bytes_accessed=4 * count * width * wide3,
            transcendentals=0,
        ),
        name="experts_backward",
    )(g_all, w_exp, x, gu, rowpos, pos, wd, gw_own, grad_prev, router_t)


def lanes(values):
    return jnp.pad(values, ((0, 0), (0, LANES - values.shape[1])))


def slot_table(route_ids):
    tokens = route_ids.shape[0]
    codes = jnp.arange(LANES, dtype=jnp.int32)
    hit = jnp.any(route_ids[:, :, None] == codes[None, None, :], axis=1)
    place = jnp.arange(tokens, dtype=jnp.int32)
    before = (place[None, :] < place[:, None]).astype(BF16)
    slots = dot(before, hit.astype(BF16)).astype(jnp.int32)
    return jnp.where(hit, slots, -1)


def shards(
    hidden_in,
    prev_logits,
    routes,
    span_starts,
    attn_norm,
    qkv_weight,
    out_weight,
    moe_norm,
    router,
    gate_mix,
    const_vec,
    const_mix,
    up_weight,
    down_weight,
    out_grad,
):
    layers = qkv_weight.shape[0]
    own, width = hidden_in.shape
    nt = lax.axis_size("tensor")
    ndp = lax.axis_size("dp")
    seq_len = own * nt
    offset = lax.axis_index("tensor") * own
    cap = seq_len // 4
    heads = qkv_weight.shape[3] // HEAD
    wide = heads * HEAD
    half = up_weight.shape[4]
    rows = qkv_weight.shape[1]
    cols = attn_norm.shape[1]
    consts = const_vec.shape[1]

    packed = jnp.concatenate(
        [attn_norm.T, moe_norm.T]
        + [router[l] for l in range(layers)]
        + [const_vec.reshape(-1, cols).T]
        + [const_mix[l, j] for l in range(layers) for j in range(consts)],
        axis=1,
    )
    small = everyone(lanes(packed), False, 0).reshape(width, LANES)
    at = 0
    fields = {}
    for name, size in (
        ("attn", layers),
        ("moe", layers),
        ("router", layers * NEXP),
        ("cvec", layers * consts),
        ("cmix", layers * consts * 2),
    ):
        fields[name] = (at, size)
        at += size

    def field(name, l, per):
        begin = fields[name][0] + l * per
        return small[:, begin : begin + per]

    attn_w, exp_w = [], []
    for l in range(layers):
        local = jnp.concatenate(
            [qkv_weight[l].reshape(rows, 3 * wide), out_weight[l].T], axis=1
        )
        attn_w.append(lax.all_gather(local, "dp", axis=0, tiled=False).reshape(width, 4 * wide))
        local = jnp.concatenate(
            [
                up_weight[l].reshape(EXPERTS, rows, 2 * half),
                jnp.swapaxes(down_weight[l], 1, 2),
            ],
            axis=2,
        )
        exp_w.append(lax.all_gather(local, "dp", axis=0, tiled=False))

    pos = [slot_table(routes[l]) for l in range(layers)]
    rowpos = [p[:, :EXPERTS].T[:, None, :] for p in pos]

    hidden = hidden_in.astype(F32)
    gain = field("attn", 0, 1).astype(F32).T
    (a_all,) = line_exchange("start", [hidden_in, gain], own, width, 1)
    z_prev = lanes(prev_logits)
    next_id = 2
    stored = []
    for l in range(layers):
        mix = jnp.pad(gate_mix[l].astype(F32), ((0, LANES - NEXP), (0, LANES - NEXP)))
        zterm = jnp.dot(z_prev, mix, precision=HIGH)
        qkv, o, lse, partial = attend_forward(span_starts, a_all, attn_w[l], heads)
        gain = field("moe", l, 1).astype(F32).T
        mid, b_all = line_exchange("fwd", [partial, hidden, gain], own, width, next_id)
        router_l = lanes(field("router", l, NEXP))
        x, gu, z, wd, partial = experts_forward(
            b_all, exp_w[l], rowpos[l], pos[l], router_l, zterm, cap
        )
        b_own = lax.dynamic_slice_in_dim(b_all, offset, own, 0)
        cmix = field("cmix", l, 2 * consts)
        cvec = field("cvec", l, consts).astype(F32).T
        logit = dot(b_own, cmix)
        alpha = jax.nn.softmax(logit.reshape(own, consts, 2), axis=2)
        gates = lax.dynamic_slice_in_dim(wd, offset, own, 0)
        copy_gate = gates[:, EXPERTS + 1 : EXPERTS + 2]
        const_gate = gates[:, EXPERTS + 2 : EXPERTS + 2 + consts]
        keep = copy_gate + jnp.sum(const_gate * alpha[:, :, 0], axis=1, keepdims=True)
        inject = const_gate * alpha[:, :, 1]
        side = keep * b_own.astype(F32)
        for j in range(consts):
            side = side + inject[:, j : j + 1] * cvec[j : j + 1]
        stored.append(
            dict(
                hidden=hidden, a_all=a_all, qkv=qkv, o=o, lse=lse, mid=mid, b_all=b_all,
                b_own=b_own, x=x, gu=gu, wd=wd, z_prev=z_prev, alpha=alpha,
                const_gate=const_gate, keep=keep, inject=inject, cvec=cvec, cmix=cmix, mix=mix,
                router=router_l,
            )
        )
        if l + 1 < layers:
            gain = field("attn", l + 1, 1).astype(F32).T
            hidden, a_all = line_exchange("fwd", [partial, mid + side, gain], own, width, next_id + 1)
        else:
            hidden, g_all = line_exchange(
                "last", [partial, mid + side, out_grad], own, width, next_id + 1
            )
        z_prev = z
        next_id += 2
    hidden_out = hidden

    grad = out_grad.astype(F32)
    grad_prev = jnp.zeros((seq_len, LANES), F32)
    attn_grads, exp_grads = [None] * layers, [None] * layers
    gains_a, gains_m = [None] * layers, [None] * layers
    routers, cvecs, cmixes, mixes = ([None] * layers for _ in range(4))
    for l in reversed(range(layers)):
        s = stored[l]
        b_own = s["b_own"].astype(F32)
        bg = jnp.sum(b_own * grad, axis=1, keepdims=True)
        cg = jnp.concatenate(
            [jnp.sum(grad * s["cvec"][j : j + 1], axis=1, keepdims=True) for j in range(consts)],
            axis=1,
        )
        alpha = s["alpha"]
        gw_const = alpha[:, :, 0] * bg + alpha[:, :, 1] * cg
        gw_own = jnp.pad(
            jnp.concatenate([bg, gw_const], axis=1),
            ((0, 0), (EXPERTS + 1, LANES - EXPERTS - 2 - consts)),
        )
        gw_own = lax.dynamic_update_slice_in_dim(
            jnp.zeros((seq_len, LANES), F32), gw_own, offset, 0
        )
        ga = s["const_gate"][:, :, None] * jnp.stack([jnp.broadcast_to(bg, cg.shape), cg], axis=2)
        gt = alpha * (ga - jnp.sum(alpha * ga, axis=2, keepdims=True))
        gt = gt.reshape(own, 2 * consts)
        own_part = s["keep"] * grad
        cmix_f = s["cmix"].astype(F32).T
        for j in range(2 * consts):
            own_part = own_part + gt[:, j : j + 1] * cmix_f[j : j + 1]
        cmixes[l] = lax.dot_general(b_own, gt, (((0,), (0,)), ((), ())), precision=HIGH)
        cvecs[l] = lax.dot_general(grad, s["inject"], (((0,), (0,)), ((), ())), precision=HIGH)

        gw_exp, gz, partial = experts_backward(
            g_all, exp_w[l], s["x"], s["gu"], rowpos[l], pos[l], s["wd"], gw_own, grad_prev,
            s["router"].T, cap,
        )
        exp_grads[l] = lax.psum_scatter(gw_exp, "dp", scatter_dimension=0, tiled=False)
        z_high, z_low = two_parts(gz)
        routers[l] = (dot_tn(s["b_all"], z_high) + dot_tn(s["b_all"], z_low))[:, :NEXP]
        mixes[l] = lax.dot_general(
            s["z_prev"], gz, (((0,), (0,)), ((), ())), precision=HIGH
        )[:NEXP, :NEXP]
        if l > 0:
            grad_prev = lax.dot_general(gz, s["mix"], (((1,), (1,)), ((), ())), precision=HIGH)
        gain = field("moe", l, 1).astype(F32).T
        grad_mid, gains_m[l], g_all = line_exchange(
            "bwd", [partial, own_part, s["mid"], grad, gain], own, width, next_id, extra=True
        )
        partial, gw_attn = attend_backward(
            span_starts, g_all, attn_w[l], s["a_all"], s["qkv"], s["o"], s["lse"], heads
        )
        attn_grads[l] = lax.psum_scatter(
            gw_attn.reshape(ndp, rows, 4 * wide), "dp", scatter_dimension=0, tiled=False
        )
        gain = field("attn", l, 1).astype(F32).T
        if l > 0:
            grad, gains_a[l], g_all = line_exchange(
                "bwd", [partial, s["hidden"], grad_mid, gain], own, width, next_id + 1
            )
        else:
            grad, gains_a[l] = line_exchange(
                "end", [partial, s["hidden"], grad_mid, gain], own, width, next_id + 1
            )
        next_id += 2

    sums = jnp.concatenate(
        [item.T for item in gains_a]
        + [item.T for item in gains_m]
        + routers
        + cvecs
        + cmixes,
        axis=1,
    )
    sums = lanes(sums).reshape(ndp * nt, cols, LANES)
    flat = jnp.stack(mixes).reshape(-1)
    mix_rows = -(-flat.shape[0] // LANES)
    flat = jnp.pad(flat, (0, mix_rows * LANES - flat.shape[0])).reshape(1, mix_rows, LANES)
    flat = jnp.broadcast_to(flat, (ndp * nt, mix_rows, LANES))
    total = everyone(jnp.concatenate([sums, flat], axis=1), True, next_id)
    mix_total = total[cols:].reshape(-1)[: layers * NEXP * NEXP].reshape(layers, NEXP, NEXP)
    total = total[:cols]

    def back(name):
        begin, size = fields[name]
        return total[:, begin : begin + size]

    router_grad = jnp.swapaxes(back("router").reshape(cols, layers, NEXP), 0, 1)
    cmix_grad = jnp.transpose(back("cmix").reshape(cols, layers, consts, 2), (1, 2, 0, 3))
    cvec_grad = back("cvec").T.reshape(layers, consts, cols)
    qkv_grad = jnp.stack(
        [item[:, : 3 * wide].reshape(rows, 3, wide) for item in attn_grads]
    ).astype(F32)
    outw_grad = jnp.stack([item[:, 3 * wide :].T for item in attn_grads]).astype(F32)
    up_grad = jnp.stack(
        [item[:, :, : 2 * half].reshape(EXPERTS, rows, 2, half) for item in exp_grads]
    ).astype(F32)
    down_grad = jnp.stack(
        [jnp.swapaxes(item[:, :, 2 * half :], 1, 2) for item in exp_grads]
    ).astype(F32)
    return (
        hidden_out,
        grad,
        back("attn").T,
        qkv_grad,
        outw_grad,
        back("moe").T,
        router_grad,
        mix_total,
        cvec_grad,
        cmix_grad,
        up_grad,
        down_grad,
    )


def solution(mesh):
    return jax.shard_map(
        shards,
        mesh=mesh,
        in_specs=(
            P(("dp", "tensor"), None),
            P("dp", None),
            P(None, "dp", None),
            P("dp", None),
            P(None, ("dp", "tensor")),
            P(None, "dp", None, "tensor"),
            P(None, "tensor", "dp"),
            P(None, ("dp", "tensor")),
            P(None, ("dp", "tensor"), None),
            P(),
            P(None, None, ("dp", "tensor")),
            P(None, None, ("dp", "tensor"), None),
            P(None, None, "dp", None, "tensor"),
            P(None, None, "tensor", "dp"),
            P(("dp", "tensor"), None),
        ),
        out_specs=(
            P(("dp", "tensor"), None),
            P(("dp", "tensor"), None),
            P(None, ("dp", "tensor")),
            P(None, "dp", None, "tensor"),
            P(None, "tensor", "dp"),
            P(None, ("dp", "tensor")),
            P(None, ("dp", "tensor"), None),
            P(),
            P(None, None, ("dp", "tensor")),
            P(None, None, ("dp", "tensor"), None),
            P(None, None, "dp", None, "tensor"),
            P(None, None, "tensor", "dp"),
        ),
        check_vma=False,
    )
```

time: 2100 us -> 1060 us (0.50)
  Pallas kernels: 0 us -> 687 us
  waiting for transfers between devices: 837 us -> 221 us
  blocking collectives: 447 us -> 0 us
  local copies, waits for them, and re-layouts: 341 us -> 72.4 us
  matrix products: 216 us -> 12.3 us
  other arithmetic: 218 us -> 44.1 us
    pallas_call x0 -> x19, Pallas kernels: none -> 687 us  [the longest x9 478 us: line_exchange(): pl.pallas_call(functools.partial(line_kernel, kind, nt, chunks, extra), o...]
    all_gather x9 -> x0, blocking collectives: 407 us -> none  [the longest x1 79.7 us: shards(): lax.all_gather(const_mix, ('dp', 'tensor'), axis=2, tiled=True)]
    reduce_scatter x10 -> x4, waiting for transfers between devices: 624 us -> 219 us  [the longest x2 219 us: shards(): lax.psum_scatter(gw_exp, 'dp', scatter_dimension=0, tiled=False)]
    all_gather x12 -> x4, waiting for transfers between devices: 208 us -> 0.05 us  [the longest x2 0.02 us: shards(): lax.all_gather(local, 'dp', axis=0, tiled=False).reshape(width, 4 * wide)]
    dot_general x71 -> x17, matrix products: 208 us -> 12.3 us  [the longest x4 4.14 us: dot(): return jnp.dot(a, b, preferred_element_type=F32)]
    gather x14 -> x0, local copies, waits for them, and re-layouts: 128 us -> none  [the longest x6 35 us: shards(): jnp.take_along_axis(logits, route_ids, axis=1)]
    reduce_sum x34 -> x9, other arithmetic: 67.5 us -> 9.22 us  [the longest x2 4.25 us: shards(): jnp.sum(const_gate * alpha[:, :, 0], axis=1, keepdims=True)]
    another operation x22 -> x2, other arithmetic: 57.7 us -> 0.02 us  [the longest x1 0.01 us: shards(): flat = jnp.stack(mixes).reshape(-1)]
  transfers between devices with their start and end apart: 25 -> 8, of which waited for: 19 -> 2; matrix products, arithmetic and copies ran while one was open for 20% -> 7% of each run, Pallas kernels for 0% -> 43%
where the time goes in v1:
time: 1060 us; the launch traced here: 1050 us
  Pallas kernels  687 us (65%)
  waiting for transfers between devices  221 us (21%)
  local copies, waits for them, and re-layouts  72.4 us (7%)
  other arithmetic  44.1 us (4%)
  between operations  15.6 us (1%)
  matrix products  12.3 us (1%)
    pallas_call x9, Pallas kernels, line_exchange(): pl.pallas_call(functools.partial(line_kernel, kind, nt, chunks, extra), o...  478 us
    reduce_scatter x2, waiting for transfers between devices, shards(): lax.psum_scatter(gw_exp, 'dp', scatter_dimension=0, tiled=False)  219 us
    pallas_call x2, Pallas kernels, experts_backward(): pl.pallas_call(functools.partial(experts_back_kernel, cap), grid=(count,)...  67.5 us
    pallas_call x2, Pallas kernels, experts_forward(): pl.pallas_call(functools.partial(experts_kernel, cap), grid=(count,), out...  45.8 us
    pallas_call x2, Pallas kernels, attend_backward(): pl.pallas_call(functools.partial(attend_back_kernel, heads, spans, PIC),...  39.2 us
    pallas_call x2, Pallas kernels, everyone(): pl.pallas_call(functools.partial(everyone_kernel, count, inner, reduce),...  31.5 us
    pallas_call x2, Pallas kernels, attend_forward(): pl.pallas_call(functools.partial(attend_kernel, heads, spans, PIC), out_s...  24.6 us
  transfers between devices with their start and end apart: 8, of which 2 were waited for; matrix products, arithmetic and copies ran while one was open for 7% of the time, Pallas kernels for 43%

profile of v1, /device:TPU:0, one launch (start us, length us, event | category | flops | bytes accessed | tf_op | source)
XLA Modules:
  0.0 1052.2 jit_solution(12310232376372088908)
XLA Ops:
  10.3 5.0 fusion.66
  15.3 2.8 reshape_squeeze.13
  29.5 14.6 %everyone.2 = bf16[32,24,128]{2,1,0:T(8,128)(2,1)} custom-call(bf16[24,128]{1,0:T(8,128)(2,1)} %pad.43.x_ref), custom_call_target="tpu_custom_call" | custom-call | tf_op jit(solution)/shard_map/everyone/pallas_call | solution.py:99
  56.2 32.2 %line_start.1 = bf16[4,2,128,768]{3,2,1,0:T(8,128)(2,1)} custom-call(bf16[2,128,768]{2,1,0:T(8,128)(2,1)} %bitcast.261, f32[1,768]{1,0:T(1,128)} %reshape.291.refs_1_.refs_3_), custom_call_target="tpu_custom_call" | custom-call | flops 7864320 | bytes 78643200 | tf_op jit(solution)/shard_map/line_start/pallas_call | solution.py:351
  95.0 12.3 %attend_forward.2 = (bf16[1024,576]{1,0:T(8,128)(2,1)}, bf16[1024,192]{1,0:T(8,128)(2,1)}, f32[1024,3]{1,0:T(8,128)}, bf16[1024,768]{1,0:T(8,128)(2,1)}) custom-call(s32[1,2]{1,0:T(1,128)} %starts_ref.7, bf16[1024,768]{1,0:T(8,128)(2,1)} %bitcast.256, bf16[768,768]{1,0:T(8,128)(2,1)} %all-gather.9.cloned.1.call-done.w_ref), custom_call_target="tpu_custom_call" | custom-call | flops 2013265920 | bytes 4718592 | tf_op jit(solution)/shard_map/attend_forward/pallas_call | solution.py:416
  107.3 61.0 %line_fwd.3 = (f32[2,128,768]{2,1,0:T(8,128)}, bf16[4,2,128,768]{3,2,1,0:T(8,128)(2,1)}) custom-call(bf16[4,2,128,768]{3,2,1,0:T(8,128)(2,1)} %bitcast.255, f32[2,128,768]{2,1,0:T(8,128)} %reshape.254.refs_1_, f32[1,768]{1,0:T(1,128)} %reshape.292.refs_2_.refs_4_), custom_call_target="tpu_custom_call" | custom-call | flops 7864320 | bytes 78643200 | tf_op jit(solution)/shard_map/line_fwd/pallas_call | solution.py:351
  171.9 23.5 %experts_forward.2 = (bf16[8,256,768]{2,1,0:T(8,128)(2,1)}, bf16[8,256,1024]{2,1,0:T(8,128)(2,1)}, f32[1024,128]{1,0:T(8,128)}, f32[1024,128]{1,0:T(8,128)}, bf16[1024,768]{1,0:T(8,128)(2,1)}) custom-call(bf16[1024,768]{1,0:T(8,128)(2,1)} %bitcast.229, bf16[8,8,96,1536]{3,2,1,0:T(8,128)(2,1)} %bitcast.309, s32[8,1,1024]{2,1,0:T(1,128)} %copy.320.rowpos_ref, ...), custom_call_target="tpu_custom_call" | custom-call | flops 11274289152 | bytes 18874368 | tf_op jit(solution)/shard_map/experts_forward/pallas_call | solution.py:557
  203.3 67.8 %line_fwd.4 = (f32[2,128,768]{2,1,0:T(8,128)}, bf16[4,2,128,768]{3,2,1,0:T(8,128)(2,1)}) custom-call(bf16[4,2,128,768]{3,2,1,0:T(8,128)(2,1)} %bitcast.252, f32[2,128,768]{2,1,0:T(8,128)} %bitcast.244, f32[1,768]{1,0:T(1,128)} %reshape.293.refs_2_.refs_3_), custom_call_target="tpu_custom_call" | custom-call | flops 7864320 | bytes 78643200 | tf_op jit(solution)/shard_map/line_fwd/pallas_call | solution.py:351
  271.2 12.3 %attend_forward.3 = (bf16[1024,576]{1,0:T(8,128)(2,1)}, bf16[1024,192]{1,0:T(8,128)(2,1)}, f32[1024,3]{1,0:T(8,128)}, bf16[1024,768]{1,0:T(8,128)(2,1)}) custom-call(s32[1,2]{1,0:T(1,128)} %starts_ref.7, bf16[1024,768]{1,0:T(8,128)(2,1)} %bitcast.313, bf16[768,768]{1,0:T(8,128)(2,1)} %all-gather.13.cloned.1.call-done.w_ref), custom_call_target="tpu_custom_call" | custom-call | flops 2013265920 | bytes 4718592 | tf_op jit(solution)/shard_map/attend_forward/pallas_call | solution.py:416
  283.4 62.0 %line_fwd.5 = (f32[2,128,768]{2,1,0:T(8,128)}, bf16[4,2,128,768]{3,2,1,0:T(8,128)(2,1)}) custom-call(bf16[4,2,128,768]{3,2,1,0:T(8,128)(2,1)} %bitcast.254, f32[2,128,768]{2,1,0:T(8,128)} %get-tuple-element.65.refs_1_, f32[1,768]{1,0:T(1,128)} %reshape.294.refs_2_.refs_4_), custom_call_target="tpu_custom_call" | custom-call | flops 7864320 | bytes 78643200 | tf_op jit(solution)/shard_map/line_fwd/pallas_call | solution.py:351
  349.5 22.3 %experts_forward.3 = (bf16[8,256,768]{2,1,0:T(8,128)(2,1)}, bf16[8,256,1024]{2,1,0:T(8,128)(2,1)}, f32[1024,128]{1,0:T(8,128)}, f32[1024,128]{1,0:T(8,128)}, bf16[1024,768]{1,0:T(8,128)(2,1)}) custom-call(bf16[1024,768]{1,0:T(8,128)(2,1)} %bitcast.237, bf16[8,8,96,1536]{3,2,1,0:T(8,128)(2,1)} %bitcast.311, s32[8,1,1024]{2,1,0:T(1,128)} %copy.331.rowpos_ref, ...), custom_call_target="tpu_custom_call" | custom-call | flops 11274289152 | bytes 18874368 | tf_op jit(solution)/shard_map/experts_forward/pallas_call | solution.py:557
  385.9 46.3 %line_last.1 = (f32[2,128,768]{2,1,0:T(8,128)}, bf16[4,2,128,768]{3,2,1,0:T(8,128)(2,1)}) custom-call(bf16[4,2,128,768]{3,2,1,0:T(8,128)(2,1)} %bitcast.258, f32[2,128,768]{2,1,0:T(8,128)} %bitcast.245, bf16[2,128,768]{2,1,0:T(8,128)(2,1)} %bitcast.242), custom_call_target="tpu_custom_call" | custom-call | flops 7864320 | bytes 78643200 | tf_op jit(solution)/shard_map/line_last/pallas_call | solution.py:351
  433.4 33.6 %experts_backward.2 = (bf16[8,8,96,1536]{3,2,1,0:T(8,128)(2,1)}, f32[1024,128]{1,0:T(8,128)}, bf16[1024,768]{1,0:T(8,128)(2,1)}) custom-call(bf16[1024,768]{1,0:T(8,128)(2,1)} %bitcast.316, bf16[8,8,96,1536]{3,2,1,0:T(8,128)(2,1)} %bitcast.312, bf16[8,256,768]{2,1,0:T(8,128)(2,1)} %get-tuple-element.73.x_ref, ...), custom_call_target="tpu_custom_call" | custom-call | flops 16106127360 | bytes 37748736 | tf_op jit(solution)/shard_map/experts_backward/pallas_call | solution.py:654
  467.0 57.5 %line_bwd.3 = (f32[2,128,768]{2,1,0:T(8,128)}, f32[1,768]{1,0:T(1,128)}, bf16[4,2,128,768]{3,2,1,0:T(8,128)(2,1)}) custom-call(bf16[4,2,128,768]{3,2,1,0:T(8,128)(2,1)} %bitcast.259, f32[2,128,768]{2,1,0:T(8,128)} %bitcast.246, f32[2,128,768]{2,1,0:T(8,128)} %get-tuple-element.69.refs_2_, f32[2,128,768]{2,1,0:T(8,128)} %convert.15.refs_3_, ...), custom_call_target="tpu_custom_call" | custom-call | flops 7864320 | bytes 78643200 | tf_op jit(solution)/shard_map/line_bwd/pallas_call | solution.py:351
  524.6 19.7 %attend_backward.2 = (bf16[1024,768]{1,0:T(8,128)(2,1)}, bf16[768,768]{1,0:T(8,128)(2,1)}) custom-call(s32[1,2]{1,0:T(1,128)} %starts_ref.7, bf16[1024,768]{1,0:T(8,128)(2,1)} %bitcast.317, bf16[768,768]{1,0:T(8,128)(2,1)} %all-gather.13.cloned.1.call-done.w_ref, bf16[1024,768]{1,0:T(8,128)(2,1)} %bitcast.314, bf16[1024,576]{1,0:T(8,128)(2,1)} %get-tuple-element.77.qkv_ref, ...), custom_call_target="tpu_custom_call" | custom-call | flops 4429185024 | bytes 9437184 | tf_op jit(solution)/shard_map/attend_backward/pallas_call | solution.py:474
  544.3 56.2 %line_bwd.4 = (f32[2,128,768]{2,1,0:T(8,128)}, f32[1,768]{1,0:T(1,128)}, bf16[4,2,128,768]{3,2,1,0:T(8,128)(2,1)}) custom-call(bf16[4,2,128,768]{3,2,1,0:T(8,128)(2,1)} %bitcast.253, f32[2,128,768]{2,1,0:T(8,128)} %get-tuple-element.65.refs_1_, f32[2,128,768]{2,1,0:T(8,128)} %get-tuple-element.81.refs_2_, f32[1,768]{1,0:T(1,128)} %reshape.293.refs_2_.refs_3_), custom_call_target="tpu_custom_call" | custom-call | flops 7864320 | bytes 78643200 | tf_op jit(solution)/shard_map/line_bwd/pallas_call | solution.py:351
  611.2 33.9 %experts_backward.3 = (bf16[8,8,96,1536]{3,2,1,0:T(8,128)(2,1)}, f32[1024,128]{1,0:T(8,128)}, bf16[1024,768]{1,0:T(8,128)(2,1)}) custom-call(bf16[1024,768]{1,0:T(8,128)(2,1)} %bitcast.315, bf16[8,8,96,1536]{3,2,1,0:T(8,128)(2,1)} %bitcast.310, bf16[8,256,768]{2,1,0:T(8,128)(2,1)} %get-tuple-element.83.x_ref, ...), custom_call_target="tpu_custom_call" | custom-call | flops 16106127360 | bytes 37748736 | tf_op jit(solution)/shard_map/experts_backward/pallas_call | solution.py:654
  645.1 60.8 %line_bwd.5 = (f32[2,128,768]{2,1,0:T(8,128)}, f32[1,768]{1,0:T(1,128)}, bf16[4,2,128,768]{3,2,1,0:T(8,128)(2,1)}) custom-call(bf16[4,2,128,768]{3,2,1,0:T(8,128)(2,1)} %bitcast.260, f32[2,128,768]{2,1,0:T(8,128)} %multiply_add_fusion.refs_1_, f32[2,128,768]{2,1,0:T(8,128)} %get-tuple-element.61.refs_2_, f32[2,128,768]{2,1,0:T(8,128)} %get-tuple-element.85.refs_3_, ...), custom_call_target="tpu_custom_call" | custom-call | flops 7864320 | bytes 78643200 | tf_op jit(solution)/shard_map/line_bwd/pallas_call | solution.py:351
  705.8 19.5 %attend_backward.3 = (bf16[1024,768]{1,0:T(8,128)(2,1)}, bf16[768,768]{1,0:T(8,128)(2,1)}) custom-call(s32[1,2]{1,0:T(1,128)} %starts_ref.7, bf16[1024,768]{1,0:T(8,128)(2,1)} %bitcast.318, bf16[768,768]{1,0:T(8,128)(2,1)} %all-gather.9.cloned.1.call-done.w_ref, bf16[1024,768]{1,0:T(8,128)(2,1)} %bitcast.257, bf16[1024,576]{1,0:T(8,128)(2,1)} %get-tuple-element.89.qkv_ref, ...), custom_call_target="tpu_custom_call" | custom-call | flops 4429185024 | bytes 9437184 | tf_op jit(solution)/shard_map/attend_backward/pallas_call | solution.py:474
  731.2 34.2 %line_end.1 = (f32[2,128,768]{2,1,0:T(8,128)}, f32[1,768]{1,0:T(1,128)}) custom-call(bf16[4,2,128,768]{3,2,1,0:T(8,128)(2,1)} %bitcast.251, f32[2,128,768]{2,1,0:T(8,128)} %reshape.254.refs_1_, f32[2,128,768]{2,1,0:T(8,128)} %get-tuple-element.93.refs_2_, f32[1,768]{1,0:T(1,128)} %reshape.291.refs_1_.refs_3_), custom_call_target="tpu_custom_call" | custom-call | flops 7864320 | bytes 78643200 | tf_op jit(solution)/shard_map/line_end/pallas_call | solution.py:351
  771.1 16.9 %everyone.3 = f32[27,128]{1,0:T(8,128)} custom-call(f32[32,27,128]{2,1,0:T(8,128)} %pad_maximum_fusion.2.x_ref), custom_call_target="tpu_custom_call" | custom-call | tf_op jit(solution)/shard_map/everyone/pallas_call | solution.py:99
  801.3 93.0 %reduce-scatter.11.cloned.1.call-done = bf16[1,8,96,1536]{3,2,1,0:T(8,128)(2,1)} async-done(((bf16[8,8,96,1536]{3,2,1,0:T(8,128)(2,1)}), bf16[1,8,96,1536]{3,2,1,0:T(8,128)(2,1)}) %reduce-scatter.11.cloned.1.call-update) | async-done | bytes 2359312 | tf_op jit(solution)/shard_map/reduce_scatter | solution.py:861
  897.9 126.4 %reduce-scatter.9.cloned.1.call-done = bf16[1,8,96,1536]{3,2,1,0:T(8,128)(2,1)} async-done(((bf16[8,8,96,1536]{3,2,1,0:T(8,128)(2,1)}), bf16[1,8,96,1536]{3,2,1,0:T(8,128)(2,1)}) %reduce-scatter.9.cloned.1.call-update) | async-done | bytes 2359312 | tf_op jit(solution)/shard_map/reduce_scatter | solution.py:861
  1032.7 8.3 maximum_convert_fusion
  (342 shorter events, 114.6 us)
Async XLA Ops:
  7.2 87.8 %all-gather.9.cloned.1.call-start = ((), (), s32[]{:S(2)}) async-start(), calls=%async_computation.8 | async-start | bytes 1327104 | tf_op jit(solution)/shard_map/all_gather | solution.py:764
  10.3 161.6 %all-gather.11.cloned.1.call-start = ((), (), s32[]{:S(2)}) async-start(), calls=%async_computation.9 | async-start | bytes 21233664 | tf_op jit(solution)/shard_map/all_gather | solution.py:772
  22.1 249.0 %all-gather.13.cloned.1.call-start = ((), (), s32[]{:S(2)}) async-start(), calls=%async_computation.10 | async-start | bytes 1327104 | tf_op jit(solution)/shard_map/all_gather | solution.py:764
  23.4 326.1 %all-gather.15.cloned.1.call-start = ((), (), s32[]{:S(2)}) async-start(), calls=%async_computation.11 | async-start | bytes 21233664 | tf_op jit(solution)/shard_map/all_gather | solution.py:772
  27.3 19.2 %copy-start.27 = (bf16[256,768]{1,0:T(8,128)(2,1)S(1)}, bf16[256,768]{1,0:T(8,128)(2,1)}, u32[]{:S(2)}) copy-start(bf16[256,768]{1,0:T(8,128)(2,1)} %param.15) | copy-start | bytes 1179652
  27.3 20.7 %copy-start.56 = (s32[2,1024,2]{1,2,0:T(2,128)S(1)}, s32[2,1024,2]{1,2,0:T(2,128)}, u32[]{:S(2)}) copy-start(s32[2,1024,2]{1,2,0:T(2,128)} %param.17) | copy-start | bytes 49156
  27.3 768.5 %reduce-scatter.7.cloned.1.call-start = ((), (), s32[]{:S(2)}) async-start(), calls=%async_computation.5 | async-start | bytes 1769472 | tf_op jit(solution)/shard_map/reduce_scatter | solution.py:876
  55.3 34.5 %copy-start.45 = (bf16[2,12,12]{2,0,1:T(2,128)(2,1)S(1)}, bf16[2,12,12]{2,0,1:T(2,128)(2,1)}, u32[]{:S(2)}) copy-start(bf16[2,12,12]{2,0,1:T(2,128)(2,1)} %param.24) | copy-start | bytes 1732
  55.3 35.1 %copy-start.37 = (f32[1024,12]{0,1:T(8,128)S(1)}, f32[1024,12]{0,1:T(8,128)}, u32[]{:S(2)}) copy-start(f32[1024,12]{0,1:T(8,128)} %param.16) | copy-start | bytes 147460
  171.9 30.3 %copy-start.3 = (bf16[4,2,128,768]{3,2,1,0:T(8,128)(2,1)S(1)}, bf16[4,2,128,768]{3,2,1,0:T(8,128)(2,1)}, u32[]{:S(2)}) copy-start(bf16[4,2,128,768]{3,2,1,0:T(8,128)(2,1)} %get-tuple-element.59) | copy-start | bytes 4718596
  283.4 64.9 %copy-start.19 = (f32[1024,128]{1,0:T(8,128)S(1)}, f32[1024,128]{1,0:T(8,128)}, u32[]{:S(2)}) copy-start(f32[1024,128]{1,0:T(8,128)} %get-tuple-element.67) | copy-start | bytes 1572868
  283.4 64.9 %copy-start.38 = (bf16[12,12]{1,0:T(8,128)(2,1)S(1)}, bf16[12,12]{1,0:T(8,128)(2,1)}, u32[]{:S(2)}) copy-start(bf16[12,12]{1,0:T(8,128)(2,1)} %get-tuple-element.248) | copy-start | bytes 868
  374.6 8.7 copy-start.50
  374.6 8.7 copy-start.51
  374.6 8.7 copy-start.52
  374.6 8.7 copy-start.53
  385.9 46.3 %copy-start.34 = (f32[256,1]{1,0:T(8,128)S(1)}, f32[256,1]{1,0:T(8,128)}, u32[]{:S(2)}) copy-start(f32[256,1]{1,0:T(8,128)} %copy.337) | copy-start | bytes 3076
  385.9 46.3 %copy-start.36 = (f32[256,2]{1,0:T(8,128)S(1)}, f32[256,2]{1,0:T(8,128)}, u32[]{:S(2)}) copy-start(f32[256,2]{1,0:T(8,128)} %get-tuple-element.213) | copy-start | bytes 6148
  608.9 188.1 %reduce-scatter.5.cloned.1.call-start = ((), (), s32[]{:S(2)}) async-start(), calls=%async_computation.4 | async-start | bytes 1769472 | tf_op jit(solution)/shard_map/reduce_scatter | solution.py:876
  727.9 166.4 %reduce-scatter.11.cloned.1.call-start = ((), (), s32[]{:S(2)}) async-start(), calls=%async_computation.7 | async-start | bytes 21233664 | tf_op jit(solution)/shard_map/reduce_scatter | solution.py:861
  728.6 295.7 %reduce-scatter.9.cloned.1.call-start = ((), (), s32[]{:S(2)}) async-start(), calls=%async_computation.6 | async-start | bytes 21233664 | tf_op jit(solution)/shard_map/reduce_scatter | solution.py:861
  731.2 34.5 %copy-start.4 = (bf16[4,2,128,768]{3,2,1,0:T(8,128)(2,1)S(1)}, bf16[4,2,128,768]{3,2,1,0:T(8,128)(2,1)}, u32[]{:S(2)}) copy-start(bf16[4,2,128,768]{3,2,1,0:T(8,128)(2,1)} %get-tuple-element.66) | copy-start | bytes 4718596
  731.2 34.5 %copy-start.43 = (f32[256,4]{0,1:T(4,128)S(1)}, f32[256,4]{0,1:T(4,128)}, u32[]{:S(2)}) copy-start(f32[256,4]{0,1:T(4,128)} %copy-done.42) | copy-start | bytes 12292
  731.2 34.8 %copy-start.11 = (f32[1024,128]{1,0:T(8,128)S(1)}, f32[1024,128]{1,0:T(8,128)}, u32[]{:S(2)}) copy-start(f32[1024,128]{1,0:T(8,128)} %get-tuple-element.99) | copy-start | bytes 1572868
  (51 other events, 114.3 us)
Sparse Core Ops, SparseCore 0:
  10.4 26.6 all-gather.8
  39.6 98.9 all-gather.10
  140.5 23.9 all-gather.12
  166.2 98.6 all-gather.14
  609.0 37.6 reduce-scatter.6
  728.0 36.0 reduce-scatter.4
  767.7 126.4 reduce-scatter.10
  897.8 126.4 reduce-scatter.8

commit v2 on v1

--- a/solution.py
+++ b/solution.py
@@ -20,6 +20,7 @@
 F32 = jnp.float32
 BF16 = jnp.bfloat16
 VMEM_SPEC = pl.BlockSpec(memory_space=pltpu.VMEM)
+AHEAD = 2
 VMEM_LIMIT = 60 * 1024 * 1024
 
 
@@ -35,16 +36,7 @@
     return lax.dot_general(a, b, (((0,), (0,)), ((), ())), preferred_element_type=F32)
 
 
-def everyone_kernel(count, inner, reduce, x_ref, out_ref, *scratch):
-    if reduce:
-        land, send_sems, recv_sems = scratch
-    else:
-        land, (send_sems, recv_sems) = out_ref, scratch
-    me = lax.axis_index("dp") * inner + lax.axis_index("tensor")
-
-    def place(other):
-        return (lax.div(other, inner), lax.rem(other, inner))
-
+def greet_all(count, me, place):
     barrier = pltpu.get_barrier_semaphore()
 
     def greet(step, carry):
@@ -55,71 +47,106 @@
     lax.fori_loop(1, count, greet, 0)
     pl.semaphore_wait(barrier, count - 1)
 
-    def copy_to(other):
+
+def swap_all(count, me, place, source, land, send_sems, recv_sems):
+    def copy(other, slot):
         return pltpu.make_async_remote_copy(
-            src_ref=x_ref.at[other] if reduce else x_ref,
-            dst_ref=land.at[me],
+            src_ref=source(other),
+            dst_ref=land.at[slot],
             send_sem=send_sems.at[other],
-            recv_sem=recv_sems.at[me],
+            recv_sem=recv_sems.at[slot],
             device_id=place(other),
             device_id_type=MESH,
         )
 
-    def send(step, carry):
-        copy_to(lax.rem(me + step, count)).start()
-        return carry
-
-    lax.fori_loop(1, count, send, 0)
-    land[me] = x_ref[me] if reduce else x_ref[...]
-
-    def finish(step, carry):
-        other = lax.rem(me + count - step, count)
-        pltpu.make_async_remote_copy(
-            src_ref=x_ref.at[other] if reduce else x_ref,
-            dst_ref=land.at[other],
-            send_sem=send_sems.at[other],
-            recv_sem=recv_sems.at[other],
-            device_id=place(other),
-            device_id_type=MESH,
-        ).wait()
-        return carry
-
-    lax.fori_loop(1, count, finish, 0)
-    if reduce:
-        out_ref[...] = jnp.sum(land[...], axis=0)
-
-
-def everyone(values, reduce, collective_id):
-    inner = lax.axis_size("tensor")
-    count = lax.axis_size("dp") * inner
-    tail = values.shape[1:] if reduce else values.shape
-    scratch = [pltpu.SemaphoreType.DMA((count,)), pltpu.SemaphoreType.DMA((count,))]
-    if reduce:
-        scratch = [pltpu.VMEM((count,) + tail, values.dtype)] + scratch
+    def start():
+        def send(step, carry):
+            other = lax.rem(me + step, count)
+            copy(other, me).start()
+            return carry
+
+        lax.fori_loop(1, count, send, 0)
+
+    def finish():
+        def wait(step, carry):
+            other = lax.rem(me + count - step, count)
+            copy(other, other).wait()
+            return carry
+
+        lax.fori_loop(1, count, wait, 0)
+
+    return start, finish
+
+
+def closing_kernel(ndp, inner, *refs):
+    small_ref, first_ref, second_ref, out_ref, first_out, second_out = refs[:6]
+    land, first_land, second_land = refs[6:9]
+    sems = refs[9:]
+    count = ndp * inner
+    row, col = lax.axis_index("dp"), lax.axis_index("tensor")
+    me = row * inner + col
+
+    def anywhere(other):
+        return (lax.div(other, inner), lax.rem(other, inner))
+
+    def along(other):
+        return (other, col)
+
+    greet_all(count, me, anywhere)
+    moves = [
+        (swap_all(count, me, anywhere, lambda o: small_ref.at[o], land, *sems[0:2])),
+        (swap_all(ndp, row, along, lambda o: first_ref.at[o], first_land, *sems[2:4])),
+        (swap_all(ndp, row, along, lambda o: second_ref.at[o], second_land, *sems[4:6])),
+    ]
+    for start, _ in moves:
+        start()
+    land[me] = small_ref[me]
+    first_land[row] = first_ref[row]
+    second_land[row] = second_ref[row]
+    for _, finish in moves:
+        finish()
+    out_ref[...] = jnp.sum(land[...], axis=0)
+    first_out[...] = jnp.sum(first_land[...].astype(F32), axis=0)
+    second_out[...] = jnp.sum(second_land[...].astype(F32), axis=0)
+
+
+def closing(small, first, second, collective_id):
+    inner, ndp = lax.axis_size("tensor"), lax.axis_size("dp")
+    pair = [pltpu.SemaphoreType.DMA((ndp * inner,))] * 2
     return pl.pallas_call(
-        functools.partial(everyone_kernel, count, inner, reduce),
-        out_shape=jax.ShapeDtypeStruct(tail if reduce else (count,) + tail, values.dtype),
-        in_specs=[VMEM_SPEC],
-        out_specs=VMEM_SPEC,
-        scratch_shapes=scratch,
+        functools.partial(closing_kernel, ndp, inner),
+        out_shape=[
+            jax.ShapeDtypeStruct(small.shape[1:], F32),
+            jax.ShapeDtypeStruct(first.shape[1:], F32),
+            jax.ShapeDtypeStruct(second.shape[1:], F32),
+        ],
+        in_specs=[VMEM_SPEC] * 3,
+        out_specs=[VMEM_SPEC] * 3,
+        scratch_shapes=[
+            pltpu.VMEM(small.shape, F32),
+            pltpu.VMEM(first.shape, BF16),
+            pltpu.VMEM(second.shape, BF16),
+        ]
+        + pair
+        + [pltpu.SemaphoreType.DMA((ndp,))] * 4,
         compiler_params=pltpu.CompilerParams(
             collective_id=collective_id, has_side_effects=True, vmem_limit_bytes=VMEM_LIMIT
         ),
-        name="everyone",
-    )(values)
+        name="closing",
+    )(small, first, second)
 
 
 def normed(values, gain):
     return values * lax.rsqrt(jnp.mean(values * values, axis=-1, keepdims=True) + EPS) * gain
 
 
-def line_kernel(kind, nt, chunks, extra, *refs):
+def line_kernel(kind, nt, chunks, lag, extra, *refs):
     refs = list(refs)
     has_sum = kind != "start"
     has_gather = kind != "end"
     part = refs.pop(0) if has_sum else None
     if kind == "start":
-        x_ref, gain_ref = refs.pop(0), refs.pop(0)
+        x_ref, small_ref = refs.pop(0), refs.pop(0)
     elif kind == "fwd":
         extra_ref, gain_ref = refs.pop(0), refs.pop(0)
     elif kind == "last":
@@ -130,27 +157,43 @@
     own_ref = refs.pop(0) if has_sum else None
     gg_ref = refs.pop(0) if kind in ("bwd", "end") else None
     all_ref = refs.pop(0) if has_gather else None
+    land_ref = refs.pop(0) if kind == "start" else None
     if has_sum:
         from_left, from_right, tx, acc, rs_send, rl_sem, rr_sem = refs[:7]
         refs = refs[7:]
     if has_gather:
         ag_right, ag_left, ag_recv = refs[:3]
+        refs = refs[3:]
 
     me = lax.axis_index("tensor")
     has_l, has_r = me > 0, me < nt - 1
     left, right = jnp.maximum(me - 1, 0), jnp.minimum(me + 1, nt - 1)
 
-    barrier = pltpu.get_barrier_semaphore()
-
-    @pl.when(has_l)
-    def _():
-        pl.semaphore_signal(barrier, inc=1, device_id={"tensor": left}, device_id_type=MESH)
-
-    @pl.when(has_r)
-    def _():
-        pl.semaphore_signal(barrier, inc=1, device_id={"tensor": right}, device_id_type=MESH)
-
-    pl.semaphore_wait(barrier, has_l.astype(jnp.int32) + has_r.astype(jnp.int32))
+    if kind == "start":
+        count = lax.axis_size("dp") * nt
+        me_all = lax.axis_index("dp") * nt + me
+
+        def place(other):
+            return (lax.div(other, nt), lax.rem(other, nt))
+
+        greet_all(count, me_all, place)
+        small_start, small_finish = swap_all(
+            count, me_all, place, lambda other: small_ref, land_ref, *refs[:2]
+        )
+        small_start()
+        land_ref[me_all] = small_ref[...]
+    else:
+        barrier = pltpu.get_barrier_semaphore()
+
+        @pl.when(has_l)
+        def _():
+            pl.semaphore_signal(barrier, inc=1, device_id={"tensor": left}, device_id_type=MESH)
+
+        @pl.when(has_r)
+        def _():
+            pl.semaphore_signal(barrier, inc=1, device_id={"tensor": right}, device_id_type=MESH)
+
+        pl.semaphore_wait(barrier, has_l.astype(jnp.int32) + has_r.astype(jnp.int32))
 
     def copy(src, dst, send_sem, recv_sem, to):
         return pltpu.make_async_remote_copy(
@@ -204,22 +247,46 @@
             def _():
                 spread_left(j, c).start()
 
-    def relay(c, t):
-        j_up, j_down = nt - 1 - t, t
-
-        @pl.when(has_l & (me < j_up))
-        def _():
-            sum_right(j_up, c, tx.at[j_up, c]).wait_recv()
-            tx[j_up, c] = (part[j_up, c].astype(F32) + from_left[j_up, c].astype(F32)).astype(BF16)
-            sum_right(j_up, c, tx.at[j_up, c]).start()
-
-        @pl.when(has_r & (me > j_down))
-        def _():
-            sum_left(j_down, c, tx.at[j_down, c]).wait_recv()
-            tx[j_down, c] = (
-                part[j_down, c].astype(F32) + from_right[j_down, c].astype(F32)
+    hops = nt - 1
+
+    count = hops * chunks
+
+    def relay(step):
+        k = jnp.clip(step - lag * me, 0, count - 1)
+        c, j = lax.div(k, hops), hops - lax.rem(k, hops)
+
+        @pl.when(has_l & (step >= lag * me) & (step - lag * me < count) & (me < j))
+        def _():
+            sum_right(j, c, tx.at[j, c]).wait_recv()
+            tx[j, c] = (part[j, c].astype(F32) + from_left[j, c].astype(F32)).astype(BF16)
+            sum_right(j, c, tx.at[j, c]).start()
+
+        far = lag * (hops - me)
+        k_down = jnp.clip(step - far, 0, count - 1)
+        c_down, j_down = lax.div(k_down, hops), lax.rem(k_down, hops)
+
+        @pl.when(has_r & (step >= far) & (step - far < count) & (me > j_down))
+        def _():
+            sum_left(j_down, c_down, tx.at[j_down, c_down]).wait_recv()
+            tx[j_down, c_down] = (
+                part[j_down, c_down].astype(F32) + from_right[j_down, c_down].astype(F32)
             ).astype(BF16)
-            sum_left(j_down, c, tx.at[j_down, c]).start()
+            sum_left(j_down, c_down, tx.at[j_down, c_down]).start()
+
+    def push(first, last):
+        ks = range(min(first, count), min(last, count))
+
+        @pl.when(jnp.logical_not(has_l))
+        def _():
+            for k in ks:
+                j, c = hops - k % hops, k // hops
+                sum_right(j, c, part.at[j, c]).start()
+
+        @pl.when(jnp.logical_not(has_r))
+        def _():
+            for k in ks:
+                j, c = k % hops, k // hops
+                sum_left(j, c, part.at[j, c]).start()
 
     def own_rows(c):
         acc[...] = part[me, c].astype(F32)
@@ -263,40 +330,33 @@
 
     if kind == "start":
         for c in range(chunks):
-            all_ref[me, c] = normed(x_ref[c].astype(F32), gain_ref[...]).astype(BF16)
+            all_ref[me, c] = x_ref[c]
             offer(c)
         for c in range(chunks):
             for d in range(1, nt):
                 pass_on(c, d)
+        small_finish()
     else:
 
-        @pl.when(jnp.logical_not(has_l))
-        def _():
-            for c in range(chunks):
-                for j in range(nt - 1, 0, -1):
-                    sum_right(j, c, part.at[j, c]).start()
-
-        @pl.when(jnp.logical_not(has_r))
-        def _():
-            for c in range(chunks):
-                for j in range(nt - 1):
-                    sum_left(j, c, part.at[j, c]).start()
-
+        push(0, AHEAD)
         if kind == "last":
             for c in range(chunks):
                 all_ref[me, c] = og_ref[c]
             for c in range(chunks):
                 offer(c)
-        for c in range(chunks + (1 if has_gather and kind != "last" else 0)):
-            for t in range(nt - 1):
-                if c < chunks:
-                    relay(c, t)
-                if kind == "last":
-                    pass_on(c, t + 1)
-                elif has_gather and c >= 1:
-                    pass_on(c - 1, t + 1)
-            if c < chunks:
-                own_rows(c)
+        delay = 0 if kind == "last" else hops * lag
+        spreads = {}
+        for c in range(chunks if has_gather else 0):
+            for d in range(1, nt):
+                spreads.setdefault(delay + hops * c + lag * d, []).append((c, d))
+        final = max([hops * (chunks - 1 + lag)] + list(spreads))
+        for step in range(1, final + 1):
+            push(step + AHEAD - 1, step + AHEAD)
+            relay(step)
+            for c, d in spreads.get(step, ()):
+                pass_on(c, d)
+            if step % hops == 0 and 0 <= step // hops - lag < chunks:
+                own_rows(step // hops - lag)
 
     for c in range(chunks):
         for j in range(nt):
@@ -321,7 +381,7 @@
                     spread_left(j, c).wait_send()
 
 
-def line_exchange(kind, args, rows, width, collective_id, extra=False, chunks=2):
+def line_exchange(kind, args, rows, width, collective_id, extra=False, chunks=2, lag=2):
     nt = lax.axis_size("tensor")
     has_sum = kind != "start"
     has_gather = kind != "end"
@@ -341,6 +401,9 @@
         outs.append(jax.ShapeDtypeStruct((1, width), F32))
     if has_gather:
         outs.append(jax.ShapeDtypeStruct((nt, chunks, piece, width), BF16))
+    if kind == "start":
+        count = lax.axis_size("dp") * nt
+        outs.append(jax.ShapeDtypeStruct((count,) + args[1].shape, args[1].dtype))
     scratch = []
     sems = pltpu.SemaphoreType.DMA((nt, chunks))
     if has_sum:
@@ -348,8 +411,10 @@
         scratch += [buf, buf, buf, pltpu.VMEM((piece, width), F32), sems, sems, sems]
     if has_gather:
         scratch += [sems, sems, sems]
+    if kind == "start":
+        scratch += [pltpu.SemaphoreType.DMA((count,))] * 2
     results = pl.pallas_call(
-        functools.partial(line_kernel, kind, nt, chunks, extra),
+        functools.partial(line_kernel, kind, nt, chunks, lag, extra),
         out_shape=outs,
         in_specs=[VMEM_SPEC] * len(split),
         out_specs=[VMEM_SPEC] * len(outs),
@@ -366,7 +431,8 @@
     if has_sum:
         results[0] = results[0].reshape(rows, width)
     if has_gather:
-        results[-1] = results[-1].reshape(nt * rows, width)
+        at = 0 if kind == "start" else -1
+        results[at] = results[at].reshape(nt * rows, width)
     return results
 
 
@@ -387,7 +453,13 @@
     return (row_at // segment + 1) * segment
 
 
-def attend_kernel(heads, spans, block, starts_ref, a_ref, w_ref, qkv_ref, o_ref, lse_ref, out_ref):
+def attend_kernel(heads, spans, block, raw, starts_ref, a_ref, w_ref, *refs):
+    if raw:
+        gain_ref, qkv_ref, o_ref, lse_ref, out_ref, normed_ref = refs
+        normed_ref[...] = normed(a_ref[...].astype(F32), gain_ref[...]).astype(BF16)
+        a_ref = normed_ref
+    else:
+        qkv_ref, o_ref, lse_ref, out_ref = refs
     seq_len = a_ref.shape[0]
     wide = heads * HEAD
     factor = HEAD ** (-0.5)
@@ -409,20 +481,22 @@
     out_ref[...] = dot_nt(o_ref[...], w_ref[:, 3 * wide :]).astype(BF16)
 
 
-def attend_forward(starts, a_all, w_attn, heads):
+def attend_forward(starts, a_all, w_attn, heads, gain=None):
     seq_len, width = a_all.shape
     wide = heads * HEAD
     spans = starts.shape[1]
+    raw = gain is not None
     return pl.pallas_call(
-        functools.partial(attend_kernel, heads, spans, PIC),
+        functools.partial(attend_kernel, heads, spans, PIC, raw),
         out_shape=[
             jax.ShapeDtypeStruct((seq_len, 3 * wide), BF16),
             jax.ShapeDtypeStruct((seq_len, wide), BF16),
             jax.ShapeDtypeStruct((seq_len, heads), F32),
             jax.ShapeDtypeStruct((seq_len, width), BF16),
-        ],
-        in_specs=[pl.BlockSpec(memory_space=pltpu.SMEM), VMEM_SPEC, VMEM_SPEC],
-        out_specs=[VMEM_SPEC] * 4,
+        ]
+        + [jax.ShapeDtypeStruct((seq_len, width), BF16)] * raw,
+        in_specs=[pl.BlockSpec(memory_space=pltpu.SMEM)] + [VMEM_SPEC] * (2 + raw),
+        out_specs=[VMEM_SPEC] * (4 + raw),
         compiler_params=pltpu.CompilerParams(vmem_limit_bytes=VMEM_LIMIT),
         cost_estimate=pl.CostEstimate(
             flops=8 * seq_len * width * wide + 4 * heads * seq_len * seq_len * HEAD,
@@ -430,7 +504,7 @@
             transcendentals=heads * seq_len * seq_len,
         ),
         name="attend_forward",
-    )(starts, a_all, w_attn)
+    )(starts, a_all, w_attn, *([gain] if raw else []))
 
 
 def attend_back_kernel(
@@ -739,7 +813,9 @@
         + [const_mix[l, j] for l in range(layers) for j in range(consts)],
         axis=1,
     )
-    small = everyone(lanes(packed), False, 0).reshape(width, LANES)
+    hidden = hidden_in.astype(F32)
+    x_all, small = line_exchange("start", [hidden_in, lanes(packed)], own, width, 0)
+    small = small.reshape(width, LANES)
     at = 0
     fields = {}
     for name, size in (
@@ -774,16 +850,20 @@
     pos = [slot_table(routes[l]) for l in range(layers)]
     rowpos = [p[:, :EXPERTS].T[:, None, :] for p in pos]
 
-    hidden = hidden_in.astype(F32)
-    gain = field("attn", 0, 1).astype(F32).T
-    (a_all,) = line_exchange("start", [hidden_in, gain], own, width, 1)
+    a_all = None
     z_prev = lanes(prev_logits)
     next_id = 2
     stored = []
     for l in range(layers):
         mix = jnp.pad(gate_mix[l].astype(F32), ((0, LANES - NEXP), (0, LANES - NEXP)))
         zterm = jnp.dot(z_prev, mix, precision=HIGH)
-        qkv, o, lse, partial = attend_forward(span_starts, a_all, attn_w[l], heads)
+        if l == 0:
+            gain = field("attn", 0, 1).astype(F32).T
+            qkv, o, lse, partial, a_all = attend_forward(
+                span_starts, x_all, attn_w[l], heads, gain
+            )
+        else:
+            qkv, o, lse, partial = attend_forward(span_starts, a_all, attn_w[l], heads)
         gain = field("moe", l, 1).astype(F32).T
         mid, b_all = line_exchange("fwd", [partial, hidden, gain], own, width, next_id)
         router_l = lanes(field("router", l, NEXP))
@@ -859,6 +939,8 @@
             s["router"].T, cap,
         )
         exp_grads[l] = lax.psum_scatter(gw_exp, "dp", scatter_dimension=0, tiled=False)
+        if l + 1 < layers:
+            partial, exp_grads[l + 1] = lax.optimization_barrier((partial, exp_grads[l + 1]))
         z_high, z_low = two_parts(gz)
         routers[l] = (dot_tn(s["b_all"], z_high) + dot_tn(s["b_all"], z_low))[:, :NEXP]
         mixes[l] = lax.dot_general(
@@ -873,9 +955,7 @@
         partial, gw_attn = attend_backward(
             span_starts, g_all, attn_w[l], s["a_all"], s["qkv"], s["o"], s["lse"], heads
         )
-        attn_grads[l] = lax.psum_scatter(
-            gw_attn.reshape(ndp, rows, 4 * wide), "dp", scatter_dimension=0, tiled=False
-        )
+        attn_grads[l] = gw_attn.reshape(ndp, rows, 4 * wide)
         gain = field("attn", l, 1).astype(F32).T
         if l > 0:
             grad, gains_a[l], g_all = line_exchange(
@@ -900,7 +980,7 @@
     mix_rows = -(-flat.shape[0] // LANES)
     flat = jnp.pad(flat, (0, mix_rows * LANES - flat.shape[0])).reshape(1, mix_rows, LANES)
     flat = jnp.broadcast_to(flat, (ndp * nt, mix_rows, LANES))
-    total = everyone(jnp.concatenate([sums, flat], axis=1), True, next_id)
+    total, *attn_grads = closing(jnp.concatenate([sums, flat], axis=1), *attn_grads, next_id)
     mix_total = total[cols:].reshape(-1)[: layers * NEXP * NEXP].reshape(layers, NEXP, NEXP)
     total = total[:cols]
 
@@ -913,8 +993,8 @@
     cvec_grad = back("cvec").T.reshape(layers, consts, cols)
     qkv_grad = jnp.stack(
         [item[:, : 3 * wide].reshape(rows, 3, wide) for item in attn_grads]
-    ).astype(F32)
-    outw_grad = jnp.stack([item[:, 3 * wide :].T for item in attn_grads]).astype(F32)
+    )
+    outw_grad = jnp.stack([item[:, 3 * wide :].T for item in attn_grads])
     up_grad = jnp.stack(
         [item[:, :, : 2 * half].reshape(EXPERTS, rows, 2, half) for item in exp_grads]
     ).astype(F32)

time: 1060 us -> 830 us (0.78)
  waiting for transfers between devices: 221 us -> 0.15 us
  Pallas kernels: 687 us -> 642 us
  local copies, waits for them, and re-layouts: 72.4 us -> 94.4 us
    reduce_scatter x2, waiting for transfers between devices: 219 us -> 0.01 us  [shards(): lax.psum_scatter(gw_exp, 'dp', scatter_dimension=0, tiled=False)]
    pallas_call x13 -> x12, Pallas kernels: 534 us -> 490 us  [the longest x9 419 us: line_exchange(): pl.pallas_call(functools.partial(line_kernel, kind, nt, chunks, lag, extr...]
  transfers between devices with their start and end apart: 8 -> 6, of which waited for: 2 -> 0; matrix products, arithmetic and copies ran while one was open for 7% -> 11% of each run, Pallas kernels for 43% -> 66%
where the time goes in v2:
time: 830 us; the launch traced here: 822 us
  Pallas kernels  642 us (77%)
  local copies, waits for them, and re-layouts  94.4 us (11%)
  other arithmetic  51.2 us (6%)
  matrix products  18.5 us (2%)
  between operations  15.5 us (2%)
    pallas_call x9, Pallas kernels, line_exchange(): pl.pallas_call(functools.partial(line_kernel, kind, nt, chunks, lag, extr...  419 us
    pallas_call x2, Pallas kernels, experts_backward(): pl.pallas_call(functools.partial(experts_back_kernel, cap), grid=(count,)...  67.7 us
    pallas_call x2, Pallas kernels, experts_forward(): pl.pallas_call(functools.partial(experts_kernel, cap), grid=(count,), out...  45.9 us
    pallas_call x1, Pallas kernels, closing(): pl.pallas_call(functools.partial(closing_kernel, ndp, inner), out_shape=[...  44.3 us
    pallas_call x2, Pallas kernels, attend_backward(): pl.pallas_call(functools.partial(attend_back_kernel, heads, spans, PIC),...  39.4 us
    pallas_call x2, Pallas kernels, attend_forward(): pl.pallas_call(functools.partial(attend_kernel, heads, spans, PIC, raw),...  25.8 us
    unnamed x147, local copies, waits for them, and re-layouts  16.7 us
  transfers between devices with their start and end apart: 6, of which 0 were waited for; matrix products, arithmetic and copies ran while one was open for 11% of the time, Pallas kernels for 66%

profile of v2, /device:TPU:0, one launch (start us, length us, event | category | flops | bytes accessed | tf_op | source)
XLA Modules:
  0.0 822.4 jit_solution(1984536905729569976)
XLA Ops:
  10.3 5.0 fusion.66
  15.3 2.8 reshape_squeeze.13
  24.6 2.7 pad_maximum_fusion.1
  30.5 43.1 %line_start.1 = (bf16[4,2,128,768]{3,2,1,0:T(8,128)(2,1)}, bf16[32,24,128]{2,1,0:T(8,128)(2,1)}) custom-call(bf16[2,128,768]{2,1,0:T(8,128)(2,1)} %bitcast.254, bf16[24,128]{1,0:T(8,128)(2,1)} %pad.43.refs_1_), custom_call_target="tpu_custom_call" | custom-call | flops 7864320 | bytes 78643200 | tf_op jit(solution)/shard_map/line_start/pallas_call | solution.py:416
  89.1 13.4 %attend_forward.2 = (bf16[1024,576]{1,0:T(8,128)(2,1)}, bf16[1024,192]{1,0:T(8,128)(2,1)}, f32[1024,3]{1,0:T(8,128)}, bf16[1024,768]{1,0:T(8,128)(2,1)}, bf16[1024,768]{1,0:T(8,128)(2,1)}) custom-call(s32[1,2]{1,0:T(1,128)} %starts_ref.7, bf16[1024,768]{1,0:T(8,128)(2,1)} %bitcast.307, bf16[768,768]{1,0:T(8,128)(2,1)} %all-gather.9.cloned.1.call-done.w_ref, ...), custom_call_target="tpu_custom_call" | custom-call | flops 2013265920 | bytes 4718592 | tf_op jit(solution)/shard_map/attend_forward/pallas_call | solution.py:489
  102.6 57.2 %line_fwd.3 = (f32[2,128,768]{2,1,0:T(8,128)}, bf16[4,2,128,768]{3,2,1,0:T(8,128)(2,1)}) custom-call(bf16[4,2,128,768]{3,2,1,0:T(8,128)(2,1)} %bitcast.252, f32[2,128,768]{2,1,0:T(8,128)} %reshape.254.refs_1_, f32[1,768]{1,0:T(1,128)} %reshape.292.refs_2_.refs_4_), custom_call_target="tpu_custom_call" | custom-call | flops 7864320 | bytes 78643200 | tf_op jit(solution)/shard_map/line_fwd/pallas_call | solution.py:416
  162.2 23.5 %experts_forward.2 = (bf16[8,256,768]{2,1,0:T(8,128)(2,1)}, bf16[8,256,1024]{2,1,0:T(8,128)(2,1)}, f32[1024,128]{1,0:T(8,128)}, f32[1024,128]{1,0:T(8,128)}, bf16[1024,768]{1,0:T(8,128)(2,1)}) custom-call(bf16[1024,768]{1,0:T(8,128)(2,1)} %bitcast.227, bf16[8,8,96,1536]{3,2,1,0:T(8,128)(2,1)} %bitcast.301, s32[8,1,1024]{2,1,0:T(1,128)} %copy.319.rowpos_ref, ...), custom_call_target="tpu_custom_call" | custom-call | flops 11274289152 | bytes 18874368 | tf_op jit(solution)/shard_map/experts_forward/pallas_call | solution.py:631
  190.2 55.6 %line_fwd.4 = (f32[2,128,768]{2,1,0:T(8,128)}, bf16[4,2,128,768]{3,2,1,0:T(8,128)(2,1)}) custom-call(bf16[4,2,128,768]{3,2,1,0:T(8,128)(2,1)} %bitcast.249, f32[2,128,768]{2,1,0:T(8,128)} %bitcast.242, f32[1,768]{1,0:T(1,128)} %reshape.293.refs_2_.refs_3_), custom_call_target="tpu_custom_call" | custom-call | flops 7864320 | bytes 78643200 | tf_op jit(solution)/shard_map/line_fwd/pallas_call | solution.py:416
  245.9 12.4 %attend_forward.3 = (bf16[1024,576]{1,0:T(8,128)(2,1)}, bf16[1024,192]{1,0:T(8,128)(2,1)}, f32[1024,3]{1,0:T(8,128)}, bf16[1024,768]{1,0:T(8,128)(2,1)}) custom-call(s32[1,2]{1,0:T(1,128)} %starts_ref.7, bf16[1024,768]{1,0:T(8,128)(2,1)} %bitcast.305, bf16[768,768]{1,0:T(8,128)(2,1)} %all-gather.13.cloned.1.call-done.w_ref), custom_call_target="tpu_custom_call" | custom-call | flops 2013265920 | bytes 4718592 | tf_op jit(solution)/shard_map/attend_forward/pallas_call | solution.py:489
  258.3 53.4 %line_fwd.5 = (f32[2,128,768]{2,1,0:T(8,128)}, bf16[4,2,128,768]{3,2,1,0:T(8,128)(2,1)}) custom-call(bf16[4,2,128,768]{3,2,1,0:T(8,128)(2,1)} %bitcast.253, f32[2,128,768]{2,1,0:T(8,128)} %get-tuple-element.75.refs_1_, f32[1,768]{1,0:T(1,128)} %reshape.294.refs_2_.refs_4_), custom_call_target="tpu_custom_call" | custom-call | flops 7864320 | bytes 78643200 | tf_op jit(solution)/shard_map/line_fwd/pallas_call | solution.py:416
  316.3 22.4 %experts_forward.3 = (bf16[8,256,768]{2,1,0:T(8,128)(2,1)}, bf16[8,256,1024]{2,1,0:T(8,128)(2,1)}, f32[1024,128]{1,0:T(8,128)}, f32[1024,128]{1,0:T(8,128)}, bf16[1024,768]{1,0:T(8,128)(2,1)}) custom-call(bf16[1024,768]{1,0:T(8,128)(2,1)} %bitcast.235, bf16[8,8,96,1536]{3,2,1,0:T(8,128)(2,1)} %bitcast.303, s32[8,1,1024]{2,1,0:T(1,128)} %copy.330.rowpos_ref, ...), custom_call_target="tpu_custom_call" | custom-call | flops 11274289152 | bytes 18874368 | tf_op jit(solution)/shard_map/experts_forward/pallas_call | solution.py:631
  354.8 2.5 multiply_reduce_fusion.6
  363.7 2.9 multiply_add_fusion.1
  366.6 40.5 %line_last.1 = (f32[2,128,768]{2,1,0:T(8,128)}, bf16[4,2,128,768]{3,2,1,0:T(8,128)(2,1)}) custom-call(bf16[4,2,128,768]{3,2,1,0:T(8,128)(2,1)} %bitcast.257, f32[2,128,768]{2,1,0:T(8,128)} %bitcast.243, bf16[2,128,768]{2,1,0:T(8,128)(2,1)} %bitcast.240), custom_call_target="tpu_custom_call" | custom-call | flops 7864320 | bytes 78643200 | tf_op jit(solution)/shard_map/line_last/pallas_call | solution.py:416
  408.4 33.6 %experts_backward.2 = (bf16[8,8,96,1536]{3,2,1,0:T(8,128)(2,1)}, f32[1024,128]{1,0:T(8,128)}, bf16[1024,768]{1,0:T(8,128)(2,1)}) custom-call(bf16[1024,768]{1,0:T(8,128)(2,1)} %bitcast.309, bf16[8,8,96,1536]{3,2,1,0:T(8,128)(2,1)} %bitcast.304, bf16[8,256,768]{2,1,0:T(8,128)(2,1)} %get-tuple-element.83.x_ref, ...), custom_call_target="tpu_custom_call" | custom-call | flops 16106127360 | bytes 37748736 | tf_op jit(solution)/shard_map/experts_backward/pallas_call | solution.py:728
  445.3 53.2 %line_bwd.3 = (f32[2,128,768]{2,1,0:T(8,128)}, f32[1,768]{1,0:T(1,128)}, bf16[4,2,128,768]{3,2,1,0:T(8,128)(2,1)}) custom-call(bf16[4,2,128,768]{3,2,1,0:T(8,128)(2,1)} %bitcast.258, f32[2,128,768]{2,1,0:T(8,128)} %bitcast.244, f32[2,128,768]{2,1,0:T(8,128)} %get-tuple-element.79.refs_2_, f32[2,128,768]{2,1,0:T(8,128)} %convert.15.refs_3_, ...), custom_call_target="tpu_custom_call" | custom-call | flops 7864320 | bytes 78643200 | tf_op jit(solution)/shard_map/line_bwd/pallas_call | solution.py:416
  498.6 19.6 %attend_backward.2 = (bf16[1024,768]{1,0:T(8,128)(2,1)}, bf16[768,768]{1,0:T(8,128)(2,1)}) custom-call(s32[1,2]{1,0:T(1,128)} %starts_ref.7, bf16[1024,768]{1,0:T(8,128)(2,1)} %bitcast.310, bf16[768,768]{1,0:T(8,128)(2,1)} %all-gather.13.cloned.1.call-done.w_ref, bf16[1024,768]{1,0:T(8,128)(2,1)} %bitcast.306, bf16[1024,576]{1,0:T(8,128)(2,1)} %get-tuple-element.87.qkv_ref, ...), custom_call_target="tpu_custom_call" | custom-call | flops 4429185024 | bytes 9437184 | tf_op jit(solution)/shard_map/attend_backward/pallas_call | solution.py:548
  518.2 47.2 %line_bwd.4 = (f32[2,128,768]{2,1,0:T(8,128)}, f32[1,768]{1,0:T(1,128)}, bf16[4,2,128,768]{3,2,1,0:T(8,128)(2,1)}) custom-call(bf16[4,2,128,768]{3,2,1,0:T(8,128)(2,1)} %bitcast.250, f32[2,128,768]{2,1,0:T(8,128)} %get-tuple-element.75.refs_1_, f32[2,128,768]{2,1,0:T(8,128)} %get-tuple-element.91.refs_2_, f32[1,768]{1,0:T(1,128)} %reshape.293.refs_2_.refs_3_), custom_call_target="tpu_custom_call" | custom-call | flops 7864320 | bytes 78643200 | tf_op jit(solution)/shard_map/line_bwd/pallas_call | solution.py:416
  575.3 34.1 %experts_backward.3 = (bf16[8,8,96,1536]{3,2,1,0:T(8,128)(2,1)}, f32[1024,128]{1,0:T(8,128)}, bf16[1024,768]{1,0:T(8,128)(2,1)}) custom-call(bf16[1024,768]{1,0:T(8,128)(2,1)} %bitcast.308, bf16[8,8,96,1536]{3,2,1,0:T(8,128)(2,1)} %bitcast.302, bf16[8,256,768]{2,1,0:T(8,128)(2,1)} %get-tuple-element.93.x_ref, ...), custom_call_target="tpu_custom_call" | custom-call | flops 16106127360 | bytes 37748736 | tf_op jit(solution)/shard_map/experts_backward/pallas_call | solution.py:728
  633.5 45.4 %line_bwd.5 = (f32[2,128,768]{2,1,0:T(8,128)}, f32[1,768]{1,0:T(1,128)}, bf16[4,2,128,768]{3,2,1,0:T(8,128)(2,1)}) custom-call(bf16[4,2,128,768]{3,2,1,0:T(8,128)(2,1)} %bitcast.256, f32[2,128,768]{2,1,0:T(8,128)} %multiply_add_fusion.refs_1_, f32[2,128,768]{2,1,0:T(8,128)} %get-tuple-element.71.refs_2_, f32[2,128,768]{2,1,0:T(8,128)} %get-tuple-element.95.refs_3_, ...), custom_call_target="tpu_custom_call" | custom-call | flops 7864320 | bytes 78643200 | tf_op jit(solution)/shard_map/line_bwd/pallas_call | solution.py:416
  678.9 19.8 %attend_backward.3 = (bf16[1024,768]{1,0:T(8,128)(2,1)}, bf16[768,768]{1,0:T(8,128)(2,1)}) custom-call(s32[1,2]{1,0:T(1,128)} %starts_ref.7, bf16[1024,768]{1,0:T(8,128)(2,1)} %bitcast.311, bf16[768,768]{1,0:T(8,128)(2,1)} %all-gather.9.cloned.1.call-done.w_ref, bf16[1024,768]{1,0:T(8,128)(2,1)} %get-tuple-element.101.a_ref, ...), custom_call_target="tpu_custom_call" | custom-call | flops 4429185024 | bytes 9437184 | tf_op jit(solution)/shard_map/attend_backward/pallas_call | solution.py:548
  698.7 23.8 %line_end.1 = (f32[2,128,768]{2,1,0:T(8,128)}, f32[1,768]{1,0:T(1,128)}) custom-call(bf16[4,2,128,768]{3,2,1,0:T(8,128)(2,1)} %bitcast.251, f32[2,128,768]{2,1,0:T(8,128)} %reshape.254.refs_1_, f32[2,128,768]{2,1,0:T(8,128)} %get-tuple-element.106.refs_2_, f32[1,768]{1,0:T(1,128)} %reshape.291.refs_0_.refs_3_), custom_call_target="tpu_custom_call" | custom-call | flops 7864320 | bytes 78643200 | tf_op jit(solution)/shard_map/line_end/pallas_call | solution.py:416
  724.5 44.3 %closing.1 = (f32[27,128]{1,0:T(8,128)}, f32[96,768]{1,0:T(8,128)}, f32[96,768]{1,0:T(8,128)}) custom-call(f32[32,27,128]{2,1,0:T(8,128)} %pad_maximum_fusion.3.refs_0_, bf16[8,96,768]{2,1,0:T(8,128)(2,1)} %bitcast.261, bf16[8,96,768]{2,1,0:T(8,128)(2,1)} %bitcast.260), custom_call_target="tpu_custom_call" | custom-call | tf_op jit(solution)/shard_map/closing/pallas_call | solution.py:116
  802.9 8.3 %maximum_convert_fusion = f32[2,8,96,2,512]{4,3,2,1,0:T(2,128)} fusion(bf16[1,8,96,2,512]{4,3,2,1,0:T(2,128)(2,1)S(1)} %copy-done.7, bf16[1,8,96,2,512]{4,3,2,1,0:T(2,128)(2,1)} %stack_reshape.14), kind=kLoop, calls=%fused_computation.3 | loop fusion | flops 3145728 | bytes 9437184 | tf_op jit(solution)/shard_map/convert_element_type | solution.py:1000
  (325 shorter events, 140.3 us)
Async XLA Ops:
  7.2 82.0 %all-gather.9.cloned.1.call-start = ((), (), s32[]{:S(2)}) async-start(), calls=%async_computation.4 | async-start | bytes 1327104 | tf_op jit(solution)/shard_map/all_gather | solution.py:840
  10.3 151.4 %all-gather.11.cloned.1.call-start = ((), (), s32[]{:S(2)}) async-start(), calls=%async_computation.5 | async-start | bytes 21233664 | tf_op jit(solution)/shard_map/all_gather | solution.py:848
  22.1 223.7 %all-gather.13.cloned.1.call-start = ((), (), s32[]{:S(2)}) async-start(), calls=%async_computation.6 | async-start | bytes 1327104 | tf_op jit(solution)/shard_map/all_gather | solution.py:840
  23.4 292.9 %all-gather.15.cloned.1.call-start = ((), (), s32[]{:S(2)}) async-start(), calls=%async_computation.7 | async-start | bytes 21233664 | tf_op jit(solution)/shard_map/all_gather | solution.py:848
  27.3 49.2 %copy-start.52 = (s32[2,1024,2]{1,2,0:T(2,128)S(1)}, s32[2,1024,2]{1,2,0:T(2,128)}, u32[]{:S(2)}) copy-start(s32[2,1024,2]{1,2,0:T(2,128)} %param.17) | copy-start | bytes 49156
  27.4 606.1 %reduce-scatter.3.cloned.1.call-start = ((), (), s32[]{:S(2)}) async-start(), calls=%async_computation.2 | async-start | bytes 21233664 | tf_op jit(solution)/shard_map/reduce_scatter | solution.py:941
  84.6 230.5 %copy-start.37 = (bf16[12,12]{1,0:T(8,128)(2,1)}, bf16[12,12]{1,0:T(8,128)(2,1)S(1)}, u32[]{:S(2)}) copy-start(bf16[12,12]{1,0:T(8,128)(2,1)S(1)} %get-tuple-element.264) | copy-start | bytes 868
  161.1 24.6 %copy-start.39 = (f32[256,4]{0,1:T(4,128)}, f32[256,4]{0,1:T(4,128)S(1)}, u32[]{:S(2)}) copy-start(f32[256,4]{0,1:T(4,128)S(1)} %fusion.29) | copy-start | bytes 12292
  161.3 24.4 %copy-start.44 = (f32[256,2]{0,1:T(2,128)}, f32[256,2]{0,1:T(2,128)S(1)}, u32[]{:S(2)}) copy-start(f32[256,2]{0,1:T(2,128)S(1)} %reduce_max.18) | copy-start | bytes 6148
  161.6 26.5 %copy-start.13 = (f32[256,2,2]{1,0,2:T(8,128)}, f32[256,2,2]{1,0,2:T(8,128)S(1)}, u32[]{:S(2)}) copy-start(f32[256,2,2]{1,0,2:T(8,128)S(1)} %fusion.31) | copy-start | bytes 12292
  162.2 26.9 %copy-start.2 = (bf16[4,2,128,768]{3,2,1,0:T(8,128)(2,1)S(1)}, bf16[4,2,128,768]{3,2,1,0:T(8,128)(2,1)}, u32[]{:S(2)}) copy-start(bf16[4,2,128,768]{3,2,1,0:T(8,128)(2,1)} %get-tuple-element.69) | copy-start | bytes 4718596
  186.9 58.9 %copy-start.22 = (f32[256,2]{1,0:T(8,128)}, f32[256,2]{1,0:T(8,128)S(1)}, u32[]{:S(2)}) copy-start(f32[256,2]{1,0:T(8,128)S(1)} %get-tuple-element.220) | copy-start | bytes 6148
  188.1 57.7 %copy-start.53 = (f32[256]{0:T(256)}, f32[256]{0:T(256)S(1)}, u32[]{:S(2)}) copy-start(f32[256]{0:T(256)S(1)} %fusion.40) | copy-start | bytes 3076
  258.3 55.0 %copy-start.4 = (bf16[256,768]{1,0:T(8,128)(2,1)S(1)}, bf16[256,768]{1,0:T(8,128)(2,1)}, u32[]{:S(2)}) copy-start(bf16[256,768]{1,0:T(8,128)(2,1)} %param.29) | copy-start | bytes 1179652
  258.3 56.9 %copy-start.17 = (f32[1024,128]{1,0:T(8,128)S(1)}, f32[1024,128]{1,0:T(8,128)}, u32[]{:S(2)}) copy-start(f32[1024,128]{1,0:T(8,128)} %get-tuple-element.77) | copy-start | bytes 1572868
  313.0 25.7 %copy-start.41 = (f32[256,4]{0,1:T(4,128)}, f32[256,4]{0,1:T(4,128)S(1)}, u32[]{:S(2)}) copy-start(f32[256,4]{0,1:T(4,128)S(1)} %fusion.25) | copy-start | bytes 12292
  313.2 26.7 %copy-start.46 = (f32[256,2]{0,1:T(2,128)}, f32[256,2]{0,1:T(2,128)S(1)}, u32[]{:S(2)}) copy-start(f32[256,2]{0,1:T(2,128)S(1)} %reduce_max.19) | copy-start | bytes 6148
  314.5 25.2 %copy-start.51 = (f32[256]{0:T(256)}, f32[256]{0:T(256)S(1)}, u32[]{:S(2)}) copy-start(f32[256]{0:T(256)S(1)} %get-tuple-element.202) | copy-start | bytes 3076
  366.6 40.6 %copy-start.28 = (f32[256,1]{1,0:T(8,128)S(1)}, f32[256,1]{1,0:T(8,128)}, u32[]{:S(2)}) copy-start(f32[256,1]{1,0:T(8,128)} %copy.336) | copy-start | bytes 3076
  366.6 40.6 %copy-start.29 = (f32[256,2]{1,0:T(8,128)S(1)}, f32[256,2]{1,0:T(8,128)}, u32[]{:S(2)}) copy-start(f32[256,2]{1,0:T(8,128)} %get-tuple-element.229) | copy-start | bytes 6148
  442.0 339.9 %reduce-scatter.5.cloned.1.call-start = ((), (), s32[]{:S(2)}) async-start(), calls=%async_computation.3 | async-start | bytes 21233664 | tf_op jit(solution)/shard_map/reduce_scatter | solution.py:941
  698.7 23.8 %copy-start.55 = (f32[1,768]{1,0:T(1,128)S(1)}, f32[1,768]{1,0:T(1,128)}, u32[]{:S(2)}) copy-start(f32[1,768]{1,0:T(1,128)} %get-tuple-element.111) | copy-start | bytes 9220
  698.7 23.8 %copy-start.56 = (f32[1,768]{1,0:T(1,128)S(1)}, f32[1,768]{1,0:T(1,128)}, u32[]{:S(2)}) copy-start(f32[1,768]{1,0:T(1,128)} %get-tuple-element.109) | copy-start | bytes 9220
  698.7 23.8 %copy-start.57 = (f32[1,768]{1,0:T(1,128)S(1)}, f32[1,768]{1,0:T(1,128)}, u32[]{:S(2)}) copy-start(f32[1,768]{1,0:T(1,128)} %get-tuple-element.110) | copy-start | bytes 9220
  (44 other events, 143.5 us)
Sparse Core Ops, SparseCore 0:
  10.4 26.6 all-gather.8
  39.6 98.5 all-gather.10
  140.1 23.9 all-gather.12
  165.8 98.5 all-gather.14
  442.1 126.4 reduce-scatter.2
  609.6 129.2 reduce-scatter.4

commit v3 on v2

--- a/solution.py
+++ b/solution.py
@@ -21,6 +21,9 @@
 BF16 = jnp.bfloat16
 VMEM_SPEC = pl.BlockSpec(memory_space=pltpu.VMEM)
 AHEAD = 2
+PIECES = 16
+LAG = 2
+MIX_STEP = 16
 VMEM_LIMIT = 60 * 1024 * 1024
 
 
@@ -34,6 +37,24 @@
 
 def dot_tn(a, b):
     return lax.dot_general(a, b, (((0,), (0,)), ((), ())), preferred_element_type=F32)
+
+
+def layout(layers, consts):
+    at, begin = {}, 0
+    for name, size in (
+        ("attn", layers),
+        ("moe", layers),
+        ("router", layers * NEXP),
+        ("cvec", layers * consts),
+        ("cmix", layers * consts * 2),
+    ):
+        at[name] = begin
+        begin += size
+    return at
+
+
+def shift(values, lanes_up):
+    return pltpu.roll(values, lanes_up % LANES, 1)
 
 
 def greet_all(count, me, place):
@@ -78,13 +99,18 @@
     return start, finish
 
 
-def closing_kernel(ndp, inner, *refs):
-    small_ref, first_ref, second_ref, out_ref, first_out, second_out = refs[:6]
-    land, first_land, second_land = refs[6:9]
-    sems = refs[9:]
+def closing_kernel(ndp, inner, layers, consts, wide, *refs):
+    small_ref, proj_refs = refs[0], refs[1 : 1 + layers]
+    refs = refs[1 + layers :]
+    attn_out, moe_out, router_out, mix_out, cvec_out, cmix_out, qkv_out, outw_out = refs[:8]
+    land, proj_lands = refs[8], refs[9 : 9 + layers]
+    square, tall = refs[9 + layers : 11 + layers]
+    sems = refs[11 + layers :]
     count = ndp * inner
     row, col = lax.axis_index("dp"), lax.axis_index("tensor")
     me = row * inner + col
+    cols = attn_out.shape[1]
+    rows = qkv_out.shape[1]
 
     def anywhere(other):
         return (lax.div(other, inner), lax.rem(other, inner))
@@ -92,48 +118,204 @@
     def along(other):
         return (other, col)
 
+    def piece(ref):
+        return lambda other: ref.at[other]
+
     greet_all(count, me, anywhere)
     moves = [
-        (swap_all(count, me, anywhere, lambda o: small_ref.at[o], land, *sems[0:2])),
-        (swap_all(ndp, row, along, lambda o: first_ref.at[o], first_land, *sems[2:4])),
-        (swap_all(ndp, row, along, lambda o: second_ref.at[o], second_land, *sems[4:6])),
-    ]
+        swap_all(ndp, row, along, piece(ref), to, *sems[2 + 2 * l : 4 + 2 * l])
+        for l, (ref, to) in enumerate(zip(proj_refs, proj_lands))
+    ] + [swap_all(count, me, anywhere, piece(small_ref), land, *sems[0:2])]
     for start, _ in moves:
         start()
     land[me] = small_ref[me]
-    first_land[row] = first_ref[row]
-    second_land[row] = second_ref[row]
-    for _, finish in moves:
-        finish()
-    out_ref[...] = jnp.sum(land[...], axis=0)
-    first_out[...] = jnp.sum(first_land[...].astype(F32), axis=0)
-    second_out[...] = jnp.sum(second_land[...].astype(F32), axis=0)
-
-
-def closing(small, first, second, collective_id):
+    for ref, to in zip(proj_refs, proj_lands):
+        to[row] = ref[row]
+    square[...] = jnp.zeros_like(square)
+    tall[...] = jnp.zeros_like(tall)
+    for l in range(layers):
+        moves[l][1]()
+        total = jnp.sum(proj_lands[l][...].astype(F32), axis=0)
+        for part in range(3):
+            qkv_out[l, :, part, :] = total[:, part * wide : (part + 1) * wide]
+        tall[:rows, :wide] = total[:, 3 * wide :]
+        outw_out[l] = tall[...].T[:wide, :rows]
+    moves[layers][1]()
+    total = jnp.sum(land[...], axis=0)
+    square[:cols, :] = total[:cols]
+    turned = square[...].T
+    at = layout(layers, consts)
+    attn_out[...] = turned[at["attn"] : at["attn"] + layers, :cols]
+    moe_out[...] = turned[at["moe"] : at["moe"] + layers, :cols]
+    for l in range(layers):
+        begin = at["router"] + l * NEXP
+        router_out[l] = total[:cols, begin : begin + NEXP]
+        mix_out[l] = total[cols : cols + NEXP, l * MIX_STEP : l * MIX_STEP + NEXP]
+        begin = at["cvec"] + l * consts
+        cvec_out[l] = turned[begin : begin + consts, :cols]
+        begin = at["cmix"] + l * 2 * consts
+        for j in range(consts):
+            for k in range(2):
+                lane = begin + k * consts + j
+                cmix_out[l, j, :, k : k + 1] = total[:cols, lane : lane + 1]
+
+
+def closing(small, projections, consts, cols, collective_id):
     inner, ndp = lax.axis_size("tensor"), lax.axis_size("dp")
+    layers = len(projections)
+    rows, packed = projections[0].shape[1:]
+    wide = packed // 4
     pair = [pltpu.SemaphoreType.DMA((ndp * inner,))] * 2
+    shapes = [
+        (layers, cols), (layers, cols), (layers, cols, NEXP), (layers, NEXP, NEXP),
+        (layers, consts, cols), (layers, consts, cols, 2),
+        (layers, rows, 3, wide), (layers, wide, rows),
+    ]
     return pl.pallas_call(
-        functools.partial(closing_kernel, ndp, inner),
-        out_shape=[
-            jax.ShapeDtypeStruct(small.shape[1:], F32),
-            jax.ShapeDtypeStruct(first.shape[1:], F32),
-            jax.ShapeDtypeStruct(second.shape[1:], F32),
-        ],
-        in_specs=[VMEM_SPEC] * 3,
-        out_specs=[VMEM_SPEC] * 3,
-        scratch_shapes=[
-            pltpu.VMEM(small.shape, F32),
-            pltpu.VMEM(first.shape, BF16),
-            pltpu.VMEM(second.shape, BF16),
+        functools.partial(closing_kernel, ndp, inner, layers, consts, wide),
+        out_shape=[jax.ShapeDtypeStruct(shape, F32) for shape in shapes],
+        in_specs=[VMEM_SPEC] * (1 + layers),
+        out_specs=[VMEM_SPEC] * len(shapes),
+        scratch_shapes=[pltpu.VMEM(small.shape, F32)]
+        + [pltpu.VMEM(item.shape, BF16) for item in projections]
+        + [
+            pltpu.VMEM((-(-cols // LANES) * LANES, LANES), F32),
+            pltpu.VMEM((-(-rows // LANES) * LANES, -(-wide // LANES) * LANES), F32),
         ]
         + pair
-        + [pltpu.SemaphoreType.DMA((ndp,))] * 4,
+        + [pltpu.SemaphoreType.DMA((ndp,))] * (2 * layers),
         compiler_params=pltpu.CompilerParams(
             collective_id=collective_id, has_side_effects=True, vmem_limit_bytes=VMEM_LIMIT
         ),
         name="closing",
-    )(small, first, second)
+    )(small, *projections)
+
+
+def join_kernel(back, gain_row, nt, pieces, lag, *refs):
+    if back:
+        part, base_ref, skip_ref, rows_ref, result_ref, gg_ref = refs[:6]
+    else:
+        part, base_ref, rows_ref, total_ref, normed_ref = refs[:5]
+    refs = refs[6 if back else 5 :]
+    inbox, half, across, full, out_sem, in_sem, cross_out, cross_in, full_out, full_in = refs
+    me = lax.axis_index("tensor")
+    is_end = (me == 0) | (me == nt - 1)
+    buddy = jnp.where(me < 2, 1 - me, 5 - me)
+    cross = 3 - me
+
+    barrier = pltpu.get_barrier_semaphore()
+    pl.semaphore_signal(barrier, inc=1, device_id={"tensor": buddy}, device_id_type=MESH)
+
+    @pl.when(jnp.logical_not(is_end))
+    def _():
+        pl.semaphore_signal(barrier, inc=1, device_id={"tensor": cross}, device_id_type=MESH)
+
+    pl.semaphore_wait(barrier, 2 - is_end.astype(jnp.int32))
+
+    def copy(src, dst, send_sem, recv_sem, to):
+        return pltpu.make_async_remote_copy(
+            src_ref=src,
+            dst_ref=dst,
+            send_sem=send_sem,
+            recv_sem=recv_sem,
+            device_id={"tensor": to},
+            device_id_type=MESH,
+        )
+
+    def inward(n):
+        return copy(part.at[n], inbox.at[n], out_sem.at[n], in_sem.at[n], buddy)
+
+    def over(n):
+        return copy(half.at[n], across.at[n], cross_out.at[n], cross_in.at[n], cross)
+
+    def outward(n):
+        return copy(full.at[n], full.at[n], full_out.at[n], full_in.at[n], buddy)
+
+    gain = rows_ref[gain_row : gain_row + 1, :]
+    if back:
+        gg_ref[...] = jnp.zeros_like(gg_ref)
+
+    def settle(n):
+        total = full[n].astype(F32)
+        base = base_ref[n].astype(F32)
+        if back:
+            scale = lax.rsqrt(jnp.mean(base * base, axis=-1, keepdims=True) + EPS)
+            unit = base * scale
+            grad_unit = total * gain
+            below = scale * (grad_unit - unit * jnp.mean(grad_unit * unit, axis=-1, keepdims=True))
+            result_ref[n] = (below + skip_ref[n].astype(F32)).astype(BF16)
+
+            @pl.when(lax.div(n, pieces // nt) == me)
+            def _():
+                gg_ref[...] += jnp.sum(total * unit, axis=0, keepdims=True)
+        else:
+            total = total + base
+            total_ref[n] = total.astype(BF16)
+            normed_ref[n] = normed(total, gain).astype(BF16)
+
+    @pl.when(is_end)
+    def _():
+        for n in range(pieces):
+            inward(n).start()
+
+        def take(n, carry):
+            outward(n).wait_recv()
+            settle(n)
+            return carry
+
+        lax.fori_loop(0, pieces, take, 0)
+        for n in range(pieces):
+            inward(n).wait_send()
+
+    @pl.when(jnp.logical_not(is_end))
+    def _():
+        def step(at, carry):
+            @pl.when(at < pieces)
+            def _():
+                inward(at).wait_recv()
+                half[at] = (part[at].astype(F32) + inbox[at].astype(F32)).astype(BF16)
+                over(at).start()
+
+            @pl.when(at >= lag)
+            def _():
+                n = at - lag
+                over(n).wait_recv()
+                full[n] = (half[n].astype(F32) + across[n].astype(F32)).astype(BF16)
+                outward(n).start()
+                settle(n)
+
+            return carry
+
+        lax.fori_loop(0, pieces + lag, step, 0)
+        for n in range(pieces):
+            over(n).wait_send()
+            outward(n).wait_send()
+
+
+def join(back, part, others, rows, gain_row, collective_id, pieces=PIECES, lag=LAG):
+    nt = lax.axis_size("tensor")
+    seq_len, width = part.shape
+    cut = (pieces, seq_len // pieces, width)
+    outs = [jax.ShapeDtypeStruct(cut, BF16)]
+    outs.append(jax.ShapeDtypeStruct((1, width) if back else cut, F32 if back else BF16))
+    sems = pltpu.SemaphoreType.DMA((pieces,))
+    results = pl.pallas_call(
+        functools.partial(join_kernel, back, gain_row, nt, pieces, lag),
+        out_shape=outs,
+        in_specs=[VMEM_SPEC] * (2 + len(others)),
+        out_specs=[VMEM_SPEC] * 2,
+        scratch_shapes=[pltpu.VMEM(cut, BF16)] * 4 + [sems] * 6,
+        compiler_params=pltpu.CompilerParams(
+            collective_id=collective_id, has_side_effects=True, vmem_limit_bytes=VMEM_LIMIT
+        ),
+        cost_estimate=pl.CostEstimate(
+            flops=10 * seq_len * width, bytes_accessed=100 * seq_len * width, transcendentals=0
+        ),
+        name="join_back" if back else "join",
+    )(part.reshape(cut), *[item.reshape(cut) for item in others], rows)
+    return results[0].reshape(seq_len, width), (
+        results[1] if back else results[1].reshape(seq_len, width)
+    )
 
 
 def normed(values, gain):
@@ -153,7 +335,7 @@
         extra_ref, og_ref = refs.pop(0), refs.pop(0)
     else:
         extra_ref = refs.pop(0) if extra else None
-        base_ref, skip_ref, gain_ref = refs.pop(0), refs.pop(0), refs.pop(0)
+        base_ref, skip_ref, rows_ref = refs.pop(0), refs.pop(0), refs.pop(0)
     own_ref = refs.pop(0) if has_sum else None
     gg_ref = refs.pop(0) if kind in ("bwd", "end") else None
     all_ref = refs.pop(0) if has_gather else None
@@ -311,12 +493,12 @@
         else:
             if extra:
                 total = total + extra_ref[c]
-            base = base_ref[c]
+            base = base_ref[c].astype(F32)
             scale = lax.rsqrt(jnp.mean(base * base, axis=-1, keepdims=True) + EPS)
             unit = base * scale
-            grad_unit = total * gain_ref[...]
+            grad_unit = total * rows_ref[0:1, :]
             below = scale * (grad_unit - unit * jnp.mean(grad_unit * unit, axis=-1, keepdims=True))
-            result = below + skip_ref[c]
+            result = below + skip_ref[c].astype(F32)
             if has_gather:
                 all_ref[me, c] = result.astype(BF16)
             own_ref[c] = result
@@ -456,7 +638,7 @@
 def attend_kernel(heads, spans, block, raw, starts_ref, a_ref, w_ref, *refs):
     if raw:
         gain_ref, qkv_ref, o_ref, lse_ref, out_ref, normed_ref = refs
-        normed_ref[...] = normed(a_ref[...].astype(F32), gain_ref[...]).astype(BF16)
+        normed_ref[...] = normed(a_ref[...].astype(F32), gain_ref[0:1, :]).astype(BF16)
         a_ref = normed_ref
     else:
         qkv_ref, o_ref, lse_ref, out_ref = refs
@@ -579,9 +761,23 @@
     return high, (values - high.astype(F32)).astype(BF16)
 
 
+def const_parts(product, wd, layer, at, consts):
+    first = EXPERTS + 2
+    zero = shift(product, first - at["cmix"] - layer * 2 * consts)
+    one = shift(product, first - at["cmix"] - layer * 2 * consts - consts)
+    lane = lax.broadcasted_iota(jnp.int32, product.shape, 1)
+    here = (lane >= first) & (lane < first + consts)
+    gap = jnp.where(here, one - zero, 0.0)
+    alpha0 = 1.0 / (1.0 + jnp.exp(gap))
+    alpha1 = 1.0 / (1.0 + jnp.exp(-gap))
+    gate = jnp.where(here, wd, 0.0)
+    keep = jnp.sum(gate * alpha0 + jnp.where(lane == EXPERTS + 1, wd, 0.0), axis=1, keepdims=True)
+    return lane, here, alpha0, alpha1, gate, keep
+
+
 def experts_kernel(
-    cap, b_ref, w_ref, rowpos_ref, pos_ref, router_ref, zterm_ref,
-    x_ref, gu_ref, z_ref, wd_ref, f_ref, pick_scr, y_scr,
+    cap, layer, at, consts, b_ref, w_ref, rowpos_ref, pos_ref, small_ref, rows_ref, mix_ref, zprev_ref,
+    mid_ref, x_ref, gu_ref, z_ref, wd_ref, f_ref, extra_ref, pick_scr, y_scr,
 ):
     e = pl.program_id(0)
     seq_len, width = b_ref.shape
@@ -589,12 +785,26 @@
 
     @pl.when(e == 0)
     def _():
-        z = dot(b_ref[...], router_ref[...]) + zterm_ref[...]
+        product = dot(b_ref[...], small_ref[...])
+        lane = lax.broadcasted_iota(jnp.int32, product.shape, 1)
+        p_high, p_low = two_parts(zprev_ref[...])
+        z = (
+            jnp.where(lane < NEXP, shift(product, -at["router"] - layer * NEXP), 0.0)
+            + dot(p_high, mix_ref[...])
+            + dot(p_low, mix_ref[...])
+        )
         z_ref[...] = z
         hit = pos_ref[...] >= 0
         top = jnp.max(jnp.where(hit, z, -3e38), axis=1, keepdims=True)
         ez = jnp.where(hit, jnp.exp(jnp.where(hit, z - top, 0.0)), 0.0)
-        wd_ref[...] = ez / jnp.sum(ez, axis=1, keepdims=True)
+        wd = ez / jnp.sum(ez, axis=1, keepdims=True)
+        wd_ref[...] = wd
+        _, _, _, alpha1, gate, keep = const_parts(product, wd, layer, at, consts)
+        extra = mid_ref[...].astype(F32) + keep * b_ref[...].astype(F32)
+        for j in range(consts):
+            row = at["cvec"] + layer * consts + j
+            extra = extra + lane_column(gate * alpha1, EXPERTS + 2 + j) * rows_ref[row : row + 1, :]
+        extra_ref[...] = extra.astype(BF16)
 
     w = w_ref[...].reshape(width, 3 * half)
     take = (
@@ -624,18 +834,21 @@
     return pl.BlockSpec(shape, lambda e: (0,) * len(shape))
 
 
-def experts_forward(b_all, w_exp, rowpos, pos, router, zterm, cap):
+def experts_forward(
+    layer, at, consts, b_all, w_exp, rowpos, pos, small, rows_t, mix, z_prev, mid, cap
+):
     seq_len, width = b_all.shape
     shards_dp, count, rows, wide3 = w_exp.shape
     half = wide3 // 3
     return pl.pallas_call(
-        functools.partial(experts_kernel, cap),
+        functools.partial(experts_kernel, cap, layer, at, consts),
         grid=(count,),
         out_shape=[
             jax.ShapeDtypeStruct((count, cap, width), BF16),
             jax.ShapeDtypeStruct((count, cap, 2 * half), BF16),
             jax.ShapeDtypeStruct((seq_len, LANES), F32),
             jax.ShapeDtypeStruct((seq_len, LANES), F32),
+            jax.ShapeDtypeStruct((seq_len, width), BF16),
             jax.ShapeDtypeStruct((seq_len, width), BF16),
         ],
         in_specs=[
@@ -644,13 +857,17 @@
             pl.BlockSpec((1, 1, seq_len), lambda e: (e, 0, 0)),
             whole((seq_len, LANES)),
             whole((width, LANES)),
+            whole(rows_t.shape),
+            whole((LANES, LANES)),
             whole((seq_len, LANES)),
+            whole((seq_len, width)),
         ],
         out_specs=[
             pl.BlockSpec((1, cap, width), lambda e: (e, 0, 0)),
             pl.BlockSpec((1, cap, 2 * half), lambda e: (e, 0, 0)),
             whole((seq_len, LANES)),
             whole((seq_len, LANES)),
+            whole((seq_len, width)),
             whole((seq_len, width)),
         ],
         scratch_shapes=[
@@ -664,12 +881,13 @@
             transcendentals=0,
         ),
         name="experts_forward",
-    )(b_all, w_exp, rowpos, pos, router, zterm)
+    )(b_all, w_exp, rowpos, pos, small, rows_t, mix, z_prev, mid)
 
 
 def experts_back_kernel(
-    cap, g_ref, w_ref, x_ref, gu_ref, rowpos_ref, pos_ref, wd_ref, gwown_ref, gprev_ref, rt_ref,
-    gw_ref, gz_ref, gb_ref, pick_scr, gx_scr, gg_scr,
+    cap, layer, at, consts, own, offset_ref, g_ref, w_ref, x_ref, gu_ref, rowpos_ref, pos_ref, wd_ref,
+    b_ref, small_ref, rows_ref, mix_ref, zprev_ref, gprev_ref, sums_ref, mixes_ref,
+    gw_ref, below_ref, gb_ref, sums_out, mixes_out, pick_scr, gx_scr, gg_scr, gb_scr, zs_scr,
 ):
     e = pl.program_id(0)
     seq_len, width = g_ref.shape
@@ -710,30 +928,80 @@
 
     @pl.when(e == pl.num_programs(0) - 1)
     def _():
+        mine = pl.ds(pl.multiple_of(offset_ref[0], own), own)
+        b_own, g_own = b_ref[mine, :], g_ref[mine, :].astype(F32)
+        wd_own = wd_ref[mine, :]
+        lane, here_own, alpha0, alpha1, gate, keep = const_parts(
+            dot(b_own, small_ref[...]), wd_own, layer, at, consts
+        )
+        b_dot = jnp.sum(b_own.astype(F32) * g_own, axis=1, keepdims=True)
+        c_dot = jnp.zeros_like(wd_own)
+        for j in range(consts):
+            row = at["cvec"] + layer * consts + j
+            one = jnp.sum(g_own * rows_ref[row : row + 1, :], axis=1, keepdims=True)
+            c_dot = jnp.where(lane == EXPERTS + 2 + j, one, c_dot)
+        gw_own = jnp.where(here_own, alpha0 * b_dot + alpha1 * c_dot, 0.0)
+        gw_own = jnp.where(lane == EXPERTS + 1, b_dot, gw_own)
+        inner = gate * (alpha0 * b_dot + alpha1 * c_dot)
+        gt0 = alpha0 * (gate * b_dot - inner)
+        gt1 = alpha1 * (gate * c_dot - inner)
+
         slots = dot(pick_scr[...], gg_scr[...])
-        gw = slots[:, :LANES] + slots[:, LANES:] + gwown_ref[...]
+        zs_scr[...] = slots[:, :LANES] + slots[:, LANES:]
+        zs_scr[mine, :] += gw_own
+        gw = zs_scr[...]
         wd = wd_ref[...]
         gz = wd * (gw - jnp.sum(wd * gw, axis=1, keepdims=True)) + gprev_ref[...]
-        gz_ref[...] = gz
         z_high, z_low = two_parts(gz)
-        gb = dot(pick_scr[...], gx_scr[...]) + dot(z_high, rt_ref[...]) + dot(z_low, rt_ref[...])
-        gb_ref[...] = gb.astype(BF16)
-
-
-def experts_backward(g_all, w_exp, x, gu, rowpos, pos, wd, gw_own, grad_prev, router_t, cap):
+        below_ref[...] = dot_nt(z_high, mix_ref[...]) + dot_nt(z_low, mix_ref[...])
+        p_high, p_low = two_parts(zprev_ref[...])
+        mixes_out[...] = mixes_ref[...] + shift(
+            dot_tn(p_high, z_high) + dot_tn(p_high, z_low) + dot_tn(p_low, z_high), layer * MIX_STEP
+        )
+        zs_scr[...] = shift(gz, at["router"] + layer * NEXP)
+        up = at["cmix"] + layer * 2 * consts - EXPERTS - 2
+        zs_scr[mine, :] += shift(gt0, up) + shift(gt1, up + consts)
+        z_high, z_low = two_parts(zs_scr[...])
+        gb_scr[...] = (
+            dot(pick_scr[...], gx_scr[...])
+            + dot_nt(z_high, small_ref[...])
+            + dot_nt(z_low, small_ref[...])
+        )
+        gb_scr[mine, :] += keep * g_own
+        gb_ref[...] = gb_scr[...].astype(BF16)
+        i_high, i_low = two_parts(
+            shift(gate * alpha1, at["cvec"] + layer * consts - EXPERTS - 2)
+        )
+        g_low = g_ref[mine, :]
+        sums_out[...] = (
+            sums_ref[...]
+            + dot_tn(b_ref[...], z_high)
+            + dot_tn(b_ref[...], z_low)
+            + dot_tn(g_low, i_high)
+            + dot_tn(g_low, i_low)
+        )
+
+
+def experts_backward(
+    layer, at, consts, own, offset, g_all, w_exp, x, gu, rowpos, pos, wd, b_all, small, rows_t, mix,
+    z_prev, grad_prev, sums, mixes, cap,
+):
     seq_len, width = g_all.shape
     shards_dp, count, rows, wide3 = w_exp.shape
     half = wide3 // 3
     weight_spec = pl.BlockSpec((shards_dp, 1, rows, wide3), lambda e: (0, e, 0, 0))
     return pl.pallas_call(
-        functools.partial(experts_back_kernel, cap),
+        functools.partial(experts_back_kernel, cap, layer, at, consts, own),
         grid=(count,),
         out_shape=[
             jax.ShapeDtypeStruct(w_exp.shape, BF16),
             jax.ShapeDtypeStruct((seq_len, LANES), F32),
             jax.ShapeDtypeStruct((seq_len, width), BF16),
+            jax.ShapeDtypeStruct((width, LANES), F32),
+            jax.ShapeDtypeStruct((LANES, LANES), F32),
         ],
         in_specs=[
+            pl.BlockSpec(memory_space=pltpu.SMEM),
             whole((seq_len, width)),
             weight_spec,
             pl.BlockSpec((1, cap, width), lambda e: (e, 0, 0)),
@@ -741,15 +1009,28 @@
             pl.BlockSpec((1, 1, seq_len), lambda e: (e, 0, 0)),
             whole((seq_len, LANES)),
             whole((seq_len, LANES)),
+            whole((seq_len, width)),
+            whole((width, LANES)),
+            whole(rows_t.shape),
+            whole((LANES, LANES)),
             whole((seq_len, LANES)),
             whole((seq_len, LANES)),
-            whole((LANES, width)),
+            whole((width, LANES)),
+            whole((LANES, LANES)),
         ],
-        out_specs=[weight_spec, whole((seq_len, LANES)), whole((seq_len, width))],
+        out_specs=[
+            weight_spec,
+            whole((seq_len, LANES)),
+            whole((seq_len, width)),
+            whole((width, LANES)),
+            whole((LANES, LANES)),
+        ],
         scratch_shapes=[
             pltpu.VMEM((seq_len, count * cap), BF16),
             pltpu.VMEM((count * cap, width), BF16),
             pltpu.VMEM((count * cap, 2 * LANES), BF16),
+            pltpu.VMEM((seq_len, width), F32),
+            pltpu.VMEM((seq_len, LANES), F32),
         ],
         compiler_params=pltpu.CompilerParams(vmem_limit_bytes=VMEM_LIMIT),
         cost_estimate=pl.CostEstimate(
@@ -758,7 +1039,44 @@
             transcendentals=0,
         ),
         name="experts_backward",
-    )(g_all, w_exp, x, gu, rowpos, pos, wd, gw_own, grad_prev, router_t)
+    )(
+        offset, g_all, w_exp, x, gu, rowpos, pos, wd, b_all, small, rows_t, mix, z_prev, grad_prev,
+        sums, mixes,
+    )
+
+
+def unpack_kernel(half, *refs):
+    *in_refs, up_ref, down_ref, tall = refs
+    rows = up_ref.shape[2]
+    tall[...] = jnp.zeros_like(tall)
+    for l, ref in enumerate(in_refs):
+        values = ref[0].astype(F32)
+        for part in range(2):
+            up_ref[l, 0, :, part, :] = values[:, part * half : (part + 1) * half]
+        tall[:rows, :] = values[:, 2 * half :]
+        down_ref[l, 0] = tall[...].T[:, :rows]
+
+
+def unpack(items):
+    count, rows, wide3 = items[0].shape
+    half = wide3 // 3
+    layers = len(items)
+    return pl.pallas_call(
+        functools.partial(unpack_kernel, half),
+        grid=(count,),
+        out_shape=[
+            jax.ShapeDtypeStruct((layers, count, rows, 2, half), F32),
+            jax.ShapeDtypeStruct((layers, count, half, rows), F32),
+        ],
+        in_specs=[pl.BlockSpec((1, rows, wide3), lambda e: (e, 0, 0))] * layers,
+        out_specs=[
+            pl.BlockSpec((layers, 1, rows, 2, half), lambda e: (0, e, 0, 0, 0)),
+            pl.BlockSpec((layers, 1, half, rows), lambda e: (0, e, 0, 0)),
+        ],
+        scratch_shapes=[pltpu.VMEM((-(-rows // LANES) * LANES, half), F32)],
+        compiler_params=pltpu.CompilerParams(vmem_limit_bytes=VMEM_LIMIT),
+        name="unpack",
+    )(*items)
 
 
 def lanes(values):
@@ -806,31 +1124,17 @@
     cols = attn_norm.shape[1]
     consts = const_vec.shape[1]
 
+    at = layout(layers, consts)
     packed = jnp.concatenate(
         [attn_norm.T, moe_norm.T]
         + [router[l] for l in range(layers)]
         + [const_vec.reshape(-1, cols).T]
-        + [const_mix[l, j] for l in range(layers) for j in range(consts)],
+        + [const_mix[l, :, :, k].T for l in range(layers) for k in range(2)],
         axis=1,
     )
-    hidden = hidden_in.astype(F32)
     x_all, small = line_exchange("start", [hidden_in, lanes(packed)], own, width, 0)
     small = small.reshape(width, LANES)
-    at = 0
-    fields = {}
-    for name, size in (
-        ("attn", layers),
-        ("moe", layers),
-        ("router", layers * NEXP),
-        ("cvec", layers * consts),
-        ("cmix", layers * consts * 2),
-    ):
-        fields[name] = (at, size)
-        at += size
-
-    def field(name, l, per):
-        begin = fields[name][0] + l * per
-        return small[:, begin : begin + per]
+    rows_t = small[:, :48].T.astype(F32)
 
     attn_w, exp_w = [], []
     for l in range(layers):
@@ -850,168 +1154,99 @@
     pos = [slot_table(routes[l]) for l in range(layers)]
     rowpos = [p[:, :EXPERTS].T[:, None, :] for p in pos]
 
-    a_all = None
     z_prev = lanes(prev_logits)
-    next_id = 2
+    hidden, a_all = x_all, None
+    grad_all = out_grad
+    next_id = 1
     stored = []
     for l in range(layers):
-        mix = jnp.pad(gate_mix[l].astype(F32), ((0, LANES - NEXP), (0, LANES - NEXP)))
-        zterm = jnp.dot(z_prev, mix, precision=HIGH)
+        mix = jnp.pad(gate_mix[l], ((0, LANES - NEXP), (0, LANES - NEXP)))
         if l == 0:
-            gain = field("attn", 0, 1).astype(F32).T
             qkv, o, lse, partial, a_all = attend_forward(
-                span_starts, x_all, attn_w[l], heads, gain
+                span_starts, x_all, attn_w[l], heads, rows_t
             )
         else:
             qkv, o, lse, partial = attend_forward(span_starts, a_all, attn_w[l], heads)
-        gain = field("moe", l, 1).astype(F32).T
-        mid, b_all = line_exchange("fwd", [partial, hidden, gain], own, width, next_id)
-        router_l = lanes(field("router", l, NEXP))
-        x, gu, z, wd, partial = experts_forward(
-            b_all, exp_w[l], rowpos[l], pos[l], router_l, zterm, cap
-        )
-        b_own = lax.dynamic_slice_in_dim(b_all, offset, own, 0)
-        cmix = field("cmix", l, 2 * consts)
-        cvec = field("cvec", l, consts).astype(F32).T
-        logit = dot(b_own, cmix)
-        alpha = jax.nn.softmax(logit.reshape(own, consts, 2), axis=2)
-        gates = lax.dynamic_slice_in_dim(wd, offset, own, 0)
-        copy_gate = gates[:, EXPERTS + 1 : EXPERTS + 2]
-        const_gate = gates[:, EXPERTS + 2 : EXPERTS + 2 + consts]
-        keep = copy_gate + jnp.sum(const_gate * alpha[:, :, 0], axis=1, keepdims=True)
-        inject = const_gate * alpha[:, :, 1]
-        side = keep * b_own.astype(F32)
-        for j in range(consts):
-            side = side + inject[:, j : j + 1] * cvec[j : j + 1]
+        if l == layers - 1:
+            partial, grad_all = lax.optimization_barrier((partial, grad_all))
+            grad_all = lax.all_gather(grad_all, "tensor", axis=0, tiled=True)
+        mid, b_all = join(False, partial, [hidden], rows_t, at["moe"] + l, next_id)
+        x, gu, z, wd, partial, extra = experts_forward(
+            l, at, consts, b_all, exp_w[l], rowpos[l], pos[l], small, rows_t, mix, z_prev, mid, cap
+        )
         stored.append(
             dict(
-                hidden=hidden, a_all=a_all, qkv=qkv, o=o, lse=lse, mid=mid, b_all=b_all,
-                b_own=b_own, x=x, gu=gu, wd=wd, z_prev=z_prev, alpha=alpha,
-                const_gate=const_gate, keep=keep, inject=inject, cvec=cvec, cmix=cmix, mix=mix,
-                router=router_l,
+                hidden=hidden, a_all=a_all, qkv=qkv, o=o, lse=lse, mid=mid, b_all=b_all, x=x, gu=gu,
+                wd=wd, z_prev=z_prev, mix=mix,
             )
         )
         if l + 1 < layers:
-            gain = field("attn", l + 1, 1).astype(F32).T
-            hidden, a_all = line_exchange("fwd", [partial, mid + side, gain], own, width, next_id + 1)
+            hidden, a_all = join(False, partial, [extra], rows_t, at["attn"] + l + 1, next_id + 1)
         else:
-            hidden, g_all = line_exchange(
-                "last", [partial, mid + side, out_grad], own, width, next_id + 1
-            )
+            hidden_out = lax.psum_scatter(partial, "tensor", scatter_dimension=0, tiled=True)
+            extra = lax.dynamic_slice_in_dim(extra, offset, own, 0)
         z_prev = z
         next_id += 2
-    hidden_out = hidden
-
-    grad = out_grad.astype(F32)
-    grad_prev = jnp.zeros((seq_len, LANES), F32)
+
+    below = jnp.zeros((seq_len, LANES), F32)
+    sums = jnp.zeros((width, LANES), F32)
+    mixes = jnp.zeros((LANES, LANES), F32)
     attn_grads, exp_grads = [None] * layers, [None] * layers
     gains_a, gains_m = [None] * layers, [None] * layers
-    routers, cvecs, cmixes, mixes = ([None] * layers for _ in range(4))
     for l in reversed(range(layers)):
         s = stored[l]
-        b_own = s["b_own"].astype(F32)
-        bg = jnp.sum(b_own * grad, axis=1, keepdims=True)
-        cg = jnp.concatenate(
-            [jnp.sum(grad * s["cvec"][j : j + 1], axis=1, keepdims=True) for j in range(consts)],
-            axis=1,
-        )
-        alpha = s["alpha"]
-        gw_const = alpha[:, :, 0] * bg + alpha[:, :, 1] * cg
-        gw_own = jnp.pad(
-            jnp.concatenate([bg, gw_const], axis=1),
-            ((0, 0), (EXPERTS + 1, LANES - EXPERTS - 2 - consts)),
-        )
-        gw_own = lax.dynamic_update_slice_in_dim(
-            jnp.zeros((seq_len, LANES), F32), gw_own, offset, 0
-        )
-        ga = s["const_gate"][:, :, None] * jnp.stack([jnp.broadcast_to(bg, cg.shape), cg], axis=2)
-        gt = alpha * (ga - jnp.sum(alpha * ga, axis=2, keepdims=True))
-        gt = gt.reshape(own, 2 * consts)
-        own_part = s["keep"] * grad
-        cmix_f = s["cmix"].astype(F32).T
-        for j in range(2 * consts):
-            own_part = own_part + gt[:, j : j + 1] * cmix_f[j : j + 1]
-        cmixes[l] = lax.dot_general(b_own, gt, (((0,), (0,)), ((), ())), precision=HIGH)
-        cvecs[l] = lax.dot_general(grad, s["inject"], (((0,), (0,)), ((), ())), precision=HIGH)
-
-        gw_exp, gz, partial = experts_backward(
-            g_all, exp_w[l], s["x"], s["gu"], rowpos[l], pos[l], s["wd"], gw_own, grad_prev,
-            s["router"].T, cap,
+        gw_exp, below, partial, sums, mixes = experts_backward(
+            l, at, consts, own, offset.reshape(1), grad_all, exp_w[l], s["x"], s["gu"], rowpos[l],
+            pos[l], s["wd"], s["b_all"], small, rows_t, s["mix"], s["z_prev"], below, sums, mixes, cap,
         )
         exp_grads[l] = lax.psum_scatter(gw_exp, "dp", scatter_dimension=0, tiled=False)
         if l + 1 < layers:
             partial, exp_grads[l + 1] = lax.optimization_barrier((partial, exp_grads[l + 1]))
-        z_high, z_low = two_parts(gz)
-        routers[l] = (dot_tn(s["b_all"], z_high) + dot_tn(s["b_all"], z_low))[:, :NEXP]
-        mixes[l] = lax.dot_general(
-            s["z_prev"], gz, (((0,), (0,)), ((), ())), precision=HIGH
-        )[:NEXP, :NEXP]
+        else:
+            partial, hidden_out = lax.optimization_barrier((partial, hidden_out))
+        grad_mid, gains_m[l] = join(
+            True, partial, [s["mid"], grad_all], rows_t, at["moe"] + l, next_id
+        )
+        partial, gw_attn = attend_backward(
+            span_starts, grad_mid, attn_w[l], s["a_all"], s["qkv"], s["o"], s["lse"], heads
+        )
+        attn_grads[l] = gw_attn.reshape(ndp, rows, 4 * wide)
         if l > 0:
-            grad_prev = lax.dot_general(gz, s["mix"], (((1,), (1,)), ((), ())), precision=HIGH)
-        gain = field("moe", l, 1).astype(F32).T
-        grad_mid, gains_m[l], g_all = line_exchange(
-            "bwd", [partial, own_part, s["mid"], grad, gain], own, width, next_id, extra=True
-        )
-        partial, gw_attn = attend_backward(
-            span_starts, g_all, attn_w[l], s["a_all"], s["qkv"], s["o"], s["lse"], heads
-        )
-        attn_grads[l] = gw_attn.reshape(ndp, rows, 4 * wide)
-        gain = field("attn", l, 1).astype(F32).T
-        if l > 0:
-            grad, gains_a[l], g_all = line_exchange(
-                "bwd", [partial, s["hidden"], grad_mid, gain], own, width, next_id + 1
+            grad_all, gains_a[l] = join(
+                True, partial, [s["hidden"], grad_mid], rows_t, at["attn"] + l, next_id + 1
             )
         else:
+            skip = lax.dynamic_slice_in_dim(grad_mid, offset, own, 0)
             grad, gains_a[l] = line_exchange(
-                "end", [partial, s["hidden"], grad_mid, gain], own, width, next_id + 1
+                "end", [partial, hidden_in, skip, rows_t], own, width, next_id + 1
             )
         next_id += 2
-
+    hidden_out = hidden_out.astype(F32) + extra.astype(F32)
+
+    gains = jnp.concatenate(gains_a + gains_m, axis=0)
+    sums = sums + jnp.pad(gains, ((0, LANES - 2 * layers), (0, 0))).T
     sums = jnp.concatenate(
-        [item.T for item in gains_a]
-        + [item.T for item in gains_m]
-        + routers
-        + cvecs
-        + cmixes,
+        [
+            sums.reshape(ndp * nt, cols, LANES),
+            jnp.broadcast_to(mixes[None, :MIX_STEP], (ndp * nt, MIX_STEP, LANES)),
+        ],
         axis=1,
     )
-    sums = lanes(sums).reshape(ndp * nt, cols, LANES)
-    flat = jnp.stack(mixes).reshape(-1)
-    mix_rows = -(-flat.shape[0] // LANES)
-    flat = jnp.pad(flat, (0, mix_rows * LANES - flat.shape[0])).reshape(1, mix_rows, LANES)
-    flat = jnp.broadcast_to(flat, (ndp * nt, mix_rows, LANES))
-    total, *attn_grads = closing(jnp.concatenate([sums, flat], axis=1), *attn_grads, next_id)
-    mix_total = total[cols:].reshape(-1)[: layers * NEXP * NEXP].reshape(layers, NEXP, NEXP)
-    total = total[:cols]
-
-    def back(name):
-        begin, size = fields[name]
-        return total[:, begin : begin + size]
-
-    router_grad = jnp.swapaxes(back("router").reshape(cols, layers, NEXP), 0, 1)
-    cmix_grad = jnp.transpose(back("cmix").reshape(cols, layers, consts, 2), (1, 2, 0, 3))
-    cvec_grad = back("cvec").T.reshape(layers, consts, cols)
-    qkv_grad = jnp.stack(
-        [item[:, : 3 * wide].reshape(rows, 3, wide) for item in attn_grads]
+    attn_g, moe_g, router_g, mix_g, cvec_g, cmix_g, qkv_g, outw_g = closing(
+        sums, attn_grads, consts, cols, next_id
     )
-    outw_grad = jnp.stack([item[:, 3 * wide :].T for item in attn_grads])
-    up_grad = jnp.stack(
-        [item[:, :, : 2 * half].reshape(EXPERTS, rows, 2, half) for item in exp_grads]
-    ).astype(F32)
-    down_grad = jnp.stack(
-        [jnp.swapaxes(item[:, :, 2 * half :], 1, 2) for item in exp_grads]
-    ).astype(F32)
+    up_grad, down_grad = unpack(exp_grads)
     return (
         hidden_out,
         grad,
-        back("attn").T,
-        qkv_grad,
-        outw_grad,
-        back("moe").T,
-        router_grad,
-        mix_total,
-        cvec_grad,
-        cmix_grad,
+        attn_g,
+        qkv_g,
+        outw_g,
+        moe_g,
+        router_g,
+        mix_g,
+        cvec_g,
+        cmix_g,
         up_grad,
         down_grad,
     )

time: 830 us -> 689 us (0.83)
  local copies, waits for them, and re-layouts: 94.4 us -> 41.7 us
  other arithmetic: 51.2 us -> 10.7 us
  Pallas kernels: 642 us -> 614 us
  matrix products: 18.5 us -> 1.44 us
    pallas_call x9 -> x2, Pallas kernels: 419 us -> 73.6 us  [line_exchange(): pl.pallas_call(functools.partial(line_kernel, kind, nt, chunks, lag, extr...]
    pallas_call x5 -> x12, Pallas kernels: 158 us -> 475 us  [the longest x6 284 us: join(): pl.pallas_call(functools.partial(join_kernel, back, gain_row, nt, pieces,...]
    slice x19 -> x3, local copies, waits for them, and re-layouts: 18.9 us -> 0.72 us  [the longest x1 0.7 us: shards(): mixes[None, :MIX_STEP]]
    dot_general x13 -> x0, matrix products: 14.4 us -> none  [the longest x2 3.91 us: shards(): lax.dot_general(s['z_prev'], gz, (((0,), (0,)), ((), ())), precision=HIGH)]
    another operation x12 -> x0, local copies, waits for them, and re-layouts: 13.1 us -> none  [the longest x2 4.7 us: shards(): jnp.stack([item[:, :, :2 * half].reshape(EXPERTS, rows, 2, half) for item...]
    reduce_sum x9 -> x0, other arithmetic: 9.75 us -> none  [the longest x2 3.69 us: shards(): jnp.sum(const_gate * alpha[:, :, 0], axis=1, keepdims=True)]
    convert_element_type x2 -> x1, other arithmetic: 10.1 us -> 0.67 us  [shards(): rows_t = small[:, :48].T.astype(F32)]
    unnamed x147 -> x60, local copies, waits for them, and re-layouts: 16.7 us -> 17.8 us
  transfers between devices with their start and end apart: 6 -> 8, of which waited for: 0 -> 0; matrix products, arithmetic and copies ran while one was open for 11% -> 6% of each run, Pallas kernels for 66% -> 88%
where the time goes in v3:
time: 689 us; the launch traced here: 684 us
  Pallas kernels  614 us (89%)
  local copies, waits for them, and re-layouts  41.7 us (6%)
  between operations  14.8 us (2%)
  other arithmetic  10.7 us (2%)
    pallas_call x6, Pallas kernels, join(): pl.pallas_call(functools.partial(join_kernel, back, gain_row, nt, pieces,...  284 us
    pallas_call x2, Pallas kernels, line_exchange(): pl.pallas_call(functools.partial(line_kernel, kind, nt, chunks, lag, extr...  73.6 us
    pallas_call x2, Pallas kernels, experts_backward(): pl.pallas_call(functools.partial(experts_back_kernel, cap, layer, at, con...  73.5 us
    pallas_call x1, Pallas kernels, closing(): pl.pallas_call(functools.partial(closing_kernel, ndp, inner, layers, cons...  57 us
    pallas_call x2, Pallas kernels, experts_forward(): pl.pallas_call(functools.partial(experts_kernel, cap, layer, at, consts),...  51.9 us
    pallas_call x2, Pallas kernels, attend_backward(): pl.pallas_call(functools.partial(attend_back_kernel, heads, spans, PIC),...  39.9 us
    pallas_call x2, Pallas kernels, attend_forward(): pl.pallas_call(functools.partial(attend_kernel, heads, spans, PIC, raw),...  25.6 us
    unnamed x60, local copies, waits for them, and re-layouts  17.8 us
  transfers between devices with their start and end apart: 8, of which 0 were waited for; matrix products, arithmetic and copies ran while one was open for 6% of the time, Pallas kernels for 88%

profile of v3, /device:TPU:0, one launch (start us, length us, event | category | flops | bytes accessed | tf_op | source)
XLA Modules:
  0.0 684.1 jit_solution(15389634186642956806)
XLA Ops:
  10.3 5.0 fusion.10
  15.3 2.8 reshape_squeeze.13
  18.1 2.4 slice_bitcast_fusion
  24.6 2.7 pad_maximum_fusion.1
  29.6 43.0 %line_start.1 = (bf16[4,2,128,768]{3,2,1,0:T(8,128)(2,1)}, bf16[32,24,128]{2,1,0:T(8,128)(2,1)}) custom-call(bf16[2,128,768]{2,1,0:T(8,128)(2,1)} %bitcast.101, bf16[24,128]{1,0:T(8,128)(2,1)} %pad.19.refs_1_), custom_call_target="tpu_custom_call" | custom-call | flops 7864320 | bytes 78643200 | tf_op jit(solution)/shard_map/line_start/pallas_call | solution.py:598
  78.0 13.2 %attend_forward.2 = (bf16[1024,576]{1,0:T(8,128)(2,1)}, bf16[1024,192]{1,0:T(8,128)(2,1)}, f32[1024,3]{1,0:T(8,128)}, bf16[1024,768]{1,0:T(8,128)(2,1)}, bf16[1024,768]{1,0:T(8,128)(2,1)}) custom-call(s32[1,2]{1,0:T(1,128)} %starts_ref.7, bf16[1024,768]{1,0:T(8,128)(2,1)} %bitcast.94, bf16[768,768]{1,0:T(8,128)(2,1)} %all-gather.12.cloned.1.call-done.w_ref, ...), custom_call_target="tpu_custom_call" | custom-call | flops 2013265920 | bytes 4718592 | tf_op jit(solution)/shard_map/attend_forward/pallas_call | solution.py:671
  91.2 48.4 %join.3 = (bf16[16,64,768]{2,1,0:T(8,128)(2,1)}, bf16[16,64,768]{2,1,0:T(8,128)(2,1)}) custom-call(bf16[16,64,768]{2,1,0:T(8,128)(2,1)} %bitcast.98, bf16[16,64,768]{2,1,0:T(8,128)(2,1)} %bitcast.95, f32[48,768]{1,0:T(8,128)} %convert_bitcast_fusion.refs_0_.refs_2_.rows_ref.refs_3_), custom_call_target="tpu_custom_call" | custom-call | flops 7864320 | bytes 78643200 | tf_op jit(solution)/shard_map/join/pallas_call | solution.py:302
  139.6 26.1 %experts_forward.2 = (bf16[8,256,768]{2,1,0:T(8,128)(2,1)}, bf16[8,256,1024]{2,1,0:T(8,128)(2,1)}, f32[1024,128]{1,0:T(8,128)}, f32[1024,128]{1,0:T(8,128)}, bf1...) custom-call(bf16[1024,768]{1,0:T(8,128)(2,1)} %bitcast.143, bf16[8,8,96,1536]{3,2,1,0:T(8,128)(2,1)} %bitcast.139, ...), custom_call_target="tpu_custom_call" | custom-call | flops 11274289152 | bytes 18874368 | tf_op jit(solution)/shard_map/experts_forward/pallas_call | solution.py:843
  165.7 49.4 %join.4 = (bf16[16,64,768]{2,1,0:T(8,128)(2,1)}, bf16[16,64,768]{2,1,0:T(8,128)(2,1)}) custom-call(bf16[16,64,768]{2,1,0:T(8,128)(2,1)} %bitcast.99, bf16[16,64,768]{2,1,0:T(8,128)(2,1)} %bitcast.100, f32[48,768]{1,0:T(8,128)} %convert_bitcast_fusion.refs_0_.refs_2_.rows_ref.refs_3_), custom_call_target="tpu_custom_call" | custom-call | flops 7864320 | bytes 78643200 | tf_op jit(solution)/shard_map/join/pallas_call | solution.py:302
  215.1 12.4 %attend_forward.3 = (bf16[1024,576]{1,0:T(8,128)(2,1)}, bf16[1024,192]{1,0:T(8,128)(2,1)}, f32[1024,3]{1,0:T(8,128)}, bf16[1024,768]{1,0:T(8,128)(2,1)}) custom-call(s32[1,2]{1,0:T(1,128)} %starts_ref.7, bf16[1024,768]{1,0:T(8,128)(2,1)} %bitcast.145, bf16[768,768]{1,0:T(8,128)(2,1)} %all-gather.16.cloned.1.call-done.w_ref), custom_call_target="tpu_custom_call" | custom-call | flops 2013265920 | bytes 4718592 | tf_op jit(solution)/shard_map/attend_forward/pallas_call | solution.py:671
  230.1 47.9 %join.5 = (bf16[16,64,768]{2,1,0:T(8,128)(2,1)}, bf16[16,64,768]{2,1,0:T(8,128)(2,1)}) custom-call(bf16[16,64,768]{2,1,0:T(8,128)(2,1)} %bitcast.96, bf16[16,64,768]{2,1,0:T(8,128)(2,1)} %get-tuple-element.88.refs_1_, f32[48,768]{1,0:T(8,128)} %convert_bitcast_fusion.refs_0_.refs_2_.rows_ref.refs_3_), custom_call_target="tpu_custom_call" | custom-call | flops 7864320 | bytes 78643200 | tf_op jit(solution)/shard_map/join/pallas_call | solution.py:302
  278.1 25.8 %experts_forward.3 = (bf16[8,256,768]{2,1,0:T(8,128)(2,1)}, bf16[8,256,1024]{2,1,0:T(8,128)(2,1)}, f32[1024,128]{1,0:T(8,128)}, f32[1024,128]{1,0:T(8,128)}, bf1...) custom-call(bf16[1024,768]{1,0:T(8,128)(2,1)} %bitcast.147, bf16[8,8,96,1536]{3,2,1,0:T(8,128)(2,1)} %bitcast.141, ...), custom_call_target="tpu_custom_call" | custom-call | flops 11274289152 | bytes 18874368 | tf_op jit(solution)/shard_map/experts_forward/pallas_call | solution.py:843
  306.7 36.7 %experts_backward.2 = (bf16[8,8,96,1536]{3,2,1,0:T(8,128)(2,1)}, f32[1024,128]{1,0:T(8,128)}, bf16[1024,768]{1,0:T(8,128)(2,1)}, f32[768,128]{1,0:T(8,128)}, f32[128,128]{1,0:T(8,128)}) custom-call(s32[1]{0:T(128)} %bitcast.offset_ref, bf16[1024,768]{1,0:T(8,128)(2,1)} %all-gather.10.cloned.1.call-done.g_ref, bf16[8,8,96,1536]{3,2,1,0:T(8,128)(2,1)} %bitcast.142, ...), custom_call_target="tpu_custom_call" | custom-call | flops 16106127360 | bytes 37748736 | tf_op jit(solution)/shard_map/experts_backward/pallas_call | solution.py:993
  343.5 46.8 %join_back.3 = (bf16[16,64,768]{2,1,0:T(8,128)(2,1)}, f32[1,768]{1,0:T(1,128)}) custom-call(bf16[16,64,768]{2,1,0:T(8,128)(2,1)} %bitcast.110, bf16[16,64,768]{2,1,0:T(8,128)(2,1)} %get-tuple-element.91.refs_1_, bf16[16,64,768]{2,1,0:T(8,128)(2,1)} %bitcast.106, f32[48,768]{1,0:T(8,128)} %convert_bitcast_fusion.refs_0_.refs_2_.rows_ref.refs_3_), custom_call_target="tpu_custom_call" | custom-call | flops 7864320 | bytes 78643200 | tf_op jit(solution)/shard_map/join_back/pallas_call | solution.py:302
  390.4 20.0 %attend_backward.2 = (bf16[1024,768]{1,0:T(8,128)(2,1)}, bf16[768,768]{1,0:T(8,128)(2,1)}) custom-call(s32[1,2]{1,0:T(1,128)} %starts_ref.7, bf16[1024,768]{1,0:T(8,128)(2,1)} %bitcast.111, bf16[768,768]{1,0:T(8,128)(2,1)} %all-gather.16.cloned.1.call-done.w_ref, bf16[1024,768]{1,0:T(8,128)(2,1)} %bitcast.146, bf16[1024,576]{1,0:T(8,128)(2,1)} %get-tuple-element.101.qkv_ref, ...), custom_call_target="tpu_custom_call" | custom-call | flops 4429185024 | bytes 9437184 | tf_op jit(solution)/shard_map/attend_backward/pallas_call | solution.py:730
  410.4 45.9 %join_back.4 = (bf16[16,64,768]{2,1,0:T(8,128)(2,1)}, f32[1,768]{1,0:T(1,128)}) custom-call(bf16[16,64,768]{2,1,0:T(8,128)(2,1)} %bitcast.112, bf16[16,64,768]{2,1,0:T(8,128)(2,1)} %get-tuple-element.88.refs_1_, bf16[16,64,768]{2,1,0:T(8,128)(2,1)} %get-tuple-element.100.refs_2_, f32[48,768]{1,0:T(8,128)} %convert_bitcast_fusion.refs_0_.refs_2_.rows_ref.refs_3_), custom_call_target="tpu_custom_call" | custom-call | flops 7864320 | bytes 78643200 | tf_op jit(solution)/shard_map/join_back/pallas_call | solution.py:302
  456.3 36.8 %experts_backward.3 = (bf16[8,8,96,1536]{3,2,1,0:T(8,128)(2,1)}, f32[1024,128]{1,0:T(8,128)}, bf16[1024,768]{1,0:T(8,128)(2,1)}, f32[768,128]{1,0:T(8,128)}, f32[128,128]{1,0:T(8,128)}) custom-call(s32[1]{0:T(128)} %bitcast.offset_ref, bf16[1024,768]{1,0:T(8,128)(2,1)} %bitcast.108, bf16[8,8,96,1536]{3,2,1,0:T(8,128)(2,1)} %bitcast.140, ...), custom_call_target="tpu_custom_call" | custom-call | flops 16106127360 | bytes 37748736 | tf_op jit(solution)/shard_map/experts_backward/pallas_call | solution.py:993
  497.0 45.3 %join_back.5 = (bf16[16,64,768]{2,1,0:T(8,128)(2,1)}, f32[1,768]{1,0:T(1,128)}) custom-call(bf16[16,64,768]{2,1,0:T(8,128)(2,1)} %bitcast.109, bf16[16,64,768]{2,1,0:T(8,128)(2,1)} %get-tuple-element.81.refs_1_, bf16[16,64,768]{2,1,0:T(8,128)(2,1)} %get-tuple-element.105.refs_2_, f32[48,768]{1,0:T(8,128)} %convert_bitcast_fusion.refs_0_.refs_2_.rows_ref.refs_3_), custom_call_target="tpu_custom_call" | custom-call | flops 7864320 | bytes 78643200 | tf_op jit(solution)/shard_map/join_back/pallas_call | solution.py:302
  544.1 19.8 %attend_backward.3 = (bf16[1024,768]{1,0:T(8,128)(2,1)}, bf16[768,768]{1,0:T(8,128)(2,1)}) custom-call(s32[1,2]{1,0:T(1,128)} %starts_ref.7, bf16[1024,768]{1,0:T(8,128)(2,1)} %bitcast.126, bf16[768,768]{1,0:T(8,128)(2,1)} %all-gather.12.cloned.1.call-done.w_ref, bf16[1024,768]{1,0:T(8,128)(2,1)} %get-tuple-element.116.a_ref, ...), custom_call_target="tpu_custom_call" | custom-call | flops 4429185024 | bytes 9437184 | tf_op jit(solution)/shard_map/attend_backward/pallas_call | solution.py:730
  563.9 30.7 %line_end.1 = (f32[2,128,768]{2,1,0:T(8,128)}, f32[1,768]{1,0:T(1,128)}) custom-call(bf16[4,2,128,768]{3,2,1,0:T(8,128)(2,1)} %bitcast.97, bf16[2,128,768]{2,1,0:T(8,128)(2,1)} %bitcast.102, bf16[2,128,768]{2,1,0:T(8,128)(2,1)} %bitcast.103, f32[48,768]{1,0:T(8,128)} %convert_bitcast_fusion.refs_0_.refs_2_.rows_ref.refs_3_), custom_call_target="tpu_custom_call" | custom-call | flops 7864320 | bytes 78643200 | tf_op jit(solution)/shard_map/line_end/pallas_call | solution.py:598
  596.4 57.0 %closing.1 = (f32[2,24]{1,0:T(2,128)}, f32[2,24]{1,0:T(2,128)}, f32[2,24,12]{2,1,0:T(8,128)}, f32[2,12,12]{2,1,0:T(8,128)}, f32[2,2,24]{2,1,0:T(2,128)}, /*index...) custom-call(f32[32,40,128]{2,1,0:T(8,128)} %pad_maximum_fusion.2.refs_0_, ...), custom_call_target="tpu_custom_call" | custom-call | tf_op jit(solution)/shard_map/closing/pallas_call | solution.py:174
  653.4 2.1 copy.158
  659.7 8.7 %unpack.1 = (f32[2,8,96,2,512]{4,3,2,1,0:T(2,128)}, f32[2,8,512,96]{3,2,1,0:T(8,128)}) custom-call(bf16[8,96,1536]{2,1,0:T(8,128)(2,1)} %bitcast.93, bf16[8,96,1536]{2,1,0:T(8,128)(2,1)} %bitcast.92), custom_call_target="tpu_custom_call" | custom-call | tf_op jit(solution)/shard_map/unpack/pallas_call | solution.py:1064
  668.4 5.3 copy.162
  (126 shorter events, 35.1 us)
Async XLA Ops:
  7.2 70.8 %all-gather.12.cloned.1.call-start = ((), (), s32[]{:S(2)}) async-start(), calls=%async_computation.7 | async-start | bytes 1327104 | tf_op jit(solution)/shard_map/all_gather | solution.py:1144
  10.3 129.3 %all-gather.14.cloned.1.call-start = ((), (), s32[]{:S(2)}) async-start(), calls=%async_computation.8 | async-start | bytes 21233664 | tf_op jit(solution)/shard_map/all_gather | solution.py:1152
  22.1 193.0 %all-gather.16.cloned.1.call-start = ((), (), s32[]{:S(2)}) async-start(), calls=%async_computation.9 | async-start | bytes 1327104 | tf_op jit(solution)/shard_map/all_gather | solution.py:1144
  23.4 254.7 %all-gather.18.cloned.1.call-start = ((), (), s32[]{:S(2)}) async-start(), calls=%async_computation.10 | async-start | bytes 21233664 | tf_op jit(solution)/shard_map/all_gather | solution.py:1152
  27.3 1.3 copy-start.18
  27.3 1.4 copy-start.19
  27.3 1.5 copy-start.15
  27.3 46.3 %copy-start.9 = (s32[2,1024,2]{1,2,0:T(2,128)S(1)}, s32[2,1024,2]{1,2,0:T(2,128)}, u32[]{:S(2)}) copy-start(s32[2,1024,2]{1,2,0:T(2,128)} %param.17) | copy-start | bytes 49156
  27.4 277.1 %all-gather.10.cloned.1.call-start = ((), (), s32[]{:S(2)}) async-start(), calls=%async_computation.3 | async-start | bytes 1966080 | tf_op jit(solution)/shard_map/all_gather | solution.py:1172
  74.0 1.6 copy-start.8
  74.0 2.3 copy-start.6
  74.8 2.6 copy-start.1
  227.5 116.0 %reduce-scatter.4.cloned.1.call-start = ((), (), s32[]{:S(2)}) async-start(), calls=%async_computation.4 | async-start | bytes 1966080 | tf_op jit(solution)/shard_map/reduce_scatter | solution.py:1186
  228.7 49.4 %copy-start.2 = (s32[1024,128]{1,0:T(8,128)}, s32[1024,128]{1,0:T(8,128)S(1)}, u32[]{:S(2)}) copy-start(s32[1024,128]{1,0:T(8,128)S(1)} %fusion.5.pos_ref) | copy-start | bytes 1572868
  303.9 193.0 %reduce-scatter.6.cloned.1.call-start = ((), (), s32[]{:S(2)}) async-start(), calls=%async_computation.5 | async-start | bytes 21233664 | tf_op jit(solution)/shard_map/reduce_scatter | solution.py:1202
  343.4 316.2 %reduce-scatter.8.cloned.1.call-start = ((), (), s32[]{:S(2)}) async-start(), calls=%async_computation.6 | async-start | bytes 21233664 | tf_op jit(solution)/shard_map/reduce_scatter | solution.py:1202
  493.1 1.9 copy-start.4
  563.9 30.7 %copy-start.11 = (f32[1,768]{1,0:T(1,128)S(1)}, f32[1,768]{1,0:T(1,128)}, u32[]{:S(2)}) copy-start(f32[1,768]{1,0:T(1,128)} %get-tuple-element.126) | copy-start | bytes 9220
  563.9 30.7 %copy-start.12 = (f32[1,768]{1,0:T(1,128)S(1)}, f32[1,768]{1,0:T(1,128)}, u32[]{:S(2)}) copy-start(f32[1,768]{1,0:T(1,128)} %get-tuple-element.124) | copy-start | bytes 9220
  563.9 30.7 %copy-start.13 = (f32[1,768]{1,0:T(1,128)S(1)}, f32[1,768]{1,0:T(1,128)}, u32[]{:S(2)}) copy-start(f32[1,768]{1,0:T(1,128)} %get-tuple-element.125) | copy-start | bytes 9220
  668.4 5.3 copy-start
  673.7 1.5 copy-start.5
  673.7 2.1 copy-start.16
  673.7 2.7 copy-start.14
  (4 other events, 3.7 us)
Sparse Core Ops, SparseCore 0:
  10.4 26.6 all-gather.11
  39.6 98.6 all-gather.13
  140.2 23.8 all-gather.15
  165.9 98.6 all-gather.17
  265.9 36.9 all-gather.9
  305.1 34.3 reduce-scatter.3
  343.6 126.0 reduce-scatter.5
  493.3 157.7 reduce-scatter.7

commit v4 on v3

--- a/solution.py
+++ b/solution.py
@@ -100,17 +100,15 @@
 
 
 def closing_kernel(ndp, inner, layers, consts, wide, *refs):
-    small_ref, proj_refs = refs[0], refs[1 : 1 + layers]
-    refs = refs[1 + layers :]
-    attn_out, moe_out, router_out, mix_out, cvec_out, cmix_out, qkv_out, outw_out = refs[:8]
-    land, proj_lands = refs[8], refs[9 : 9 + layers]
-    square, tall = refs[9 + layers : 11 + layers]
-    sems = refs[11 + layers :]
+    small_ref, proj_ref, above_ref = refs[:3]
+    attn_out, moe_out, router_out, mix_out, cvec_out, cmix_out, qkv_out, outw_out = refs[3:11]
+    land, proj_land, square, tall = refs[11:15]
+    sems = refs[15:]
     count = ndp * inner
     row, col = lax.axis_index("dp"), lax.axis_index("tensor")
     me = row * inner + col
     cols = attn_out.shape[1]
-    rows = qkv_out.shape[1]
+    rows = qkv_out.shape[2]
 
     def anywhere(other):
         return (lax.div(other, inner), lax.rem(other, inner))
@@ -123,24 +121,27 @@
 
     greet_all(count, me, anywhere)
     moves = [
-        swap_all(ndp, row, along, piece(ref), to, *sems[2 + 2 * l : 4 + 2 * l])
-        for l, (ref, to) in enumerate(zip(proj_refs, proj_lands))
-    ] + [swap_all(count, me, anywhere, piece(small_ref), land, *sems[0:2])]
+        swap_all(ndp, row, along, piece(proj_ref), proj_land, *sems[2:4]),
+        swap_all(count, me, anywhere, piece(small_ref), land, *sems[0:2]),
+    ]
     for start, _ in moves:
         start()
     land[me] = small_ref[me]
-    for ref, to in zip(proj_refs, proj_lands):
-        to[row] = ref[row]
+    proj_land[row] = proj_ref[row]
     square[...] = jnp.zeros_like(square)
     tall[...] = jnp.zeros_like(tall)
-    for l in range(layers):
-        moves[l][1]()
-        total = jnp.sum(proj_lands[l][...].astype(F32), axis=0)
+
+    def place(l, total):
         for part in range(3):
-            qkv_out[l, :, part, :] = total[:, part * wide : (part + 1) * wide]
+            qkv_out[l, part] = total[:, part * wide : (part + 1) * wide]
         tall[:rows, :wide] = total[:, 3 * wide :]
         outw_out[l] = tall[...].T[:wide, :rows]
-    moves[layers][1]()
+
+    for l in range(1, layers):
+        place(l, above_ref[l - 1].astype(F32))
+    moves[0][1]()
+    place(0, jnp.sum(proj_land[...].astype(F32), axis=0))
+    moves[1][1]()
     total = jnp.sum(land[...], axis=0)
     square[:cols, :] = total[:cols]
     turned = square[...].T
@@ -149,46 +150,47 @@
     moe_out[...] = turned[at["moe"] : at["moe"] + layers, :cols]
     for l in range(layers):
         begin = at["router"] + l * NEXP
-        router_out[l] = total[:cols, begin : begin + NEXP]
-        mix_out[l] = total[cols : cols + NEXP, l * MIX_STEP : l * MIX_STEP + NEXP]
+        for e in range(NEXP):
+            router_out[e, l : l + 1, :] = turned[begin + e : begin + e + 1, :cols]
+            mix_out[e, l : l + 1, :] = total[
+                cols + e : cols + e + 1, l * MIX_STEP : l * MIX_STEP + NEXP
+            ]
         begin = at["cvec"] + l * consts
         cvec_out[l] = turned[begin : begin + consts, :cols]
         begin = at["cmix"] + l * 2 * consts
         for j in range(consts):
             for k in range(2):
                 lane = begin + k * consts + j
-                cmix_out[l, j, :, k : k + 1] = total[:cols, lane : lane + 1]
-
-
-def closing(small, projections, consts, cols, collective_id):
+                cmix_out[l, j, k : k + 1, :] = turned[lane : lane + 1, :cols]
+
+
+def closing(small, projection, above, consts, layers, cols, collective_id):
     inner, ndp = lax.axis_size("tensor"), lax.axis_size("dp")
-    layers = len(projections)
-    rows, packed = projections[0].shape[1:]
+    rows, packed = projection.shape[1:]
     wide = packed // 4
-    pair = [pltpu.SemaphoreType.DMA((ndp * inner,))] * 2
     shapes = [
-        (layers, cols), (layers, cols), (layers, cols, NEXP), (layers, NEXP, NEXP),
-        (layers, consts, cols), (layers, consts, cols, 2),
-        (layers, rows, 3, wide), (layers, wide, rows),
+        (layers, cols), (layers, cols), (NEXP, layers, cols), (NEXP, layers, NEXP),
+        (layers, consts, cols), (layers, consts, 2, cols),
+        (layers, 3, rows, wide), (layers, wide, rows),
     ]
     return pl.pallas_call(
         functools.partial(closing_kernel, ndp, inner, layers, consts, wide),
         out_shape=[jax.ShapeDtypeStruct(shape, F32) for shape in shapes],
-        in_specs=[VMEM_SPEC] * (1 + layers),
+        in_specs=[VMEM_SPEC] * 3,
         out_specs=[VMEM_SPEC] * len(shapes),
-        scratch_shapes=[pltpu.VMEM(small.shape, F32)]
-        + [pltpu.VMEM(item.shape, BF16) for item in projections]
-        + [
+        scratch_shapes=[
+            pltpu.VMEM(small.shape, F32),
+            pltpu.VMEM(projection.shape, BF16),
             pltpu.VMEM((-(-cols // LANES) * LANES, LANES), F32),
             pltpu.VMEM((-(-rows // LANES) * LANES, -(-wide // LANES) * LANES), F32),
         ]
-        + pair
-        + [pltpu.SemaphoreType.DMA((ndp,))] * (2 * layers),
+        + [pltpu.SemaphoreType.DMA((ndp * inner,))] * 2
+        + [pltpu.SemaphoreType.DMA((ndp,))] * 2,
         compiler_params=pltpu.CompilerParams(
             collective_id=collective_id, has_side_effects=True, vmem_limit_bytes=VMEM_LIMIT
         ),
         name="closing",
-    )(small, *projections)
+    )(small, projection, above)
 
 
 def join_kernel(back, gain_row, nt, pieces, lag, *refs):
@@ -885,14 +887,65 @@
 
 
 def experts_back_kernel(
-    cap, layer, at, consts, own, offset_ref, g_ref, w_ref, x_ref, gu_ref, rowpos_ref, pos_ref, wd_ref,
+    cap, layer, at, consts, own, g_ref, w_ref, x_ref, gu_ref, rowpos_ref, pos_ref, wd_ref,
     b_ref, small_ref, rows_ref, mix_ref, zprev_ref, gprev_ref, sums_ref, mixes_ref,
     gw_ref, below_ref, gb_ref, sums_out, mixes_out, pick_scr, gx_scr, gg_scr, gb_scr, zs_scr,
+    halves, inbox, out_sems, in_sems,
 ):
     e = pl.program_id(0)
+    last = pl.num_programs(0) - 1
+    me = lax.axis_index("dp")
+    parity = lax.rem(me, 2)
+    partner = me + 1 - 2 * parity
+
+    def to_partner(expert):
+        return pltpu.make_async_remote_copy(
+            src_ref=halves.at[lax.rem(expert, 2), 1 - parity],
+            dst_ref=inbox.at[expert],
+            send_sem=out_sems.at[expert],
+            recv_sem=in_sems.at[expert],
+            device_id={"dp": partner},
+            device_id_type=MESH,
+        )
+
+    @pl.when(e == 0)
+    def _():
+        barrier = pltpu.get_barrier_semaphore()
+        pl.semaphore_signal(barrier, inc=1, device_id={"dp": partner}, device_id_type=MESH)
+        pl.semaphore_wait(barrier, 1)
+
+    @pl.when(e < last)
+    def _():
+        one_expert_back(
+            cap, e, g_ref, w_ref, x_ref, gu_ref, rowpos_ref, pos_ref, wd_ref, pick_scr, gx_scr, gg_scr,
+            halves,
+        )
+        to_partner(e).start()
+
+    @pl.when(e > 0)
+    def _():
+        before = e - 1
+        to_partner(before).wait()
+        gw_ref[:, 0] = (
+            halves[lax.rem(before, 2), parity].astype(F32) + inbox[before].astype(F32)
+        ).astype(BF16)
+
+    @pl.when(e == last)
+    def _():
+        tokens_back(
+            layer, at, consts, own, g_ref, wd_ref, b_ref, small_ref, rows_ref, mix_ref, zprev_ref,
+            gprev_ref, sums_ref, mixes_ref, below_ref, gb_ref, sums_out, mixes_out, pick_scr, gx_scr,
+            gg_scr, gb_scr, zs_scr,
+        )
+
+
+def one_expert_back(
+    cap, e, g_ref, w_ref, x_ref, gu_ref, rowpos_ref, pos_ref, wd_ref, pick_scr, gx_scr, gg_scr, halves,
+):
     seq_len, width = g_ref.shape
     shards_dp, _, rows, wide3 = w_ref.shape
     half = wide3 // 3
+    slot = lax.rem(e, 2)
     w = w_ref[...].reshape(width, wide3)
     take = (
         lax.broadcasted_iota(jnp.int32, (cap, seq_len), 0) == rowpos_ref[0]
@@ -911,10 +964,12 @@
     gup = gh * g * sig
     both = jnp.concatenate([gg.astype(BF16), gup.astype(BF16)], axis=1)
     gy = (gf * weight).astype(BF16)
-    gw_ref[:, 0, :, : 2 * half] = dot_tn(x_ref[0], both).astype(BF16).reshape(
-        shards_dp, rows, 2 * half
-    )
-    gw_ref[:, 0, :, 2 * half :] = dot_tn(gy, h).astype(BF16).reshape(shards_dp, rows, half)
+    gw_in = dot_tn(x_ref[0], both).astype(BF16)
+    gw_down = dot_tn(gy, h).astype(BF16)
+    for shard in range(shards_dp):
+        own_rows = slice(shard * rows, (shard + 1) * rows)
+        halves[slot, shard % 2, shard // 2, :, : 2 * half] = gw_in[own_rows]
+        halves[slot, shard % 2, shard // 2, :, 2 * half :] = gw_down[own_rows]
     here = pl.ds(pl.multiple_of(e * cap, cap), cap)
     gx_scr[here, :] = dot_nt(both, w[:, : 2 * half]).astype(BF16)
     s_high, s_low = two_parts(slot_grad)
@@ -926,87 +981,92 @@
         lax.broadcasted_iota(jnp.int32, (seq_len, cap), 1) == column
     ).astype(F32).astype(BF16)
 
-    @pl.when(e == pl.num_programs(0) - 1)
-    def _():
-        mine = pl.ds(pl.multiple_of(offset_ref[0], own), own)
-        b_own, g_own = b_ref[mine, :], g_ref[mine, :].astype(F32)
-        wd_own = wd_ref[mine, :]
-        lane, here_own, alpha0, alpha1, gate, keep = const_parts(
-            dot(b_own, small_ref[...]), wd_own, layer, at, consts
-        )
-        b_dot = jnp.sum(b_own.astype(F32) * g_own, axis=1, keepdims=True)
-        c_dot = jnp.zeros_like(wd_own)
-        for j in range(consts):
-            row = at["cvec"] + layer * consts + j
-            one = jnp.sum(g_own * rows_ref[row : row + 1, :], axis=1, keepdims=True)
-            c_dot = jnp.where(lane == EXPERTS + 2 + j, one, c_dot)
-        gw_own = jnp.where(here_own, alpha0 * b_dot + alpha1 * c_dot, 0.0)
-        gw_own = jnp.where(lane == EXPERTS + 1, b_dot, gw_own)
-        inner = gate * (alpha0 * b_dot + alpha1 * c_dot)
-        gt0 = alpha0 * (gate * b_dot - inner)
-        gt1 = alpha1 * (gate * c_dot - inner)
-
-        slots = dot(pick_scr[...], gg_scr[...])
-        zs_scr[...] = slots[:, :LANES] + slots[:, LANES:]
-        zs_scr[mine, :] += gw_own
-        gw = zs_scr[...]
-        wd = wd_ref[...]
-        gz = wd * (gw - jnp.sum(wd * gw, axis=1, keepdims=True)) + gprev_ref[...]
-        z_high, z_low = two_parts(gz)
-        below_ref[...] = dot_nt(z_high, mix_ref[...]) + dot_nt(z_low, mix_ref[...])
-        p_high, p_low = two_parts(zprev_ref[...])
-        mixes_out[...] = mixes_ref[...] + shift(
-            dot_tn(p_high, z_high) + dot_tn(p_high, z_low) + dot_tn(p_low, z_high), layer * MIX_STEP
-        )
-        zs_scr[...] = shift(gz, at["router"] + layer * NEXP)
-        up = at["cmix"] + layer * 2 * consts - EXPERTS - 2
-        zs_scr[mine, :] += shift(gt0, up) + shift(gt1, up + consts)
-        z_high, z_low = two_parts(zs_scr[...])
-        gb_scr[...] = (
-            dot(pick_scr[...], gx_scr[...])
-            + dot_nt(z_high, small_ref[...])
-            + dot_nt(z_low, small_ref[...])
-        )
-        gb_scr[mine, :] += keep * g_own
-        gb_ref[...] = gb_scr[...].astype(BF16)
-        i_high, i_low = two_parts(
-            shift(gate * alpha1, at["cvec"] + layer * consts - EXPERTS - 2)
-        )
-        g_low = g_ref[mine, :]
-        sums_out[...] = (
-            sums_ref[...]
-            + dot_tn(b_ref[...], z_high)
-            + dot_tn(b_ref[...], z_low)
-            + dot_tn(g_low, i_high)
-            + dot_tn(g_low, i_low)
-        )
+
+def tokens_back(
+    layer, at, consts, own, g_ref, wd_ref, b_ref, small_ref, rows_ref, mix_ref, zprev_ref, gprev_ref,
+    sums_ref, mixes_ref, below_ref, gb_ref, sums_out, mixes_out, pick_scr, gx_scr, gg_scr, gb_scr, zs_scr,
+):
+    mine = pl.ds(pl.multiple_of(lax.axis_index("tensor") * own, own), own)
+    b_own, g_own = b_ref[mine, :], g_ref[mine, :].astype(F32)
+    wd_own = wd_ref[mine, :]
+    lane, here_own, alpha0, alpha1, gate, keep = const_parts(
+        dot(b_own, small_ref[...]), wd_own, layer, at, consts
+    )
+    b_dot = jnp.sum(b_own.astype(F32) * g_own, axis=1, keepdims=True)
+    c_dot = jnp.zeros_like(wd_own)
+    for j in range(consts):
+        row = at["cvec"] + layer * consts + j
+        one = jnp.sum(g_own * rows_ref[row : row + 1, :], axis=1, keepdims=True)
+        c_dot = jnp.where(lane == EXPERTS + 2 + j, one, c_dot)
+    gw_own = jnp.where(here_own, alpha0 * b_dot + alpha1 * c_dot, 0.0)
+    gw_own = jnp.where(lane == EXPERTS + 1, b_dot, gw_own)
+    inner = gate * (alpha0 * b_dot + alpha1 * c_dot)
+    gt0 = alpha0 * (gate * b_dot - inner)
+    gt1 = alpha1 * (gate * c_dot - inner)
+
+    slots = dot(pick_scr[...], gg_scr[...])
+    zs_scr[...] = slots[:, :LANES] + slots[:, LANES:]
+    zs_scr[mine, :] += gw_own
+    gw = zs_scr[...]
+    wd = wd_ref[...]
+    gz = wd * (gw - jnp.sum(wd * gw, axis=1, keepdims=True)) + gprev_ref[...]
+    z_high, z_low = two_parts(gz)
+    below_ref[...] = dot_nt(z_high, mix_ref[...]) + dot_nt(z_low, mix_ref[...])
+    p_high, p_low = two_parts(zprev_ref[...])
+    mixes_out[...] = mixes_ref[...] + shift(
+        dot_tn(p_high, z_high) + dot_tn(p_high, z_low) + dot_tn(p_low, z_high), layer * MIX_STEP
+    )
+    zs_scr[...] = shift(gz, at["router"] + layer * NEXP)
+    up = at["cmix"] + layer * 2 * consts - EXPERTS - 2
+    zs_scr[mine, :] += shift(gt0, up) + shift(gt1, up + consts)
+    z_high, z_low = two_parts(zs_scr[...])
+    gb_scr[...] = (
+        dot(pick_scr[...], gx_scr[...])
+        + dot_nt(z_high, small_ref[...])
+        + dot_nt(z_low, small_ref[...])
+    )
+    gb_scr[mine, :] += keep * g_own
+    gb_ref[...] = gb_scr[...].astype(BF16)
+    i_high, i_low = two_parts(
+        shift(gate * alpha1, at["cvec"] + layer * consts - EXPERTS - 2)
+    )
+    g_low = g_ref[mine, :]
+    sums_out[...] = (
+        sums_ref[...]
+        + dot_tn(b_ref[...], z_high)
+        + dot_tn(b_ref[...], z_low)
+        + dot_tn(g_low, i_high)
+        + dot_tn(g_low, i_low)
+    )
 
 
 def experts_backward(
-    layer, at, consts, own, offset, g_all, w_exp, x, gu, rowpos, pos, wd, b_all, small, rows_t, mix,
+    collective_id, layer, at, consts, own, g_all, w_exp, x, gu, rowpos, pos, wd, b_all, small, rows_t, mix,
     z_prev, grad_prev, sums, mixes, cap,
 ):
     seq_len, width = g_all.shape
     shards_dp, count, rows, wide3 = w_exp.shape
     half = wide3 // 3
-    weight_spec = pl.BlockSpec((shards_dp, 1, rows, wide3), lambda e: (0, e, 0, 0))
+    weight_spec = pl.BlockSpec(
+        (shards_dp, 1, rows, wide3), lambda e: (0, jnp.minimum(e, count - 1), 0, 0)
+    )
+    half_shape = (shards_dp // 2, 1, rows, wide3)
     return pl.pallas_call(
         functools.partial(experts_back_kernel, cap, layer, at, consts, own),
-        grid=(count,),
+        grid=(count + 1,),
         out_shape=[
-            jax.ShapeDtypeStruct(w_exp.shape, BF16),
+            jax.ShapeDtypeStruct((shards_dp // 2,) + w_exp.shape[1:], BF16),
             jax.ShapeDtypeStruct((seq_len, LANES), F32),
             jax.ShapeDtypeStruct((seq_len, width), BF16),
             jax.ShapeDtypeStruct((width, LANES), F32),
             jax.ShapeDtypeStruct((LANES, LANES), F32),
         ],
         in_specs=[
-            pl.BlockSpec(memory_space=pltpu.SMEM),
             whole((seq_len, width)),
             weight_spec,
-            pl.BlockSpec((1, cap, width), lambda e: (e, 0, 0)),
-            pl.BlockSpec((1, cap, 2 * half), lambda e: (e, 0, 0)),
-            pl.BlockSpec((1, 1, seq_len), lambda e: (e, 0, 0)),
+            pl.BlockSpec((1, cap, width), lambda e: (jnp.minimum(e, count - 1), 0, 0)),
+            pl.BlockSpec((1, cap, 2 * half), lambda e: (jnp.minimum(e, count - 1), 0, 0)),
+            pl.BlockSpec((1, 1, seq_len), lambda e: (jnp.minimum(e, count - 1), 0, 0)),
             whole((seq_len, LANES)),
             whole((seq_len, LANES)),
             whole((seq_len, width)),
@@ -1019,7 +1079,7 @@
             whole((LANES, LANES)),
         ],
         out_specs=[
-            weight_spec,
+            pl.BlockSpec(half_shape, lambda e: (0, jnp.maximum(e - 1, 0), 0, 0)),
             whole((seq_len, LANES)),
             whole((seq_len, width)),
             whole((width, LANES)),
@@ -1031,8 +1091,14 @@
             pltpu.VMEM((count * cap, 2 * LANES), BF16),
             pltpu.VMEM((seq_len, width), F32),
             pltpu.VMEM((seq_len, LANES), F32),
+            pltpu.VMEM((2, 2, shards_dp // 2, rows, wide3), BF16),
+            pltpu.VMEM((count, shards_dp // 2, rows, wide3), BF16),
+            pltpu.SemaphoreType.DMA((count,)),
+            pltpu.SemaphoreType.DMA((count,)),
         ],
-        compiler_params=pltpu.CompilerParams(vmem_limit_bytes=VMEM_LIMIT),
+        compiler_params=pltpu.CompilerParams(
+            collective_id=collective_id, has_side_effects=True, vmem_limit_bytes=VMEM_LIMIT
+        ),
         cost_estimate=pl.CostEstimate(
             flops=count * (4 * cap * seq_len * width + 12 * cap * width * half),
             bytes_accessed=4 * count * width * wide3,
@@ -1040,21 +1106,18 @@
         ),
         name="experts_backward",
     )(
-        offset, g_all, w_exp, x, gu, rowpos, pos, wd, b_all, small, rows_t, mix, z_prev, grad_prev,
+        g_all, w_exp, x, gu, rowpos, pos, wd, b_all, small, rows_t, mix, z_prev, grad_prev,
         sums, mixes,
     )
 
 
 def unpack_kernel(half, *refs):
-    *in_refs, up_ref, down_ref, tall = refs
-    rows = up_ref.shape[2]
-    tall[...] = jnp.zeros_like(tall)
+    *in_refs, up_ref, down_ref = refs
     for l, ref in enumerate(in_refs):
         values = ref[0].astype(F32)
         for part in range(2):
             up_ref[l, 0, :, part, :] = values[:, part * half : (part + 1) * half]
-        tall[:rows, :] = values[:, 2 * half :]
-        down_ref[l, 0] = tall[...].T[:, :rows]
+        down_ref[l, 0] = values[:, 2 * half :]
 
 
 def unpack(items):
@@ -1066,14 +1129,13 @@
         grid=(count,),
         out_shape=[
             jax.ShapeDtypeStruct((layers, count, rows, 2, half), F32),
-            jax.ShapeDtypeStruct((layers, count, half, rows), F32),
+            jax.ShapeDtypeStruct((layers, count, rows, half), F32),
         ],
         in_specs=[pl.BlockSpec((1, rows, wide3), lambda e: (e, 0, 0))] * layers,
         out_specs=[
             pl.BlockSpec((layers, 1, rows, 2, half), lambda e: (0, e, 0, 0, 0)),
-            pl.BlockSpec((layers, 1, half, rows), lambda e: (0, e, 0, 0)),
+            pl.BlockSpec((layers, 1, rows, half), lambda e: (0, e, 0, 0)),
         ],
-        scratch_shapes=[pltpu.VMEM((-(-rows // LANES) * LANES, half), F32)],
         compiler_params=pltpu.CompilerParams(vmem_limit_bytes=VMEM_LIMIT),
         name="unpack",
     )(*items)
@@ -1196,10 +1258,10 @@
     for l in reversed(range(layers)):
         s = stored[l]
         gw_exp, below, partial, sums, mixes = experts_backward(
-            l, at, consts, own, offset.reshape(1), grad_all, exp_w[l], s["x"], s["gu"], rowpos[l],
+            next_id + 2, l, at, consts, own, grad_all, exp_w[l], s["x"], s["gu"], rowpos[l],
             pos[l], s["wd"], s["b_all"], small, rows_t, s["mix"], s["z_prev"], below, sums, mixes, cap,
         )
-        exp_grads[l] = lax.psum_scatter(gw_exp, "dp", scatter_dimension=0, tiled=False)
+        exp_grads[l] = sum_over_pairs(gw_exp)
         if l + 1 < layers:
             partial, exp_grads[l + 1] = lax.optimization_barrier((partial, exp_grads[l + 1]))
         else:
@@ -1212,15 +1274,17 @@
         )
         attn_grads[l] = gw_attn.reshape(ndp, rows, 4 * wide)
         if l > 0:
+            attn_grads[l] = lax.psum_scatter(attn_grads[l], "dp", scatter_dimension=0, tiled=False)
             grad_all, gains_a[l] = join(
                 True, partial, [s["hidden"], grad_mid], rows_t, at["attn"] + l, next_id + 1
             )
         else:
+            partial, attn_grads[1:] = lax.optimization_barrier((partial, attn_grads[1:]))
             skip = lax.dynamic_slice_in_dim(grad_mid, offset, own, 0)
             grad, gains_a[l] = line_exchange(
                 "end", [partial, hidden_in, skip, rows_t], own, width, next_id + 1
             )
-        next_id += 2
+        next_id += 3
     hidden_out = hidden_out.astype(F32) + extra.astype(F32)
 
     gains = jnp.concatenate(gains_a + gains_m, axis=0)
@@ -1233,9 +1297,14 @@
         axis=1,
     )
     attn_g, moe_g, router_g, mix_g, cvec_g, cmix_g, qkv_g, outw_g = closing(
-        sums, attn_grads, consts, cols, next_id
+        sums, attn_grads[0], jnp.stack(attn_grads[1:]), consts, layers, cols, next_id
     )
     up_grad, down_grad = unpack(exp_grads)
+    qkv_g = jnp.swapaxes(qkv_g, 1, 2)
+    router_g = jnp.transpose(router_g, (1, 2, 0))
+    mix_g = jnp.swapaxes(mix_g, 0, 1)
+    cmix_g = jnp.swapaxes(cmix_g, 2, 3)
+    down_grad = jnp.swapaxes(down_grad, 2, 3)
     return (
         hidden_out,
         grad,
@@ -1249,6 +1318,14 @@
         cmix_g,
         up_grad,
         down_grad,
+    )
+
+
+def sum_over_pairs(values):
+    members = lax.axis_size("dp")
+    groups = [list(range(parity, members, 2)) for parity in range(2)]
+    return lax.psum_scatter(
+        values, "dp", scatter_dimension=0, axis_index_groups=groups, tiled=False
     )
 
 

time: 689 us -> 669 us (0.971)
  Pallas kernels: 614 us -> 604 us
  local copies, waits for them, and re-layouts: 41.7 us -> 32.7 us
    pallas_call x1, Pallas kernels: 57 us -> 29.2 us  [closing(): pl.pallas_call(functools.partial(closing_kernel, ndp, inner, layers, cons...]
    pallas_call x2, Pallas kernels: 73.5 us -> 82.9 us  [experts_backward(): pl.pallas_call(functools.partial(experts_back_kernel, cap, layer, at, con...]
    unnamed x60 -> x67, local copies, waits for them, and re-layouts: 17.8 us -> 8.81 us
    pallas_call x6, Pallas kernels: 284 us -> 292 us  [join(): pl.pallas_call(functools.partial(join_kernel, back, gain_row, nt, pieces,...]
  transfers between devices with their start and end apart: 8 -> 9, of which waited for: 0 -> 0; matrix products, arithmetic and copies ran while one was open for 6% -> 5% of each run, Pallas kernels for 88% -> 90%
where the time goes in v4:
time: 669 us; the launch traced here: 665 us
  Pallas kernels  604 us (90%)
  local copies, waits for them, and re-layouts  32.7 us (5%)
  between operations  14.6 us (2%)
  other arithmetic  10.7 us (2%)
    pallas_call x6, Pallas kernels, join(): pl.pallas_call(functools.partial(join_kernel, back, gain_row, nt, pieces,...  292 us
    pallas_call x2, Pallas kernels, experts_backward(): pl.pallas_call(functools.partial(experts_back_kernel, cap, layer, at, con...  82.9 us
    pallas_call x2, Pallas kernels, line_exchange(): pl.pallas_call(functools.partial(line_kernel, kind, nt, chunks, lag, extr...  75.2 us
    pallas_call x2, Pallas kernels, experts_forward(): pl.pallas_call(functools.partial(experts_kernel, cap, layer, at, consts),...  51.9 us
    pallas_call x2, Pallas kernels, attend_backward(): pl.pallas_call(functools.partial(attend_back_kernel, heads, spans, PIC),...  39.4 us
    pallas_call x1, Pallas kernels, closing(): pl.pallas_call(functools.partial(closing_kernel, ndp, inner, layers, cons...  29.2 us
    pallas_call x2, Pallas kernels, attend_forward(): pl.pallas_call(functools.partial(attend_kernel, heads, spans, PIC, raw),...  25.5 us
  transfers between devices with their start and end apart: 9, of which 0 were waited for; matrix products, arithmetic and copies ran while one was open for 5% of the time, Pallas kernels for 90%

profile of v4, /device:TPU:0, one launch (start us, length us, event | category | flops | bytes accessed | tf_op | source)
XLA Modules:
  0.0 665.2 jit_solution(15297757294470598864)
XLA Ops:
  10.3 5.0 fusion.10
  15.3 2.8 reshape_squeeze.13
  18.1 2.4 slice_bitcast_fusion
  24.6 2.7 pad_maximum_fusion.1
  29.6 43.0 %line_start.1 = (bf16[4,2,128,768]{3,2,1,0:T(8,128)(2,1)}, bf16[32,24,128]{2,1,0:T(8,128)(2,1)}) custom-call(bf16[2,128,768]{2,1,0:T(8,128)(2,1)} %bitcast.108, bf16[24,128]{1,0:T(8,128)(2,1)} %pad.19.refs_1_), custom_call_target="tpu_custom_call" | custom-call | flops 7864320 | bytes 78643200 | tf_op jit(solution)/shard_map/line_start/pallas_call | solution.py:600
  78.0 13.2 %attend_forward.2 = (bf16[1024,576]{1,0:T(8,128)(2,1)}, bf16[1024,192]{1,0:T(8,128)(2,1)}, f32[1024,3]{1,0:T(8,128)}, bf16[1024,768]{1,0:T(8,128)(2,1)}, bf16[1024,768]{1,0:T(8,128)(2,1)}) custom-call(s32[1,2]{1,0:T(1,128)} %starts_ref.7, bf16[1024,768]{1,0:T(8,128)(2,1)} %bitcast.101, bf16[768,768]{1,0:T(8,128)(2,1)} %all-gather.12.cloned.1.call-done.w_ref, ...), custom_call_target="tpu_custom_call" | custom-call | flops 2013265920 | bytes 4718592 | tf_op jit(solution)/shard_map/attend_forward/pallas_call | solution.py:673
  91.1 48.4 %join.3 = (bf16[16,64,768]{2,1,0:T(8,128)(2,1)}, bf16[16,64,768]{2,1,0:T(8,128)(2,1)}) custom-call(bf16[16,64,768]{2,1,0:T(8,128)(2,1)} %bitcast.105, bf16[16,64,768]{2,1,0:T(8,128)(2,1)} %bitcast.102, f32[48,768]{1,0:T(8,128)} %convert_bitcast_fusion.refs_0_.refs_2_.rows_ref.refs_3_), custom_call_target="tpu_custom_call" | custom-call | flops 7864320 | bytes 78643200 | tf_op jit(solution)/shard_map/join/pallas_call | solution.py:304
  139.6 26.1 %experts_forward.2 = (bf16[8,256,768]{2,1,0:T(8,128)(2,1)}, bf16[8,256,1024]{2,1,0:T(8,128)(2,1)}, f32[1024,128]{1,0:T(8,128)}, f32[1024,128]{1,0:T(8,128)}, bf1...) custom-call(bf16[1024,768]{1,0:T(8,128)(2,1)} %bitcast.155, bf16[8,8,96,1536]{3,2,1,0:T(8,128)(2,1)} %bitcast.150, ...), custom_call_target="tpu_custom_call" | custom-call | flops 11274289152 | bytes 18874368 | tf_op jit(solution)/shard_map/experts_forward/pallas_call | solution.py:845
  165.7 49.5 %join.4 = (bf16[16,64,768]{2,1,0:T(8,128)(2,1)}, bf16[16,64,768]{2,1,0:T(8,128)(2,1)}) custom-call(bf16[16,64,768]{2,1,0:T(8,128)(2,1)} %bitcast.106, bf16[16,64,768]{2,1,0:T(8,128)(2,1)} %bitcast.107, f32[48,768]{1,0:T(8,128)} %convert_bitcast_fusion.refs_0_.refs_2_.rows_ref.refs_3_), custom_call_target="tpu_custom_call" | custom-call | flops 7864320 | bytes 78643200 | tf_op jit(solution)/shard_map/join/pallas_call | solution.py:304
  215.2 12.3 %attend_forward.3 = (bf16[1024,576]{1,0:T(8,128)(2,1)}, bf16[1024,192]{1,0:T(8,128)(2,1)}, f32[1024,3]{1,0:T(8,128)}, bf16[1024,768]{1,0:T(8,128)(2,1)}) custom-call(s32[1,2]{1,0:T(1,128)} %starts_ref.7, bf16[1024,768]{1,0:T(8,128)(2,1)} %bitcast.157, bf16[768,768]{1,0:T(8,128)(2,1)} %all-gather.16.cloned.1.call-done.w_ref), custom_call_target="tpu_custom_call" | custom-call | flops 2013265920 | bytes 4718592 | tf_op jit(solution)/shard_map/attend_forward/pallas_call | solution.py:673
  230.1 47.9 %join.5 = (bf16[16,64,768]{2,1,0:T(8,128)(2,1)}, bf16[16,64,768]{2,1,0:T(8,128)(2,1)}) custom-call(bf16[16,64,768]{2,1,0:T(8,128)(2,1)} %bitcast.103, bf16[16,64,768]{2,1,0:T(8,128)(2,1)} %get-tuple-element.90.refs_1_, f32[48,768]{1,0:T(8,128)} %convert_bitcast_fusion.refs_0_.refs_2_.rows_ref.refs_3_), custom_call_target="tpu_custom_call" | custom-call | flops 7864320 | bytes 78643200 | tf_op jit(solution)/shard_map/join/pallas_call | solution.py:304
  278.1 25.8 %experts_forward.3 = (bf16[8,256,768]{2,1,0:T(8,128)(2,1)}, bf16[8,256,1024]{2,1,0:T(8,128)(2,1)}, f32[1024,128]{1,0:T(8,128)}, f32[1024,128]{1,0:T(8,128)}, bf1...) custom-call(bf16[1024,768]{1,0:T(8,128)(2,1)} %bitcast.159, bf16[8,8,96,1536]{3,2,1,0:T(8,128)(2,1)} %bitcast.152, ...), custom_call_target="tpu_custom_call" | custom-call | flops 11274289152 | bytes 18874368 | tf_op jit(solution)/shard_map/experts_forward/pallas_call | solution.py:845
  306.7 41.5 %experts_backward.2 = (bf16[4,8,96,1536]{3,2,1,0:T(8,128)(2,1)}, f32[1024,128]{1,0:T(8,128)}, bf16[1024,768]{1,0:T(8,128)(2,1)}, f32[768,128]{1,0:T(8,128)}, f32[128,128]{1,0:T(8,128)}) custom-call(bf16[1024,768]{1,0:T(8,128)(2,1)} %all-gather.10.cloned.1.call-done.g_ref, bf16[8,8,96,1536]{3,2,1,0:T(8,128)(2,1)} %bitcast.153, ...), custom_call_target="tpu_custom_call" | custom-call | flops 16106127360 | bytes 37748736 | tf_op jit(solution)/shard_map/experts_backward/pallas_call | solution.py:1054
  348.3 49.0 %join_back.3 = (bf16[16,64,768]{2,1,0:T(8,128)(2,1)}, f32[1,768]{1,0:T(1,128)}) custom-call(bf16[16,64,768]{2,1,0:T(8,128)(2,1)} %bitcast.117, bf16[16,64,768]{2,1,0:T(8,128)(2,1)} %get-tuple-element.93.refs_1_, bf16[16,64,768]{2,1,0:T(8,128)(2,1)} %bitcast.113, f32[48,768]{1,0:T(8,128)} %convert_bitcast_fusion.refs_0_.refs_2_.rows_ref.refs_3_), custom_call_target="tpu_custom_call" | custom-call | flops 7864320 | bytes 78643200 | tf_op jit(solution)/shard_map/join_back/pallas_call | solution.py:304
  397.3 19.8 %attend_backward.2 = (bf16[1024,768]{1,0:T(8,128)(2,1)}, bf16[768,768]{1,0:T(8,128)(2,1)}) custom-call(s32[1,2]{1,0:T(1,128)} %starts_ref.7, bf16[1024,768]{1,0:T(8,128)(2,1)} %bitcast.118, bf16[768,768]{1,0:T(8,128)(2,1)} %all-gather.16.cloned.1.call-done.w_ref, bf16[1024,768]{1,0:T(8,128)(2,1)} %bitcast.158, bf16[1024,576]{1,0:T(8,128)(2,1)} %get-tuple-element.103.qkv_ref, ...), custom_call_target="tpu_custom_call" | custom-call | flops 4429185024 | bytes 9437184 | tf_op jit(solution)/shard_map/attend_backward/pallas_call | solution.py:732
  417.2 48.3 %join_back.4 = (bf16[16,64,768]{2,1,0:T(8,128)(2,1)}, f32[1,768]{1,0:T(1,128)}) custom-call(bf16[16,64,768]{2,1,0:T(8,128)(2,1)} %bitcast.119, bf16[16,64,768]{2,1,0:T(8,128)(2,1)} %get-tuple-element.90.refs_1_, bf16[16,64,768]{2,1,0:T(8,128)(2,1)} %get-tuple-element.102.refs_2_, f32[48,768]{1,0:T(8,128)} %convert_bitcast_fusion.refs_0_.refs_2_.rows_ref.refs_3_), custom_call_target="tpu_custom_call" | custom-call | flops 7864320 | bytes 78643200 | tf_op jit(solution)/shard_map/join_back/pallas_call | solution.py:304
  465.4 41.4 %experts_backward.3 = (bf16[4,8,96,1536]{3,2,1,0:T(8,128)(2,1)}, f32[1024,128]{1,0:T(8,128)}, bf16[1024,768]{1,0:T(8,128)(2,1)}, f32[768,128]{1,0:T(8,128)}, f32[128,128]{1,0:T(8,128)}) custom-call(bf16[1024,768]{1,0:T(8,128)(2,1)} %bitcast.114, bf16[8,8,96,1536]{3,2,1,0:T(8,128)(2,1)} %bitcast.151, bf16[8,256,768]{2,1,0:T(8,128)(2,1)} %get-tuple-element.108.x_ref, ...), custom_call_target="tpu_custom_call" | custom-call | flops 16106127360 | bytes 37748736 | tf_op jit(solution)/shard_map/experts_backward/pallas_call | solution.py:1054
  508.7 2.0 convert_add_fusion
  510.7 49.0 %join_back.5 = (bf16[16,64,768]{2,1,0:T(8,128)(2,1)}, f32[1,768]{1,0:T(1,128)}) custom-call(bf16[16,64,768]{2,1,0:T(8,128)(2,1)} %bitcast.116, bf16[16,64,768]{2,1,0:T(8,128)(2,1)} %get-tuple-element.83.refs_1_, bf16[16,64,768]{2,1,0:T(8,128)(2,1)} %get-tuple-element.107.refs_2_, f32[48,768]{1,0:T(8,128)} %convert_bitcast_fusion.refs_0_.refs_2_.rows_ref.refs_3_), custom_call_target="tpu_custom_call" | custom-call | flops 7864320 | bytes 78643200 | tf_op jit(solution)/shard_map/join_back/pallas_call | solution.py:304
  559.7 19.6 %attend_backward.3 = (bf16[1024,768]{1,0:T(8,128)(2,1)}, bf16[768,768]{1,0:T(8,128)(2,1)}) custom-call(s32[1,2]{1,0:T(1,128)} %starts_ref.7, bf16[1024,768]{1,0:T(8,128)(2,1)} %bitcast.133, bf16[768,768]{1,0:T(8,128)(2,1)} %all-gather.12.cloned.1.call-done.w_ref, bf16[1024,768]{1,0:T(8,128)(2,1)} %get-tuple-element.118.a_ref, ...), custom_call_target="tpu_custom_call" | custom-call | flops 4429185024 | bytes 9437184 | tf_op jit(solution)/shard_map/attend_backward/pallas_call | solution.py:732
  579.3 1.8 constant_dynamic-slice_fusion
  581.1 32.2 %line_end.1 = (f32[2,128,768]{2,1,0:T(8,128)}, f32[1,768]{1,0:T(1,128)}) custom-call(bf16[4,2,128,768]{3,2,1,0:T(8,128)(2,1)} %bitcast.104, bf16[2,128,768]{2,1,0:T(8,128)(2,1)} %bitcast.109, bf16[2,128,768]{2,1,0:T(8,128)(2,1)} %bitcast.110, f32[48,768]{1,0:T(8,128)} %convert_bitcast_fusion.refs_0_.refs_2_.rows_ref.refs_3_), custom_call_target="tpu_custom_call" | custom-call | flops 7864320 | bytes 78643200 | tf_op jit(solution)/shard_map/line_end/pallas_call | solution.py:600
  615.2 29.2 %closing.1 = (f32[2,24]{1,0:T(2,128)}, f32[2,24]{1,0:T(2,128)}, f32[12,2,24]{2,1,0:T(2,128)}, f32[12,2,12]{2,1,0:T(2,128)}, f32[2,2,24]{2,1,0:T(2,128)}, /*index...) custom-call(f32[32,40,128]{2,1,0:T(8,128)} %pad_maximum_fusion.2.refs_0_, ...), custom_call_target="tpu_custom_call" | custom-call | tf_op jit(solution)/shard_map/closing/pallas_call | solution.py:176
  644.4 8.1 %unpack.1 = (f32[2,8,96,2,512]{4,3,2,1,0:T(2,128)}, f32[2,8,96,512]{3,2,1,0:T(8,128)}) custom-call(bf16[8,96,1536]{2,1,0:T(8,128)(2,1)} %bitcast.100, bf16[8,96,1536]{2,1,0:T(8,128)(2,1)} %bitcast.99), custom_call_target="tpu_custom_call" | custom-call | tf_op jit(solution)/shard_map/unpack/pallas_call | solution.py:1127
  (136 shorter events, 29.8 us)
Async XLA Ops:
  7.2 70.8 %all-gather.12.cloned.1.call-start = ((), (), s32[]{:S(2)}) async-start(), calls=%async_computation.7 | async-start | bytes 1327104 | tf_op jit(solution)/shard_map/all_gather | solution.py:1206
  10.3 129.3 %all-gather.14.cloned.1.call-start = ((), (), s32[]{:S(2)}) async-start(), calls=%async_computation.8 | async-start | bytes 21233664 | tf_op jit(solution)/shard_map/all_gather | solution.py:1214
  22.1 193.0 %all-gather.16.cloned.1.call-start = ((), (), s32[]{:S(2)}) async-start(), calls=%async_computation.9 | async-start | bytes 1327104 | tf_op jit(solution)/shard_map/all_gather | solution.py:1206
  23.4 254.7 %all-gather.18.cloned.1.call-start = ((), (), s32[]{:S(2)}) async-start(), calls=%async_computation.10 | async-start | bytes 21233664 | tf_op jit(solution)/shard_map/all_gather | solution.py:1214
  27.3 46.3 %copy-start.10 = (s32[2,1024,2]{1,2,0:T(2,128)S(1)}, s32[2,1024,2]{1,2,0:T(2,128)}, u32[]{:S(2)}) copy-start(s32[2,1024,2]{1,2,0:T(2,128)} %param.17) | copy-start | bytes 49156
  27.3 277.2 %all-gather.10.cloned.1.call-start = ((), (), s32[]{:S(2)}) async-start(), calls=%async_computation.4 | async-start | bytes 1966080 | tf_op jit(solution)/shard_map/all_gather | solution.py:1234
  74.0 2.2 copy-start.7
  74.7 2.6 copy-start.2
  227.6 120.8 %reduce-scatter.9.cloned.1.call-start = ((), (), s32[]{:S(2)}) async-start(), calls=%async_computation.5 | async-start | bytes 1966080 | tf_op jit(solution)/shard_map/reduce_scatter | solution.py:1248
  228.7 49.4 %copy-start.3 = (s32[1024,128]{1,0:T(8,128)}, s32[1024,128]{1,0:T(8,128)S(1)}, u32[]{:S(2)}) copy-start(s32[1024,128]{1,0:T(8,128)S(1)} %fusion.5.pos_ref) | copy-start | bytes 1572868
  304.0 206.7 %reduce-scatter.13.cloned.1.call-start = ((), (), s32[]{:S(2)}) async-start(), calls=%async_computation.11 | async-start | bytes 11796480
  348.2 231.0 %reduce-scatter.11.cloned.1.call-start = ((), (), s32[]{:S(2)}) async-start(), calls=%async_computation.6 | async-start | bytes 1327104 | tf_op jit(solution)/shard_map/reduce_scatter | solution.py:1277
  417.1 227.3 %reduce-scatter.15.cloned.1.call-start = ((), (), s32[]{:S(2)}) async-start(), calls=%async_computation.12 | async-start | bytes 11796480
  506.9 1.9 copy-start.5
  579.3 34.1 %copy-start.15 = (f32[1,768]{1,0:T(1,128)S(1)}, f32[1,768]{1,0:T(1,128)}, u32[]{:S(2)}) copy-start(f32[1,768]{1,0:T(1,128)} %get-tuple-element.130) | copy-start | bytes 9220
  579.3 34.1 %copy-start.16 = (f32[1,768]{1,0:T(1,128)S(1)}, f32[1,768]{1,0:T(1,128)}, u32[]{:S(2)}) copy-start(f32[1,768]{1,0:T(1,128)} %get-tuple-element.128) | copy-start | bytes 9220
  579.3 34.1 %copy-start.17 = (f32[1,768]{1,0:T(1,128)S(1)}, f32[1,768]{1,0:T(1,128)}, u32[]{:S(2)}) copy-start(f32[1,768]{1,0:T(1,128)} %get-tuple-element.129) | copy-start | bytes 9220
  644.4 8.1 %copy-start = (f32[2,128,768]{2,1,0:T(8,128)S(1)}, f32[2,128,768]{2,1,0:T(8,128)}, u32[]{:S(2)}) copy-start(f32[2,128,768]{2,1,0:T(8,128)} %get-tuple-element.125) | copy-start | bytes 2359300
  652.5 2.3 copy-start.6
  652.5 3.0 copy-start.20
  652.5 3.6 copy-start.12
  652.5 4.1 copy-start.11
  652.5 4.7 copy-start.18
  652.5 5.3 copy-start.14
  (9 other events, 11.0 us)
Sparse Core Ops, SparseCore 0:
  10.4 26.6 all-gather.11
  39.6 98.6 all-gather.13
  140.1 23.9 all-gather.15
  165.8 98.5 all-gather.17
  265.9 36.9 all-gather.9
  305.1 34.3 reduce-scatter.8
  348.4 94.3 reduce-scatter.12
  446.0 36.6 reduce-scatter.10
  507.0 94.3 reduce-scatter.14

commit v5 on v4

--- a/solution.py
+++ b/solution.py
@@ -21,8 +21,9 @@
 BF16 = jnp.bfloat16
 VMEM_SPEC = pl.BlockSpec(memory_space=pltpu.VMEM)
 AHEAD = 2
-PIECES = 16
-LAG = 2
+PIECES = 32
+LAG = 4
+APART = 16000
 MIX_STEP = 16
 VMEM_LIMIT = 60 * 1024 * 1024
 
@@ -193,7 +194,7 @@
     )(small, projection, above)
 
 
-def join_kernel(back, gain_row, nt, pieces, lag, *refs):
+def join_kernel(back, gain_row, nt, pieces, lag, wait, *refs):
     if back:
         part, base_ref, skip_ref, rows_ref, result_ref, gg_ref = refs[:6]
     else:
@@ -205,6 +206,11 @@
     buddy = jnp.where(me < 2, 1 - me, 5 - me)
     cross = 3 - me
 
+    if wait:
+        @pl.when(lax.rem(lax.axis_index("dp"), 2) == 1)
+        def _():
+            pl.delay(wait)
+
     barrier = pltpu.get_barrier_semaphore()
     pl.semaphore_signal(barrier, inc=1, device_id={"tensor": buddy}, device_id_type=MESH)
 
@@ -294,7 +300,7 @@
             outward(n).wait_send()
 
 
-def join(back, part, others, rows, gain_row, collective_id, pieces=PIECES, lag=LAG):
+def join(back, part, others, rows, gain_row, collective_id, wait=0, pieces=PIECES, lag=LAG):
     nt = lax.axis_size("tensor")
     seq_len, width = part.shape
     cut = (pieces, seq_len // pieces, width)
@@ -302,7 +308,7 @@
     outs.append(jax.ShapeDtypeStruct((1, width) if back else cut, F32 if back else BF16))
     sems = pltpu.SemaphoreType.DMA((pieces,))
     results = pl.pallas_call(
-        functools.partial(join_kernel, back, gain_row, nt, pieces, lag),
+        functools.partial(join_kernel, back, gain_row, nt, pieces, lag, wait),
         out_shape=outs,
         in_specs=[VMEM_SPEC] * (2 + len(others)),
         out_specs=[VMEM_SPEC] * 2,
@@ -331,6 +337,7 @@
     part = refs.pop(0) if has_sum else None
     if kind == "start":
         x_ref, small_ref = refs.pop(0), refs.pop(0)
+        proj_refs = [refs.pop(0) for _ in range(extra)]
     elif kind == "fwd":
         extra_ref, gain_ref = refs.pop(0), refs.pop(0)
     elif kind == "last":
@@ -341,7 +348,9 @@
     own_ref = refs.pop(0) if has_sum else None
     gg_ref = refs.pop(0) if kind in ("bwd", "end") else None
     all_ref = refs.pop(0) if has_gather else None
-    land_ref = refs.pop(0) if kind == "start" else None
+    if kind == "start":
+        land_ref = refs.pop(0)
+        proj_lands = [refs.pop(0) for _ in range(extra)]
     if has_sum:
         from_left, from_right, tx, acc, rs_send, rl_sem, rr_sem = refs[:7]
         refs = refs[7:]
@@ -364,8 +373,21 @@
         small_start, small_finish = swap_all(
             count, me_all, place, lambda other: small_ref, land_ref, *refs[:2]
         )
+        row = lax.axis_index("dp")
+        members = lax.axis_size("dp")
+        proj_moves = [
+            swap_all(
+                members, row, lambda other: (other, me), lambda other, ref=ref: ref, to,
+                *refs[2 + 2 * n : 4 + 2 * n],
+            )
+            for n, (ref, to) in enumerate(zip(proj_refs, proj_lands))
+        ]
         small_start()
+        for start, _ in proj_moves:
+            start()
         land_ref[me_all] = small_ref[...]
+        for ref, to in zip(proj_refs, proj_lands):
+            to[row] = ref[...]
     else:
         barrier = pltpu.get_barrier_semaphore()
 
@@ -520,6 +542,8 @@
             for d in range(1, nt):
                 pass_on(c, d)
         small_finish()
+        for _, finish in proj_moves:
+            finish()
     else:
 
         push(0, AHEAD)
@@ -572,7 +596,9 @@
     piece = rows // chunks
     split = []
     for item in args:
-        if item.shape[0] == nt * rows:
+        if item.shape[1] != width or kind == "start" and split:
+            split.append(item)
+        elif item.shape[0] == nt * rows:
             split.append(item.reshape(nt, chunks, piece, width))
         elif item.shape[0] == rows:
             split.append(item.reshape(chunks, piece, width))
@@ -588,6 +614,9 @@
     if kind == "start":
         count = lax.axis_size("dp") * nt
         outs.append(jax.ShapeDtypeStruct((count,) + args[1].shape, args[1].dtype))
+        members = lax.axis_size("dp")
+        for item in args[2:]:
+            outs.append(jax.ShapeDtypeStruct((members,) + item.shape, item.dtype))
     scratch = []
     sems = pltpu.SemaphoreType.DMA((nt, chunks))
     if has_sum:
@@ -597,6 +626,7 @@
         scratch += [sems, sems, sems]
     if kind == "start":
         scratch += [pltpu.SemaphoreType.DMA((count,))] * 2
+        scratch += [pltpu.SemaphoreType.DMA((members,))] * (2 * extra)
     results = pl.pallas_call(
         functools.partial(line_kernel, kind, nt, chunks, lag, extra),
         out_shape=outs,
@@ -1194,24 +1224,23 @@
         + [const_mix[l, :, :, k].T for l in range(layers) for k in range(2)],
         axis=1,
     )
-    x_all, small = line_exchange("start", [hidden_in, lanes(packed)], own, width, 0)
+    exp_local = [
+        jnp.concatenate(
+            [up_weight[l].reshape(EXPERTS, rows, 2 * half), jnp.swapaxes(down_weight[l], 1, 2)], axis=2
+        )
+        for l in range(layers)
+    ]
+    attn_local = [
+        jnp.concatenate([qkv_weight[l].reshape(rows, 3 * wide), out_weight[l].T], axis=1)
+        for l in range(layers)
+    ]
+    exp_w = [lax.all_gather(item, "dp", axis=0, tiled=False) for item in exp_local]
+    x_all, small, *attn_w = line_exchange(
+        "start", [hidden_in, lanes(packed)] + attn_local, own, width, 0, extra=layers
+    )
+    attn_w = [item.reshape(width, 4 * wide) for item in attn_w]
     small = small.reshape(width, LANES)
     rows_t = small[:, :48].T.astype(F32)
-
-    attn_w, exp_w = [], []
-    for l in range(layers):
-        local = jnp.concatenate(
-            [qkv_weight[l].reshape(rows, 3 * wide), out_weight[l].T], axis=1
-        )
-        attn_w.append(lax.all_gather(local, "dp", axis=0, tiled=False).reshape(width, 4 * wide))
-        local = jnp.concatenate(
-            [
-                up_weight[l].reshape(EXPERTS, rows, 2 * half),
-                jnp.swapaxes(down_weight[l], 1, 2),
-            ],
-            axis=2,
-        )
-        exp_w.append(lax.all_gather(local, "dp", axis=0, tiled=False))
 
     pos = [slot_table(routes[l]) for l in range(layers)]
     rowpos = [p[:, :EXPERTS].T[:, None, :] for p in pos]
@@ -1232,7 +1261,9 @@
         if l == layers - 1:
             partial, grad_all = lax.optimization_barrier((partial, grad_all))
             grad_all = lax.all_gather(grad_all, "tensor", axis=0, tiled=True)
-        mid, b_all = join(False, partial, [hidden], rows_t, at["moe"] + l, next_id)
+        mid, b_all = join(
+            False, partial, [hidden], rows_t, at["moe"] + l, next_id, APART if l == 0 else 0
+        )
         x, gu, z, wd, partial, extra = experts_forward(
             l, at, consts, b_all, exp_w[l], rowpos[l], pos[l], small, rows_t, mix, z_prev, mid, cap
         )
@@ -1267,7 +1298,7 @@
         else:
             partial, hidden_out = lax.optimization_barrier((partial, hidden_out))
         grad_mid, gains_m[l] = join(
-            True, partial, [s["mid"], grad_all], rows_t, at["moe"] + l, next_id
+            True, partial, [s["mid"], grad_all], rows_t, at["moe"] + l, next_id, APART
         )
         partial, gw_attn = attend_backward(
             span_starts, grad_mid, attn_w[l], s["a_all"], s["qkv"], s["o"], s["lse"], heads

time: 669 us -> 682 us (1.019)
  Pallas kernels: 604 us -> 619 us
    pallas_call x6, Pallas kernels: 292 us -> 272 us  [join(): pl.pallas_call(functools.partial(join_kernel, back, gain_row, nt, pieces,...]
    pallas_call x2, Pallas kernels: 82.9 us -> 98.4 us  [experts_backward(): pl.pallas_call(functools.partial(experts_back_kernel, cap, layer, at, con...]
    pallas_call x1, Pallas kernels: 29.2 us -> 39.7 us  [closing(): pl.pallas_call(functools.partial(closing_kernel, ndp, inner, layers, cons...]
    pallas_call x2, Pallas kernels: 75.2 us -> 83.3 us  [line_exchange(): pl.pallas_call(functools.partial(line_kernel, kind, nt, chunks, lag, extr...]
  transfers between devices with their start and end apart: 9 -> 7, of which waited for: 0 -> 1; matrix products, arithmetic and copies ran while one was open for 5% -> 3% of each run, Pallas kernels for 90% -> 90%
where the time goes in v5:
time: 682 us; the launch traced here: 679 us
  Pallas kernels  619 us (91%)
  local copies, waits for them, and re-layouts  31.2 us (5%)
  between operations  14.9 us (2%)
  other arithmetic  9.99 us (1%)
    pallas_call x6, Pallas kernels, join(): pl.pallas_call(functools.partial(join_kernel, back, gain_row, nt, pieces,...  272 us
    pallas_call x2, Pallas kernels, experts_backward(): pl.pallas_call(functools.partial(experts_back_kernel, cap, layer, at, con...  98.4 us
    pallas_call x2, Pallas kernels, line_exchange(): pl.pallas_call(functools.partial(line_kernel, kind, nt, chunks, lag, extr...  83.3 us
    pallas_call x2, Pallas kernels, experts_forward(): pl.pallas_call(functools.partial(experts_kernel, cap, layer, at, consts),...  52.3 us
    pallas_call x1, Pallas kernels, closing(): pl.pallas_call(functools.partial(closing_kernel, ndp, inner, layers, cons...  39.7 us
    pallas_call x2, Pallas kernels, attend_backward(): pl.pallas_call(functools.partial(attend_back_kernel, heads, spans, PIC),...  39.6 us
    pallas_call x2, Pallas kernels, attend_forward(): pl.pallas_call(functools.partial(attend_kernel, heads, spans, PIC, raw),...  26.3 us
  transfers between devices with their start and end apart: 7, of which 1 were waited for; matrix products, arithmetic and copies ran while one was open for 3% of the time, Pallas kernels for 90%

profile of v5, /device:TPU:0, one launch (start us, length us, event | category | flops | bytes accessed | tf_op | source)
XLA Modules:
  0.0 678.5 jit_solution(10553399424890688831)
XLA Ops:
  7.2 5.0 fusion.10
  12.2 2.8 reshape_squeeze.14
  15.0 2.4 slice_bitcast_fusion
  20.2 2.7 pad_maximum_fusion.1
  27.0 60.6 %line_start.1 = (bf16[4,2,128,768]{3,2,1,0:T(8,128)(2,1)}, bf16[32,24,128]{2,1,0:T(8,128)(2,1)}, bf16[8,96,768]{2,1,0:T(8,128)(2,1)}, bf16[8,96,768]{2,1,0:T(8,128)(2,1)}) custom-call(bf16[2,128,768]{2,1,0:T(8,128)(2,1)} %bitcast.110, bf16[24,128]{1,0:T(8,128)(2,1)} %pad.19.refs_1_, bf16[96,768]{1,0:T(8,128)(2,1)} %get-tuple-element.168.refs_2_, ...), custom_call_target="tpu_custom_call" | custom-call | flops 7864320 | bytes 78643200 | tf_op jit(solution)/shard_map/line_start/pallas_call | solution.py:630
  93.0 14.0 %attend_forward.2 = (bf16[1024,576]{1,0:T(8,128)(2,1)}, bf16[1024,192]{1,0:T(8,128)(2,1)}, f32[1024,3]{1,0:T(8,128)}, bf16[1024,768]{1,0:T(8,128)(2,1)}, bf16[1024,768]{1,0:T(8,128)(2,1)}) custom-call(s32[1,2]{1,0:T(1,128)} %starts_ref.7, bf16[1024,768]{1,0:T(8,128)(2,1)} %bitcast.103, bf16[768,768]{1,0:T(8,128)(2,1)} %bitcast.163, ...), custom_call_target="tpu_custom_call" | custom-call | flops 2013265920 | bytes 4718592 | tf_op jit(solution)/shard_map/attend_forward/pallas_call | solution.py:703
  107.0 39.9 %join.3 = (bf16[32,32,768]{2,1,0:T(8,128)(2,1)}, bf16[32,32,768]{2,1,0:T(8,128)(2,1)}) custom-call(bf16[32,32,768]{2,1,0:T(8,128)(2,1)} %bitcast.107, bf16[32,32,768]{2,1,0:T(8,128)(2,1)} %bitcast.104, f32[48,768]{1,0:T(8,128)} %convert_bitcast_fusion.refs_0_.refs_2_.rows_ref.refs_3_), custom_call_target="tpu_custom_call" | custom-call | flops 7864320 | bytes 78643200 | tf_op jit(solution)/shard_map/join/pallas_call | solution.py:310
  147.6 26.5 %experts_forward.2 = (bf16[8,256,768]{2,1,0:T(8,128)(2,1)}, bf16[8,256,1024]{2,1,0:T(8,128)(2,1)}, f32[1024,128]{1,0:T(8,128)}, f32[1024,128]{1,0:T(8,128)}, bf1...) custom-call(bf16[1024,768]{1,0:T(8,128)(2,1)} %bitcast.157, bf16[8,8,96,1536]{3,2,1,0:T(8,128)(2,1)} %bitcast.152, ...), custom_call_target="tpu_custom_call" | custom-call | flops 11274289152 | bytes 18874368 | tf_op jit(solution)/shard_map/experts_forward/pallas_call | solution.py:875
  174.2 43.6 %join.4 = (bf16[32,32,768]{2,1,0:T(8,128)(2,1)}, bf16[32,32,768]{2,1,0:T(8,128)(2,1)}) custom-call(bf16[32,32,768]{2,1,0:T(8,128)(2,1)} %bitcast.108, bf16[32,32,768]{2,1,0:T(8,128)(2,1)} %bitcast.109, f32[48,768]{1,0:T(8,128)} %convert_bitcast_fusion.refs_0_.refs_2_.rows_ref.refs_3_), custom_call_target="tpu_custom_call" | custom-call | flops 7864320 | bytes 78643200 | tf_op jit(solution)/shard_map/join/pallas_call | solution.py:310
  217.8 12.3 %attend_forward.3 = (bf16[1024,576]{1,0:T(8,128)(2,1)}, bf16[1024,192]{1,0:T(8,128)(2,1)}, f32[1024,3]{1,0:T(8,128)}, bf16[1024,768]{1,0:T(8,128)(2,1)}) custom-call(s32[1,2]{1,0:T(1,128)} %starts_ref.7, bf16[1024,768]{1,0:T(8,128)(2,1)} %bitcast.159, bf16[768,768]{1,0:T(8,128)(2,1)} %bitcast.165), custom_call_target="tpu_custom_call" | custom-call | flops 2013265920 | bytes 4718592 | tf_op jit(solution)/shard_map/attend_forward/pallas_call | solution.py:703
  232.7 69.1 %join.5 = (bf16[32,32,768]{2,1,0:T(8,128)(2,1)}, bf16[32,32,768]{2,1,0:T(8,128)(2,1)}) custom-call(bf16[32,32,768]{2,1,0:T(8,128)(2,1)} %bitcast.105, bf16[32,32,768]{2,1,0:T(8,128)(2,1)} %get-tuple-element.94.refs_1_, f32[48,768]{1,0:T(8,128)} %convert_bitcast_fusion.refs_0_.refs_2_.rows_ref.refs_3_), custom_call_target="tpu_custom_call" | custom-call | flops 7864320 | bytes 78643200 | tf_op jit(solution)/shard_map/join/pallas_call | solution.py:310
  301.9 25.8 %experts_forward.3 = (bf16[8,256,768]{2,1,0:T(8,128)(2,1)}, bf16[8,256,1024]{2,1,0:T(8,128)(2,1)}, f32[1024,128]{1,0:T(8,128)}, f32[1024,128]{1,0:T(8,128)}, bf1...) custom-call(bf16[1024,768]{1,0:T(8,128)(2,1)} %bitcast.161, bf16[8,8,96,1536]{3,2,1,0:T(8,128)(2,1)} %bitcast.154, ...), custom_call_target="tpu_custom_call" | custom-call | flops 11274289152 | bytes 18874368 | tf_op jit(solution)/shard_map/experts_forward/pallas_call | solution.py:875
  330.3 47.7 %experts_backward.2 = (bf16[4,8,96,1536]{3,2,1,0:T(8,128)(2,1)}, f32[1024,128]{1,0:T(8,128)}, bf16[1024,768]{1,0:T(8,128)(2,1)}, f32[768,128]{1,0:T(8,128)}, f32[128,128]{1,0:T(8,128)}) custom-call(bf16[1024,768]{1,0:T(8,128)(2,1)} %all-gather.6.cloned.1.call-done.g_ref, bf16[8,8,96,1536]{3,2,1,0:T(8,128)(2,1)} %bitcast.155, ...), custom_call_target="tpu_custom_call" | custom-call | flops 16106127360 | bytes 37748736 | tf_op jit(solution)/shard_map/experts_backward/pallas_call | solution.py:1084
  378.1 39.1 %join_back.3 = (bf16[32,32,768]{2,1,0:T(8,128)(2,1)}, f32[1,768]{1,0:T(1,128)}) custom-call(bf16[32,32,768]{2,1,0:T(8,128)(2,1)} %bitcast.119, bf16[32,32,768]{2,1,0:T(8,128)(2,1)} %get-tuple-element.97.refs_1_, bf16[32,32,768]{2,1,0:T(8,128)(2,1)} %bitcast.115, f32[48,768]{1,0:T(8,128)} %convert_bitcast_fusion.refs_0_.refs_2_.rows_ref.refs_3_), custom_call_target="tpu_custom_call" | custom-call | flops 7864320 | bytes 78643200 | tf_op jit(solution)/shard_map/join_back/pallas_call | solution.py:310
  417.2 19.8 %attend_backward.2 = (bf16[1024,768]{1,0:T(8,128)(2,1)}, bf16[768,768]{1,0:T(8,128)(2,1)}) custom-call(s32[1,2]{1,0:T(1,128)} %starts_ref.7, bf16[1024,768]{1,0:T(8,128)(2,1)} %bitcast.120, bf16[768,768]{1,0:T(8,128)(2,1)} %bitcast.166, bf16[1024,768]{1,0:T(8,128)(2,1)} %bitcast.160, bf16[1024,576]{1,0:T(8,128)(2,1)} %get-tuple-element.107.qkv_ref, ...), custom_call_target="tpu_custom_call" | custom-call | flops 4429185024 | bytes 9437184 | tf_op jit(solution)/shard_map/attend_backward/pallas_call | solution.py:762
  437.0 40.5 %join_back.4 = (bf16[32,32,768]{2,1,0:T(8,128)(2,1)}, f32[1,768]{1,0:T(1,128)}) custom-call(bf16[32,32,768]{2,1,0:T(8,128)(2,1)} %bitcast.121, bf16[32,32,768]{2,1,0:T(8,128)(2,1)} %get-tuple-element.94.refs_1_, bf16[32,32,768]{2,1,0:T(8,128)(2,1)} %get-tuple-element.106.refs_2_, f32[48,768]{1,0:T(8,128)} %convert_bitcast_fusion.refs_0_.refs_2_.rows_ref.refs_3_), custom_call_target="tpu_custom_call" | custom-call | flops 7864320 | bytes 78643200 | tf_op jit(solution)/shard_map/join_back/pallas_call | solution.py:310
  477.5 50.7 %experts_backward.3 = (bf16[4,8,96,1536]{3,2,1,0:T(8,128)(2,1)}, f32[1024,128]{1,0:T(8,128)}, bf16[1024,768]{1,0:T(8,128)(2,1)}, f32[768,128]{1,0:T(8,128)}, f32[128,128]{1,0:T(8,128)}) custom-call(bf16[1024,768]{1,0:T(8,128)(2,1)} %bitcast.116, bf16[8,8,96,1536]{3,2,1,0:T(8,128)(2,1)} %bitcast.153, bf16[8,256,768]{2,1,0:T(8,128)(2,1)} %get-tuple-element.112.x_ref, ...), custom_call_target="tpu_custom_call" | custom-call | flops 16106127360 | bytes 37748736 | tf_op jit(solution)/shard_map/experts_backward/pallas_call | solution.py:1084
  530.1 2.0 convert_add_fusion
  532.1 39.6 %join_back.5 = (bf16[32,32,768]{2,1,0:T(8,128)(2,1)}, f32[1,768]{1,0:T(1,128)}) custom-call(bf16[32,32,768]{2,1,0:T(8,128)(2,1)} %bitcast.118, bf16[32,32,768]{2,1,0:T(8,128)(2,1)} %get-tuple-element.86.refs_1_, bf16[32,32,768]{2,1,0:T(8,128)(2,1)} %get-tuple-element.111.refs_2_, f32[48,768]{1,0:T(8,128)} %convert_bitcast_fusion.refs_0_.refs_2_.rows_ref.refs_3_), custom_call_target="tpu_custom_call" | custom-call | flops 7864320 | bytes 78643200 | tf_op jit(solution)/shard_map/join_back/pallas_call | solution.py:310
  571.6 19.8 %attend_backward.3 = (bf16[1024,768]{1,0:T(8,128)(2,1)}, bf16[768,768]{1,0:T(8,128)(2,1)}) custom-call(s32[1,2]{1,0:T(1,128)} %starts_ref.7, bf16[1024,768]{1,0:T(8,128)(2,1)} %bitcast.135, bf16[768,768]{1,0:T(8,128)(2,1)} %bitcast.164, bf16[1024,768]{1,0:T(8,128)(2,1)} %get-tuple-element.122.a_ref, bf16[1024,576]{1,0:T(8,128)(2,1)} %get-tuple-element.123.qkv_ref, ...), custom_call_target="tpu_custom_call" | custom-call | flops 4429185024 | bytes 9437184 | tf_op jit(solution)/shard_map/attend_backward/pallas_call | solution.py:762
  591.5 1.8 constant_dynamic-slice_fusion
  593.2 22.6 %line_end.1 = (f32[2,128,768]{2,1,0:T(8,128)}, f32[1,768]{1,0:T(1,128)}) custom-call(bf16[4,2,128,768]{3,2,1,0:T(8,128)(2,1)} %bitcast.106, bf16[2,128,768]{2,1,0:T(8,128)(2,1)} %bitcast.111, bf16[2,128,768]{2,1,0:T(8,128)(2,1)} %bitcast.112, f32[48,768]{1,0:T(8,128)} %convert_bitcast_fusion.refs_0_.refs_2_.rows_ref.refs_3_), custom_call_target="tpu_custom_call" | custom-call | flops 7864320 | bytes 78643200 | tf_op jit(solution)/shard_map/line_end/pallas_call | solution.py:630
  617.7 39.7 %closing.1 = (f32[2,24]{1,0:T(2,128)}, f32[2,24]{1,0:T(2,128)}, f32[12,2,24]{2,1,0:T(2,128)}, f32[12,2,12]{2,1,0:T(2,128)}, f32[2,2,24]{2,1,0:T(2,128)}, /*index...) custom-call(f32[32,40,128]{2,1,0:T(8,128)} %pad_maximum_fusion.2.refs_0_, ...), custom_call_target="tpu_custom_call" | custom-call | tf_op jit(solution)/shard_map/closing/pallas_call | solution.py:177
  657.4 8.1 %unpack.1 = (f32[2,8,96,2,512]{4,3,2,1,0:T(2,128)}, f32[2,8,96,512]{3,2,1,0:T(8,128)}) custom-call(bf16[8,96,1536]{2,1,0:T(8,128)(2,1)} %bitcast.102, bf16[8,96,1536]{2,1,0:T(8,128)(2,1)} %bitcast.101), custom_call_target="tpu_custom_call" | custom-call | tf_op jit(solution)/shard_map/unpack/pallas_call | solution.py:1157
  (133 shorter events, 27.6 us)
Async XLA Ops:
  7.2 140.5 %all-gather.8.cloned.1.call-start = ((), (), s32[]{:S(2)}) async-start(), calls=%async_computation.7 | async-start | bytes 21233664 | tf_op jit(solution)/shard_map/all_gather | solution.py:1237
  19.0 282.8 %all-gather.10.cloned.1.call-start = ((), (), s32[]{:S(2)}) async-start(), calls=%async_computation.8 | async-start | bytes 21233664 | tf_op jit(solution)/shard_map/all_gather | solution.py:1237
  23.0 1.6 copy-start.6
  23.0 2.3 copy-start.8
  23.0 305.0 %all-gather.6.cloned.1.call-start = ((), (), s32[]{:S(2)}) async-start(), calls=%async_computation.4 | async-start | bytes 1966080 | tf_op jit(solution)/shard_map/all_gather | solution.py:1263
  24.6 64.1 %copy-start.12 = (s32[2,1024,2]{1,2,0:T(2,128)S(1)}, s32[2,1024,2]{1,2,0:T(2,128)}, u32[]{:S(2)}) copy-start(s32[2,1024,2]{1,2,0:T(2,128)} %param.17) | copy-start | bytes 49156
  89.1 2.2 copy-start.9
  89.8 2.6 copy-start.2
  230.1 148.0 %reduce-scatter.9.cloned.1.call-start = ((), (), s32[]{:S(2)}) async-start(), calls=%async_computation.5 | async-start | bytes 1966080 | tf_op jit(solution)/shard_map/reduce_scatter | solution.py:1279
  231.3 70.6 %copy-start.3 = (s32[1024,128]{1,0:T(8,128)}, s32[1024,128]{1,0:T(8,128)S(1)}, u32[]{:S(2)}) copy-start(s32[1024,128]{1,0:T(8,128)S(1)} %fusion.5.pos_ref) | copy-start | bytes 1572868
  327.7 204.3 %reduce-scatter.13.cloned.1.call-start = ((), (), s32[]{:S(2)}) async-start(), calls=%async_computation.9 | async-start | bytes 11796480
  378.0 213.4 %reduce-scatter.11.cloned.1.call-start = ((), (), s32[]{:S(2)}) async-start(), calls=%async_computation.6 | async-start | bytes 1327104 | tf_op jit(solution)/shard_map/reduce_scatter | solution.py:1308
  437.0 220.4 %reduce-scatter.15.cloned.1.call-start = ((), (), s32[]{:S(2)}) async-start(), calls=%async_computation.10 | async-start | bytes 11796480
  528.2 1.9 copy-start.5
  591.4 24.4 %copy-start.17 = (f32[1,768]{1,0:T(1,128)S(1)}, f32[1,768]{1,0:T(1,128)}, u32[]{:S(2)}) copy-start(f32[1,768]{1,0:T(1,128)} %get-tuple-element.134) | copy-start | bytes 9220
  591.4 24.4 %copy-start.18 = (f32[1,768]{1,0:T(1,128)S(1)}, f32[1,768]{1,0:T(1,128)}, u32[]{:S(2)}) copy-start(f32[1,768]{1,0:T(1,128)} %get-tuple-element.132) | copy-start | bytes 9220
  591.5 24.4 %copy-start.19 = (f32[1,768]{1,0:T(1,128)S(1)}, f32[1,768]{1,0:T(1,128)}, u32[]{:S(2)}) copy-start(f32[1,768]{1,0:T(1,128)} %get-tuple-element.133) | copy-start | bytes 9220
  657.4 8.1 %copy-start = (f32[2,128,768]{2,1,0:T(8,128)S(1)}, f32[2,128,768]{2,1,0:T(8,128)}, u32[]{:S(2)}) copy-start(f32[2,128,768]{2,1,0:T(8,128)} %get-tuple-element.129) | copy-start | bytes 2359300
  665.5 2.3 copy-start.7
  665.5 3.0 copy-start.22
  665.5 3.6 copy-start.14
  665.5 4.1 copy-start.13
  665.5 4.7 copy-start.20
  665.5 5.3 copy-start.16
  (9 other events, 11.0 us)
Sparse Core Ops, SparseCore 0:
  19.2 128.4 all-gather.7
  149.5 98.5 all-gather.9
  249.7 48.7 all-gather.5
  327.8 40.2 reduce-scatter.8
  378.2 93.2 reduce-scatter.12
  474.5 36.6 reduce-scatter.10
  528.4 93.7 reduce-scatter.14

commit v6 on v4

--- a/solution.py
+++ b/solution.py
@@ -21,8 +21,8 @@
 BF16 = jnp.bfloat16
 VMEM_SPEC = pl.BlockSpec(memory_space=pltpu.VMEM)
 AHEAD = 2
-PIECES = 16
-LAG = 2
+PIECES = 32
+LAG = 4
 MIX_STEP = 16
 VMEM_LIMIT = 60 * 1024 * 1024
 
@@ -100,10 +100,10 @@
 
 
 def closing_kernel(ndp, inner, layers, consts, wide, *refs):
-    small_ref, proj_ref, above_ref = refs[:3]
+    small_ref, first_ref, above_ref = refs[:3]
     attn_out, moe_out, router_out, mix_out, cvec_out, cmix_out, qkv_out, outw_out = refs[3:11]
-    land, proj_land, square, tall = refs[11:15]
-    sems = refs[15:]
+    land, square, tall = refs[11:14]
+    sems = refs[14:]
     count = ndp * inner
     row, col = lax.axis_index("dp"), lax.axis_index("tensor")
     me = row * inner + col
@@ -113,21 +113,10 @@
     def anywhere(other):
         return (lax.div(other, inner), lax.rem(other, inner))
 
-    def along(other):
-        return (other, col)
-
-    def piece(ref):
-        return lambda other: ref.at[other]
-
     greet_all(count, me, anywhere)
-    moves = [
-        swap_all(ndp, row, along, piece(proj_ref), proj_land, *sems[2:4]),
-        swap_all(count, me, anywhere, piece(small_ref), land, *sems[0:2]),
-    ]
-    for start, _ in moves:
-        start()
+    start, finish = swap_all(count, me, anywhere, lambda other: small_ref.at[other], land, *sems)
+    start()
     land[me] = small_ref[me]
-    proj_land[row] = proj_ref[row]
     square[...] = jnp.zeros_like(square)
     tall[...] = jnp.zeros_like(tall)
 
@@ -139,9 +128,8 @@
 
     for l in range(1, layers):
         place(l, above_ref[l - 1].astype(F32))
-    moves[0][1]()
-    place(0, jnp.sum(proj_land[...].astype(F32), axis=0))
-    moves[1][1]()
+    place(0, first_ref[...])
+    finish()
     total = jnp.sum(land[...], axis=0)
     square[:cols, :] = total[:cols]
     turned = square[...].T
@@ -166,7 +154,7 @@
 
 def closing(small, projection, above, consts, layers, cols, collective_id):
     inner, ndp = lax.axis_size("tensor"), lax.axis_size("dp")
-    rows, packed = projection.shape[1:]
+    rows, packed = projection.shape
     wide = packed // 4
     shapes = [
         (layers, cols), (layers, cols), (NEXP, layers, cols), (NEXP, layers, NEXP),
@@ -180,12 +168,10 @@
         out_specs=[VMEM_SPEC] * len(shapes),
         scratch_shapes=[
             pltpu.VMEM(small.shape, F32),
-            pltpu.VMEM(projection.shape, BF16),
             pltpu.VMEM((-(-cols // LANES) * LANES, LANES), F32),
             pltpu.VMEM((-(-rows // LANES) * LANES, -(-wide // LANES) * LANES), F32),
         ]
-        + [pltpu.SemaphoreType.DMA((ndp * inner,))] * 2
-        + [pltpu.SemaphoreType.DMA((ndp,))] * 2,
+        + [pltpu.SemaphoreType.DMA((ndp * inner,))] * 2,
         compiler_params=pltpu.CompilerParams(
             collective_id=collective_id, has_side_effects=True, vmem_limit_bytes=VMEM_LIMIT
         ),
@@ -338,13 +324,16 @@
     else:
         extra_ref = refs.pop(0) if extra else None
         base_ref, skip_ref, rows_ref = refs.pop(0), refs.pop(0), refs.pop(0)
+        proj_ref = refs.pop(0)
     own_ref = refs.pop(0) if has_sum else None
     gg_ref = refs.pop(0) if kind in ("bwd", "end") else None
+    proj_out = refs.pop(0) if kind == "end" else None
     all_ref = refs.pop(0) if has_gather else None
     land_ref = refs.pop(0) if kind == "start" else None
     if has_sum:
         from_left, from_right, tx, acc, rs_send, rl_sem, rr_sem = refs[:7]
-        refs = refs[7:]
+        proj_land, proj_send, proj_recv = refs[7:10]
+        refs = refs[10:]
     if has_gather:
         ag_right, ag_left, ag_recv = refs[:3]
         refs = refs[3:]
@@ -368,6 +357,7 @@
         land_ref[me_all] = small_ref[...]
     else:
         barrier = pltpu.get_barrier_semaphore()
+        members, row = lax.axis_size("dp"), lax.axis_index("dp")
 
         @pl.when(has_l)
         def _():
@@ -377,7 +367,19 @@
         def _():
             pl.semaphore_signal(barrier, inc=1, device_id={"tensor": right}, device_id_type=MESH)
 
-        pl.semaphore_wait(barrier, has_l.astype(jnp.int32) + has_r.astype(jnp.int32))
+        def greet(step, carry):
+            other = lax.rem(row + step, members)
+            pl.semaphore_signal(barrier, inc=1, device_id={"dp": other}, device_id_type=MESH)
+            return carry
+
+        lax.fori_loop(1, members, greet, 0)
+        pl.semaphore_wait(
+            barrier, members - 1 + has_l.astype(jnp.int32) + has_r.astype(jnp.int32)
+        )
+        proj_start, proj_finish = swap_all(
+            members, row, lambda other: (other, me), lambda other: proj_ref.at[other], proj_land,
+            proj_send, proj_recv,
+        )
 
     def copy(src, dst, send_sem, recv_sem, to):
         return pltpu.make_async_remote_copy(
@@ -500,7 +502,7 @@
             unit = base * scale
             grad_unit = total * rows_ref[0:1, :]
             below = scale * (grad_unit - unit * jnp.mean(grad_unit * unit, axis=-1, keepdims=True))
-            result = below + skip_ref[c].astype(F32)
+            result = below + skip_ref[me, c].astype(F32)
             if has_gather:
                 all_ref[me, c] = result.astype(BF16)
             own_ref[c] = result
@@ -523,6 +525,8 @@
     else:
 
         push(0, AHEAD)
+        proj_start()
+        proj_land[row] = proj_ref[row]
         if kind == "last":
             for c in range(chunks):
                 all_ref[me, c] = og_ref[c]
@@ -542,6 +546,10 @@
             if step % hops == 0 and 0 <= step // hops - lag < chunks:
                 own_rows(step // hops - lag)
 
+    if kind == "end":
+        proj_finish()
+        proj_out[...] = jnp.sum(proj_land[...].astype(F32), axis=0)
+
     for c in range(chunks):
         for j in range(nt):
             if has_sum:
@@ -583,6 +591,7 @@
         outs.append(jax.ShapeDtypeStruct((chunks, piece, width), F32))
     if kind in ("bwd", "end"):
         outs.append(jax.ShapeDtypeStruct((1, width), F32))
+        outs.append(jax.ShapeDtypeStruct(args[-1].shape[1:], F32))
     if has_gather:
         outs.append(jax.ShapeDtypeStruct((nt, chunks, piece, width), BF16))
     if kind == "start":
@@ -593,6 +602,8 @@
     if has_sum:
         buf = pltpu.VMEM((nt, chunks, piece, width), BF16)
         scratch += [buf, buf, buf, pltpu.VMEM((piece, width), F32), sems, sems, sems]
+        scratch.append(pltpu.VMEM(args[-1].shape, args[-1].dtype))
+        scratch += [pltpu.SemaphoreType.DMA((lax.axis_size("dp"),))] * 2
     if has_gather:
         scratch += [sems, sems, sems]
     if kind == "start":
@@ -1280,9 +1291,8 @@
             )
         else:
             partial, attn_grads[1:] = lax.optimization_barrier((partial, attn_grads[1:]))
-            skip = lax.dynamic_slice_in_dim(grad_mid, offset, own, 0)
-            grad, gains_a[l] = line_exchange(
-                "end", [partial, hidden_in, skip, rows_t], own, width, next_id + 1
+            grad, gains_a[l], attn_grads[l] = line_exchange(
+                "end", [partial, hidden_in, grad_mid, rows_t, attn_grads[l]], own, width, next_id + 1
             )
         next_id += 3
     hidden_out = hidden_out.astype(F32) + extra.astype(F32)

time: 669 us -> 662 us (0.990)
    pallas_call x1, Pallas kernels: 29.2 us -> 21.2 us  [closing(): pl.pallas_call(functools.partial(closing_kernel, ndp, inner, layers, cons...]
where the time goes in v6:
time: 662 us; the launch traced here: 658 us
  Pallas kernels  599 us (90%)
  local copies, waits for them, and re-layouts  30.8 us (5%)
  between operations  14.6 us (2%)
  other arithmetic  10.7 us (2%)
    pallas_call x6, Pallas kernels, join(): pl.pallas_call(functools.partial(join_kernel, back, gain_row, nt, pieces,...  291 us
    pallas_call x2, Pallas kernels, experts_backward(): pl.pallas_call(functools.partial(experts_back_kernel, cap, layer, at, con...  82.7 us
    pallas_call x2, Pallas kernels, line_exchange(): pl.pallas_call(functools.partial(line_kernel, kind, nt, chunks, lag, extr...  79.2 us
    pallas_call x2, Pallas kernels, experts_forward(): pl.pallas_call(functools.partial(experts_kernel, cap, layer, at, consts),...  51.9 us
    pallas_call x2, Pallas kernels, attend_backward(): pl.pallas_call(functools.partial(attend_back_kernel, heads, spans, PIC),...  39.4 us
    pallas_call x2, Pallas kernels, attend_forward(): pl.pallas_call(functools.partial(attend_kernel, heads, spans, PIC, raw),...  25.5 us
    pallas_call x1, Pallas kernels, closing(): pl.pallas_call(functools.partial(closing_kernel, ndp, inner, layers, cons...  21.2 us
  transfers between devices with their start and end apart: 9, of which 0 were waited for; matrix products, arithmetic and copies ran while one was open for 5% of the time, Pallas kernels for 90%

profile of v6, /device:TPU:0, one launch (start us, length us, event | category | flops | bytes accessed | tf_op | source)
XLA Modules:
  0.0 657.7 jit_solution(16263220881614608883)
XLA Ops:
  10.3 5.0 fusion.10
  15.3 2.8 reshape_squeeze.13
  18.1 2.4 slice_bitcast_fusion
  20.5 1.6 pad_maximum_fusion
  24.6 2.7 pad_maximum_fusion.1
  29.6 43.0 %line_start.1 = (bf16[4,2,128,768]{3,2,1,0:T(8,128)(2,1)}, bf16[32,24,128]{2,1,0:T(8,128)(2,1)}) custom-call(bf16[2,128,768]{2,1,0:T(8,128)(2,1)} %bitcast.107, bf16[24,128]{1,0:T(8,128)(2,1)} %pad.19.refs_1_), custom_call_target="tpu_custom_call" | custom-call | flops 7864320 | bytes 78643200 | tf_op jit(solution)/shard_map/line_start/pallas_call | solution.py:611
  78.0 13.2 %attend_forward.2 = (bf16[1024,576]{1,0:T(8,128)(2,1)}, bf16[1024,192]{1,0:T(8,128)(2,1)}, f32[1024,3]{1,0:T(8,128)}, bf16[1024,768]{1,0:T(8,128)(2,1)}, bf16[1024,768]{1,0:T(8,128)(2,1)}) custom-call(s32[1,2]{1,0:T(1,128)} %starts_ref.7, bf16[1024,768]{1,0:T(8,128)(2,1)} %bitcast.101, bf16[768,768]{1,0:T(8,128)(2,1)} %all-gather.12.cloned.1.call-done.w_ref, ...), custom_call_target="tpu_custom_call" | custom-call | flops 2013265920 | bytes 4718592 | tf_op jit(solution)/shard_map/attend_forward/pallas_call | solution.py:684
  91.1 48.2 %join.3 = (bf16[32,32,768]{2,1,0:T(8,128)(2,1)}, bf16[32,32,768]{2,1,0:T(8,128)(2,1)}) custom-call(bf16[32,32,768]{2,1,0:T(8,128)(2,1)} %bitcast.104, bf16[32,32,768]{2,1,0:T(8,128)(2,1)} %bitcast.102, f32[48,768]{1,0:T(8,128)} %convert_bitcast_fusion.refs_0_.refs_2_.rows_ref.refs_3_), custom_call_target="tpu_custom_call" | custom-call | flops 7864320 | bytes 78643200 | tf_op jit(solution)/shard_map/join/pallas_call | solution.py:290
  139.4 26.1 %experts_forward.2 = (bf16[8,256,768]{2,1,0:T(8,128)(2,1)}, bf16[8,256,1024]{2,1,0:T(8,128)(2,1)}, f32[1024,128]{1,0:T(8,128)}, f32[1024,128]{1,0:T(8,128)}, bf1...) custom-call(bf16[1024,768]{1,0:T(8,128)(2,1)} %bitcast.154, bf16[8,8,96,1536]{3,2,1,0:T(8,128)(2,1)} %bitcast.149, ...), custom_call_target="tpu_custom_call" | custom-call | flops 11274289152 | bytes 18874368 | tf_op jit(solution)/shard_map/experts_forward/pallas_call | solution.py:856
  165.5 48.9 %join.4 = (bf16[32,32,768]{2,1,0:T(8,128)(2,1)}, bf16[32,32,768]{2,1,0:T(8,128)(2,1)}) custom-call(bf16[32,32,768]{2,1,0:T(8,128)(2,1)} %bitcast.105, bf16[32,32,768]{2,1,0:T(8,128)(2,1)} %bitcast.106, f32[48,768]{1,0:T(8,128)} %convert_bitcast_fusion.refs_0_.refs_2_.rows_ref.refs_3_), custom_call_target="tpu_custom_call" | custom-call | flops 7864320 | bytes 78643200 | tf_op jit(solution)/shard_map/join/pallas_call | solution.py:290
  214.4 12.3 %attend_forward.3 = (bf16[1024,576]{1,0:T(8,128)(2,1)}, bf16[1024,192]{1,0:T(8,128)(2,1)}, f32[1024,3]{1,0:T(8,128)}, bf16[1024,768]{1,0:T(8,128)(2,1)}) custom-call(s32[1,2]{1,0:T(1,128)} %starts_ref.7, bf16[1024,768]{1,0:T(8,128)(2,1)} %bitcast.156, bf16[768,768]{1,0:T(8,128)(2,1)} %all-gather.16.cloned.1.call-done.w_ref), custom_call_target="tpu_custom_call" | custom-call | flops 2013265920 | bytes 4718592 | tf_op jit(solution)/shard_map/attend_forward/pallas_call | solution.py:684
  229.4 48.2 %join.5 = (bf16[32,32,768]{2,1,0:T(8,128)(2,1)}, bf16[32,32,768]{2,1,0:T(8,128)(2,1)}) custom-call(bf16[32,32,768]{2,1,0:T(8,128)(2,1)} %bitcast.103, bf16[32,32,768]{2,1,0:T(8,128)(2,1)} %get-tuple-element.91.refs_1_, f32[48,768]{1,0:T(8,128)} %convert_bitcast_fusion.refs_0_.refs_2_.rows_ref.refs_3_), custom_call_target="tpu_custom_call" | custom-call | flops 7864320 | bytes 78643200 | tf_op jit(solution)/shard_map/join/pallas_call | solution.py:290
  277.6 25.8 %experts_forward.3 = (bf16[8,256,768]{2,1,0:T(8,128)(2,1)}, bf16[8,256,1024]{2,1,0:T(8,128)(2,1)}, f32[1024,128]{1,0:T(8,128)}, f32[1024,128]{1,0:T(8,128)}, bf1...) custom-call(bf16[1024,768]{1,0:T(8,128)(2,1)} %bitcast.158, bf16[8,8,96,1536]{3,2,1,0:T(8,128)(2,1)} %bitcast.151, ...), custom_call_target="tpu_custom_call" | custom-call | flops 11274289152 | bytes 18874368 | tf_op jit(solution)/shard_map/experts_forward/pallas_call | solution.py:856
  306.3 41.2 %experts_backward.2 = (bf16[4,8,96,1536]{3,2,1,0:T(8,128)(2,1)}, f32[1024,128]{1,0:T(8,128)}, bf16[1024,768]{1,0:T(8,128)(2,1)}, f32[768,128]{1,0:T(8,128)}, f32[128,128]{1,0:T(8,128)}) custom-call(bf16[1024,768]{1,0:T(8,128)(2,1)} %all-gather.10.cloned.1.call-done.g_ref, bf16[8,8,96,1536]{3,2,1,0:T(8,128)(2,1)} %bitcast.152, ...), custom_call_target="tpu_custom_call" | custom-call | flops 16106127360 | bytes 37748736 | tf_op jit(solution)/shard_map/experts_backward/pallas_call | solution.py:1065
  347.6 48.7 %join_back.3 = (bf16[32,32,768]{2,1,0:T(8,128)(2,1)}, f32[1,768]{1,0:T(1,128)}) custom-call(bf16[32,32,768]{2,1,0:T(8,128)(2,1)} %bitcast.115, bf16[32,32,768]{2,1,0:T(8,128)(2,1)} %get-tuple-element.94.refs_1_, bf16[32,32,768]{2,1,0:T(8,128)(2,1)} %bitcast.111, f32[48,768]{1,0:T(8,128)} %convert_bitcast_fusion.refs_0_.refs_2_.rows_ref.refs_3_), custom_call_target="tpu_custom_call" | custom-call | flops 7864320 | bytes 78643200 | tf_op jit(solution)/shard_map/join_back/pallas_call | solution.py:290
  396.4 19.8 %attend_backward.2 = (bf16[1024,768]{1,0:T(8,128)(2,1)}, bf16[768,768]{1,0:T(8,128)(2,1)}) custom-call(s32[1,2]{1,0:T(1,128)} %starts_ref.7, bf16[1024,768]{1,0:T(8,128)(2,1)} %bitcast.116, bf16[768,768]{1,0:T(8,128)(2,1)} %all-gather.16.cloned.1.call-done.w_ref, bf16[1024,768]{1,0:T(8,128)(2,1)} %bitcast.157, bf16[1024,576]{1,0:T(8,128)(2,1)} %get-tuple-element.104.qkv_ref, ...), custom_call_target="tpu_custom_call" | custom-call | flops 4429185024 | bytes 9437184 | tf_op jit(solution)/shard_map/attend_backward/pallas_call | solution.py:743
  416.2 47.7 %join_back.4 = (bf16[32,32,768]{2,1,0:T(8,128)(2,1)}, f32[1,768]{1,0:T(1,128)}) custom-call(bf16[32,32,768]{2,1,0:T(8,128)(2,1)} %bitcast.119, bf16[32,32,768]{2,1,0:T(8,128)(2,1)} %get-tuple-element.91.refs_1_, bf16[32,32,768]{2,1,0:T(8,128)(2,1)} %get-tuple-element.103.refs_2_, f32[48,768]{1,0:T(8,128)} %convert_bitcast_fusion.refs_0_.refs_2_.rows_ref.refs_3_), custom_call_target="tpu_custom_call" | custom-call | flops 7864320 | bytes 78643200 | tf_op jit(solution)/shard_map/join_back/pallas_call | solution.py:290
  463.9 41.5 %experts_backward.3 = (bf16[4,8,96,1536]{3,2,1,0:T(8,128)(2,1)}, f32[1024,128]{1,0:T(8,128)}, bf16[1024,768]{1,0:T(8,128)(2,1)}, f32[768,128]{1,0:T(8,128)}, f32[128,128]{1,0:T(8,128)}) custom-call(bf16[1024,768]{1,0:T(8,128)(2,1)} %bitcast.112, bf16[8,8,96,1536]{3,2,1,0:T(8,128)(2,1)} %bitcast.150, bf16[8,256,768]{2,1,0:T(8,128)(2,1)} %get-tuple-element.109.x_ref, ...), custom_call_target="tpu_custom_call" | custom-call | flops 16106127360 | bytes 37748736 | tf_op jit(solution)/shard_map/experts_backward/pallas_call | solution.py:1065
  507.2 2.0 convert_add_fusion
  509.2 48.8 %join_back.5 = (bf16[32,32,768]{2,1,0:T(8,128)(2,1)}, f32[1,768]{1,0:T(1,128)}) custom-call(bf16[32,32,768]{2,1,0:T(8,128)(2,1)} %bitcast.114, bf16[32,32,768]{2,1,0:T(8,128)(2,1)} %get-tuple-element.84.refs_1_, bf16[32,32,768]{2,1,0:T(8,128)(2,1)} %get-tuple-element.108.refs_2_, f32[48,768]{1,0:T(8,128)} %convert_bitcast_fusion.refs_0_.refs_2_.rows_ref.refs_3_), custom_call_target="tpu_custom_call" | custom-call | flops 7864320 | bytes 78643200 | tf_op jit(solution)/shard_map/join_back/pallas_call | solution.py:290
  558.0 19.6 %attend_backward.3 = (bf16[1024,768]{1,0:T(8,128)(2,1)}, bf16[768,768]{1,0:T(8,128)(2,1)}) custom-call(s32[1,2]{1,0:T(1,128)} %starts_ref.7, bf16[1024,768]{1,0:T(8,128)(2,1)} %bitcast.117, bf16[768,768]{1,0:T(8,128)(2,1)} %all-gather.12.cloned.1.call-done.w_ref, bf16[1024,768]{1,0:T(8,128)(2,1)} %get-tuple-element.119.a_ref, ...), custom_call_target="tpu_custom_call" | custom-call | flops 4429185024 | bytes 9437184 | tf_op jit(solution)/shard_map/attend_backward/pallas_call | solution.py:743
  577.6 36.2 %line_end.1 = (f32[2,128,768]{2,1,0:T(8,128)}, f32[1,768]{1,0:T(1,128)}, f32[96,768]{1,0:T(8,128)}) custom-call(bf16[4,2,128,768]{3,2,1,0:T(8,128)(2,1)} %bitcast.120, bf16[2,128,768]{2,1,0:T(8,128)(2,1)} %bitcast.108, bf16[4,2,128,768]{3,2,1,0:T(8,128)(2,1)} %bitcast.118, f32[48,768]{1,0:T(8,128)} %convert_bitcast_fusion.refs_0_.refs_2_.rows_ref.refs_3_, ...), custom_call_target="tpu_custom_call" | custom-call | flops 7864320 | bytes 78643200 | tf_op jit(solution)/shard_map/line_end/pallas_call | solution.py:611
  615.7 21.2 %closing.1 = (f32[2,24]{1,0:T(2,128)}, f32[2,24]{1,0:T(2,128)}, f32[12,2,24]{2,1,0:T(2,128)}, f32[12,2,12]{2,1,0:T(2,128)}, f32[2,2,24]{2,1,0:T(2,128)}, /*index...) custom-call(f32[32,40,128]{2,1,0:T(8,128)} %pad_maximum_fusion.2.refs_0_, ...), custom_call_target="tpu_custom_call" | custom-call | tf_op jit(solution)/shard_map/closing/pallas_call | solution.py:164
  636.9 8.1 %unpack.1 = (f32[2,8,96,2,512]{4,3,2,1,0:T(2,128)}, f32[2,8,96,512]{3,2,1,0:T(8,128)}) custom-call(bf16[8,96,1536]{2,1,0:T(8,128)(2,1)} %bitcast.100, bf16[8,96,1536]{2,1,0:T(8,128)(2,1)} %bitcast.99), custom_call_target="tpu_custom_call" | custom-call | tf_op jit(solution)/shard_map/unpack/pallas_call | solution.py:1138
  (135 shorter events, 28.2 us)
Async XLA Ops:
  7.2 70.8 %all-gather.12.cloned.1.call-start = ((), (), s32[]{:S(2)}) async-start(), calls=%async_computation.7 | async-start | bytes 1327104 | tf_op jit(solution)/shard_map/all_gather | solution.py:1217
  10.3 129.1 %all-gather.14.cloned.1.call-start = ((), (), s32[]{:S(2)}) async-start(), calls=%async_computation.8 | async-start | bytes 21233664 | tf_op jit(solution)/shard_map/all_gather | solution.py:1225
  22.1 192.3 %all-gather.16.cloned.1.call-start = ((), (), s32[]{:S(2)}) async-start(), calls=%async_computation.9 | async-start | bytes 1327104 | tf_op jit(solution)/shard_map/all_gather | solution.py:1217
  23.4 254.2 %all-gather.18.cloned.1.call-start = ((), (), s32[]{:S(2)}) async-start(), calls=%async_computation.10 | async-start | bytes 21233664 | tf_op jit(solution)/shard_map/all_gather | solution.py:1225
  27.3 46.3 %copy-start.10 = (s32[2,1024,2]{1,2,0:T(2,128)S(1)}, s32[2,1024,2]{1,2,0:T(2,128)}, u32[]{:S(2)}) copy-start(s32[2,1024,2]{1,2,0:T(2,128)} %param.17) | copy-start | bytes 49156
  27.3 276.7 %all-gather.10.cloned.1.call-start = ((), (), s32[]{:S(2)}) async-start(), calls=%async_computation.4 | async-start | bytes 1966080 | tf_op jit(solution)/shard_map/all_gather | solution.py:1245
  74.0 2.2 copy-start.7
  74.7 2.6 copy-start.2
  226.8 120.8 %reduce-scatter.9.cloned.1.call-start = ((), (), s32[]{:S(2)}) async-start(), calls=%async_computation.5 | async-start | bytes 1966080 | tf_op jit(solution)/shard_map/reduce_scatter | solution.py:1259
  227.9 49.7 %copy-start.3 = (s32[1024,128]{1,0:T(8,128)}, s32[1024,128]{1,0:T(8,128)S(1)}, u32[]{:S(2)}) copy-start(s32[1024,128]{1,0:T(8,128)S(1)} %fusion.5.pos_ref) | copy-start | bytes 1572868
  303.5 205.7 %reduce-scatter.13.cloned.1.call-start = ((), (), s32[]{:S(2)}) async-start(), calls=%async_computation.11 | async-start | bytes 11796480
  347.5 230.0 %reduce-scatter.11.cloned.1.call-start = ((), (), s32[]{:S(2)}) async-start(), calls=%async_computation.6 | async-start | bytes 1327104 | tf_op jit(solution)/shard_map/reduce_scatter | solution.py:1288
  416.2 220.7 %reduce-scatter.15.cloned.1.call-start = ((), (), s32[]{:S(2)}) async-start(), calls=%async_computation.12 | async-start | bytes 11796480
  505.4 1.9 copy-start.5
  577.6 36.3 %copy-start.15 = (f32[1,768]{1,0:T(1,128)S(1)}, f32[1,768]{1,0:T(1,128)}, u32[]{:S(2)}) copy-start(f32[1,768]{1,0:T(1,128)} %get-tuple-element.132) | copy-start | bytes 9220
  577.6 36.3 %copy-start.16 = (f32[1,768]{1,0:T(1,128)S(1)}, f32[1,768]{1,0:T(1,128)}, u32[]{:S(2)}) copy-start(f32[1,768]{1,0:T(1,128)} %get-tuple-element.130) | copy-start | bytes 9220
  577.6 36.3 %copy-start.17 = (f32[1,768]{1,0:T(1,128)S(1)}, f32[1,768]{1,0:T(1,128)}, u32[]{:S(2)}) copy-start(f32[1,768]{1,0:T(1,128)} %get-tuple-element.131) | copy-start | bytes 9220
  636.9 8.1 %copy-start = (f32[2,128,768]{2,1,0:T(8,128)S(1)}, f32[2,128,768]{2,1,0:T(8,128)}, u32[]{:S(2)}) copy-start(f32[2,128,768]{2,1,0:T(8,128)} %get-tuple-element.127) | copy-start | bytes 2359300
  645.0 2.3 copy-start.6
  645.0 3.0 copy-start.20
  645.0 3.6 copy-start.12
  645.1 4.1 copy-start.11
  645.1 4.7 copy-start.18
  645.1 5.3 copy-start.14
  (9 other events, 11.0 us)
Sparse Core Ops, SparseCore 0:
  10.4 26.6 all-gather.11
  39.6 98.6 all-gather.13
  140.2 23.8 all-gather.15
  165.9 98.6 all-gather.17
  265.9 36.9 all-gather.9
  305.1 34.2 reduce-scatter.8
  347.7 94.2 reduce-scatter.12
  445.2 36.6 reduce-scatter.10
  505.5 106.9 reduce-scatter.14

commit v7 on v6

--- a/solution.py
+++ b/solution.py
@@ -23,6 +23,7 @@
 AHEAD = 2
 PIECES = 32
 LAG = 4
+APART = 16000
 MIX_STEP = 16
 VMEM_LIMIT = 60 * 1024 * 1024
 
@@ -130,7 +131,7 @@
         place(l, above_ref[l - 1].astype(F32))
     place(0, first_ref[...])
     finish()
-    total = jnp.sum(land[...], axis=0)
+    total = jnp.sum(land[...].astype(F32), axis=0)
     square[:cols, :] = total[:cols]
     turned = square[...].T
     at = layout(layers, consts)
@@ -167,7 +168,7 @@
         in_specs=[VMEM_SPEC] * 3,
         out_specs=[VMEM_SPEC] * len(shapes),
         scratch_shapes=[
-            pltpu.VMEM(small.shape, F32),
+            pltpu.VMEM(small.shape, BF16),
             pltpu.VMEM((-(-cols // LANES) * LANES, LANES), F32),
             pltpu.VMEM((-(-rows // LANES) * LANES, -(-wide // LANES) * LANES), F32),
         ]
@@ -179,7 +180,7 @@
     )(small, projection, above)
 
 
-def join_kernel(back, gain_row, nt, pieces, lag, *refs):
+def join_kernel(back, gain_row, nt, pieces, lag, wait, *refs):
     if back:
         part, base_ref, skip_ref, rows_ref, result_ref, gg_ref = refs[:6]
     else:
@@ -191,6 +192,11 @@
     buddy = jnp.where(me < 2, 1 - me, 5 - me)
     cross = 3 - me
 
+    if wait:
+        @pl.when(lax.rem(lax.axis_index("dp"), 2) == 1)
+        def _():
+            pl.delay(wait)
+
     barrier = pltpu.get_barrier_semaphore()
     pl.semaphore_signal(barrier, inc=1, device_id={"tensor": buddy}, device_id_type=MESH)
 
@@ -280,7 +286,7 @@
             outward(n).wait_send()
 
 
-def join(back, part, others, rows, gain_row, collective_id, pieces=PIECES, lag=LAG):
+def join(back, part, others, rows, gain_row, collective_id, wait=0, pieces=PIECES, lag=LAG):
     nt = lax.axis_size("tensor")
     seq_len, width = part.shape
     cut = (pieces, seq_len // pieces, width)
@@ -288,7 +294,7 @@
     outs.append(jax.ShapeDtypeStruct((1, width) if back else cut, F32 if back else BF16))
     sems = pltpu.SemaphoreType.DMA((pieces,))
     results = pl.pallas_call(
-        functools.partial(join_kernel, back, gain_row, nt, pieces, lag),
+        functools.partial(join_kernel, back, gain_row, nt, pieces, lag, wait),
         out_shape=outs,
         in_specs=[VMEM_SPEC] * (2 + len(others)),
         out_specs=[VMEM_SPEC] * 2,
@@ -898,11 +904,14 @@
 
 
 def experts_back_kernel(
-    cap, layer, at, consts, own, g_ref, w_ref, x_ref, gu_ref, rowpos_ref, pos_ref, wd_ref,
-    b_ref, small_ref, rows_ref, mix_ref, zprev_ref, gprev_ref, sums_ref, mixes_ref,
-    gw_ref, below_ref, gb_ref, sums_out, mixes_out, pick_scr, gx_scr, gg_scr, gb_scr, zs_scr,
-    halves, inbox, out_sems, in_sems,
+    cap, layer, at, consts, own, top, g_ref, w_ref, x_ref, gu_ref, rowpos_ref, pos_ref, wd_ref,
+    b_ref, small_ref, rows_ref, mix_ref, zprev_ref, *refs,
 ):
+    gprev_ref, sums_ref, mixes_ref = (None,) * 3 if top else refs[:3]
+    (
+        gw_ref, below_ref, gb_ref, sums_out, mixes_out, pick_scr, gx_scr, gg_scr, gb_scr, zs_scr,
+        halves, inbox, out_sems, in_sems,
+    ) = refs[0 if top else 3 :]
     e = pl.program_id(0)
     last = pl.num_programs(0) - 1
     me = lax.axis_index("dp")
@@ -1020,13 +1029,16 @@
     zs_scr[mine, :] += gw_own
     gw = zs_scr[...]
     wd = wd_ref[...]
-    gz = wd * (gw - jnp.sum(wd * gw, axis=1, keepdims=True)) + gprev_ref[...]
+    gz = wd * (gw - jnp.sum(wd * gw, axis=1, keepdims=True))
+    if gprev_ref is not None:
+        gz = gz + gprev_ref[...]
     z_high, z_low = two_parts(gz)
     below_ref[...] = dot_nt(z_high, mix_ref[...]) + dot_nt(z_low, mix_ref[...])
     p_high, p_low = two_parts(zprev_ref[...])
-    mixes_out[...] = mixes_ref[...] + shift(
+    mixed = shift(
         dot_tn(p_high, z_high) + dot_tn(p_high, z_low) + dot_tn(p_low, z_high), layer * MIX_STEP
     )
+    mixes_out[...] = mixed if mixes_ref is None else mixes_ref[...] + mixed
     zs_scr[...] = shift(gz, at["router"] + layer * NEXP)
     up = at["cmix"] + layer * 2 * consts - EXPERTS - 2
     zs_scr[mine, :] += shift(gt0, up) + shift(gt1, up + consts)
@@ -1043,7 +1055,7 @@
     )
     g_low = g_ref[mine, :]
     sums_out[...] = (
-        sums_ref[...]
+        (0.0 if sums_ref is None else sums_ref[...])
         + dot_tn(b_ref[...], z_high)
         + dot_tn(b_ref[...], z_low)
         + dot_tn(g_low, i_high)
@@ -1053,7 +1065,7 @@
 
 def experts_backward(
     collective_id, layer, at, consts, own, g_all, w_exp, x, gu, rowpos, pos, wd, b_all, small, rows_t, mix,
-    z_prev, grad_prev, sums, mixes, cap,
+    z_prev, above, cap,
 ):
     seq_len, width = g_all.shape
     shards_dp, count, rows, wide3 = w_exp.shape
@@ -1063,7 +1075,7 @@
     )
     half_shape = (shards_dp // 2, 1, rows, wide3)
     return pl.pallas_call(
-        functools.partial(experts_back_kernel, cap, layer, at, consts, own),
+        functools.partial(experts_back_kernel, cap, layer, at, consts, own, not above),
         grid=(count + 1,),
         out_shape=[
             jax.ShapeDtypeStruct((shards_dp // 2,) + w_exp.shape[1:], BF16),
@@ -1085,10 +1097,8 @@
             whole(rows_t.shape),
             whole((LANES, LANES)),
             whole((seq_len, LANES)),
-            whole((seq_len, LANES)),
-            whole((width, LANES)),
-            whole((LANES, LANES)),
-        ],
+        ]
+        + [whole(item.shape) for item in above],
         out_specs=[
             pl.BlockSpec(half_shape, lambda e: (0, jnp.maximum(e - 1, 0), 0, 0)),
             whole((seq_len, LANES)),
@@ -1117,8 +1127,8 @@
         ),
         name="experts_backward",
     )(
-        g_all, w_exp, x, gu, rowpos, pos, wd, b_all, small, rows_t, mix, z_prev, grad_prev,
-        sums, mixes,
+        g_all, w_exp, x, gu, rowpos, pos, wd, b_all, small, rows_t, mix, z_prev,
+        *above,
     )
 
 
@@ -1254,31 +1264,32 @@
             )
         )
         if l + 1 < layers:
-            hidden, a_all = join(False, partial, [extra], rows_t, at["attn"] + l + 1, next_id + 1)
+            hidden, a_all = join(
+                False, partial, [extra], rows_t, at["attn"] + l + 1, next_id + 1, APART
+            )
         else:
             hidden_out = lax.psum_scatter(partial, "tensor", scatter_dimension=0, tiled=True)
             extra = lax.dynamic_slice_in_dim(extra, offset, own, 0)
         z_prev = z
         next_id += 2
 
-    below = jnp.zeros((seq_len, LANES), F32)
-    sums = jnp.zeros((width, LANES), F32)
-    mixes = jnp.zeros((LANES, LANES), F32)
+    above = []
     attn_grads, exp_grads = [None] * layers, [None] * layers
     gains_a, gains_m = [None] * layers, [None] * layers
     for l in reversed(range(layers)):
         s = stored[l]
         gw_exp, below, partial, sums, mixes = experts_backward(
             next_id + 2, l, at, consts, own, grad_all, exp_w[l], s["x"], s["gu"], rowpos[l],
-            pos[l], s["wd"], s["b_all"], small, rows_t, s["mix"], s["z_prev"], below, sums, mixes, cap,
-        )
+            pos[l], s["wd"], s["b_all"], small, rows_t, s["mix"], s["z_prev"], above, cap,
+        )
+        above = [below, sums, mixes]
         exp_grads[l] = sum_over_pairs(gw_exp)
         if l + 1 < layers:
             partial, exp_grads[l + 1] = lax.optimization_barrier((partial, exp_grads[l + 1]))
         else:
             partial, hidden_out = lax.optimization_barrier((partial, hidden_out))
         grad_mid, gains_m[l] = join(
-            True, partial, [s["mid"], grad_all], rows_t, at["moe"] + l, next_id
+            True, partial, [s["mid"], grad_all], rows_t, at["moe"] + l, next_id, APART if l > 0 else 0
         )
         partial, gw_attn = attend_backward(
             span_starts, grad_mid, attn_w[l], s["a_all"], s["qkv"], s["o"], s["lse"], heads
@@ -1307,7 +1318,7 @@
         axis=1,
     )
     attn_g, moe_g, router_g, mix_g, cvec_g, cmix_g, qkv_g, outw_g = closing(
-        sums, attn_grads[0], jnp.stack(attn_grads[1:]), consts, layers, cols, next_id
+        sums.astype(BF16), attn_grads[0], jnp.stack(attn_grads[1:]), consts, layers, cols, next_id
     )
     up_grad, down_grad = unpack(exp_grads)
     qkv_g = jnp.swapaxes(qkv_g, 1, 2)

time: 662 us -> 647 us (0.977)
  Pallas kernels: 599 us -> 570 us
  waiting for transfers between devices: 0.28 us -> 16.6 us
    pallas_call x6, Pallas kernels: 291 us -> 260 us  [join(): pl.pallas_call(functools.partial(join_kernel, back, gain_row, nt, pieces,...]
    all_gather x1, waiting for transfers between devices: 0.02 us -> 12.1 us  [shards(): grad_all = lax.all_gather(grad_all, 'tensor', axis=0, tiled=True)]
    pallas_call x2, Pallas kernels: 82.7 us -> 91 us  [experts_backward(): pl.pallas_call(functools.partial(experts_back_kernel, cap, layer, at, con...]
    pallas_call x1, Pallas kernels: 21.2 us -> 14.1 us  [closing(): pl.pallas_call(functools.partial(closing_kernel, ndp, inner, layers, cons...]
  transfers between devices with their start and end apart: 9 -> 9, of which waited for: 0 -> 2; matrix products, arithmetic and copies ran while one was open for 5% -> 5% of each run, Pallas kernels for 90% -> 87%
where the time goes in v7:
time: 647 us; the launch traced here: 643 us
  Pallas kernels  570 us (88%)
  local copies, waits for them, and re-layouts  28.6 us (4%)
  waiting for transfers between devices  16.6 us (3%)
  between operations  14.6 us (2%)
  other arithmetic  10.5 us (2%)
    pallas_call x6, Pallas kernels, join(): pl.pallas_call(functools.partial(join_kernel, back, gain_row, nt, pieces,...  260 us
    pallas_call x2, Pallas kernels, experts_backward(): pl.pallas_call(functools.partial(experts_back_kernel, cap, layer, at, con...  91 us
    pallas_call x2, Pallas kernels, line_exchange(): pl.pallas_call(functools.partial(line_kernel, kind, nt, chunks, lag, extr...  79.5 us
    pallas_call x2, Pallas kernels, experts_forward(): pl.pallas_call(functools.partial(experts_kernel, cap, layer, at, consts),...  51.9 us
    pallas_call x2, Pallas kernels, attend_backward(): pl.pallas_call(functools.partial(attend_back_kernel, heads, spans, PIC),...  39.2 us
    pallas_call x2, Pallas kernels, attend_forward(): pl.pallas_call(functools.partial(attend_kernel, heads, spans, PIC, raw),...  25.5 us
    pallas_call x1, Pallas kernels, closing(): pl.pallas_call(functools.partial(closing_kernel, ndp, inner, layers, cons...  14.1 us
  transfers between devices with their start and end apart: 9, of which 2 were waited for; matrix products, arithmetic and copies ran while one was open for 5% of the time, Pallas kernels for 87%

profile of v7, /device:TPU:0, one launch (start us, length us, event | category | flops | bytes accessed | tf_op | source)
XLA Modules:
  0.0 642.7 jit_solution(3045151853480186894)
XLA Ops:
  10.3 5.0 fusion.11
  15.3 2.8 reshape_squeeze.13
  18.1 2.4 slice_bitcast_fusion
  24.6 2.7 pad_maximum_fusion.1
  29.6 43.0 %line_start.1 = (bf16[4,2,128,768]{3,2,1,0:T(8,128)(2,1)}, bf16[32,24,128]{2,1,0:T(8,128)(2,1)}) custom-call(bf16[2,128,768]{2,1,0:T(8,128)(2,1)} %bitcast.109, bf16[24,128]{1,0:T(8,128)(2,1)} %pad.19.refs_1_), custom_call_target="tpu_custom_call" | custom-call | flops 7864320 | bytes 78643200 | tf_op jit(solution)/shard_map/line_start/pallas_call | solution.py:617
  77.9 13.2 %attend_forward.2 = (bf16[1024,576]{1,0:T(8,128)(2,1)}, bf16[1024,192]{1,0:T(8,128)(2,1)}, f32[1024,3]{1,0:T(8,128)}, bf16[1024,768]{1,0:T(8,128)(2,1)}, bf16[1024,768]{1,0:T(8,128)(2,1)}) custom-call(s32[1,2]{1,0:T(1,128)} %starts_ref.7, bf16[1024,768]{1,0:T(8,128)(2,1)} %bitcast.103, bf16[768,768]{1,0:T(8,128)(2,1)} %all-gather.12.cloned.1.call-done.w_ref, ...), custom_call_target="tpu_custom_call" | custom-call | flops 2013265920 | bytes 4718592 | tf_op jit(solution)/shard_map/attend_forward/pallas_call | solution.py:690
  91.1 48.2 %join.3 = (bf16[32,32,768]{2,1,0:T(8,128)(2,1)}, bf16[32,32,768]{2,1,0:T(8,128)(2,1)}) custom-call(bf16[32,32,768]{2,1,0:T(8,128)(2,1)} %bitcast.106, bf16[32,32,768]{2,1,0:T(8,128)(2,1)} %bitcast.104, f32[48,768]{1,0:T(8,128)} %convert_bitcast_fusion.refs_0_.refs_2_.rows_ref.refs_3_), custom_call_target="tpu_custom_call" | custom-call | flops 7864320 | bytes 78643200 | tf_op jit(solution)/shard_map/join/pallas_call | solution.py:296
  139.3 26.1 %experts_forward.2 = (bf16[8,256,768]{2,1,0:T(8,128)(2,1)}, bf16[8,256,1024]{2,1,0:T(8,128)(2,1)}, f32[1024,128]{1,0:T(8,128)}, f32[1024,128]{1,0:T(8,128)}, bf1...) custom-call(bf16[1024,768]{1,0:T(8,128)(2,1)} %bitcast.156, bf16[8,8,96,1536]{3,2,1,0:T(8,128)(2,1)} %bitcast.151, ...), custom_call_target="tpu_custom_call" | custom-call | flops 11274289152 | bytes 18874368 | tf_op jit(solution)/shard_map/experts_forward/pallas_call | solution.py:862
  165.4 39.0 %join.4 = (bf16[32,32,768]{2,1,0:T(8,128)(2,1)}, bf16[32,32,768]{2,1,0:T(8,128)(2,1)}) custom-call(bf16[32,32,768]{2,1,0:T(8,128)(2,1)} %bitcast.107, bf16[32,32,768]{2,1,0:T(8,128)(2,1)} %bitcast.108, f32[48,768]{1,0:T(8,128)} %convert_bitcast_fusion.refs_0_.refs_2_.rows_ref.refs_3_), custom_call_target="tpu_custom_call" | custom-call | flops 7864320 | bytes 78643200 | tf_op jit(solution)/shard_map/join/pallas_call | solution.py:296
  204.5 12.4 %attend_forward.3 = (bf16[1024,576]{1,0:T(8,128)(2,1)}, bf16[1024,192]{1,0:T(8,128)(2,1)}, f32[1024,3]{1,0:T(8,128)}, bf16[1024,768]{1,0:T(8,128)(2,1)}) custom-call(s32[1,2]{1,0:T(1,128)} %starts_ref.7, bf16[1024,768]{1,0:T(8,128)(2,1)} %bitcast.158, bf16[768,768]{1,0:T(8,128)(2,1)} %all-gather.16.cloned.1.call-done.w_ref), custom_call_target="tpu_custom_call" | custom-call | flops 2013265920 | bytes 4718592 | tf_op jit(solution)/shard_map/attend_forward/pallas_call | solution.py:690
  219.4 40.8 %join.5 = (bf16[32,32,768]{2,1,0:T(8,128)(2,1)}, bf16[32,32,768]{2,1,0:T(8,128)(2,1)}) custom-call(bf16[32,32,768]{2,1,0:T(8,128)(2,1)} %bitcast.105, bf16[32,32,768]{2,1,0:T(8,128)(2,1)} %get-tuple-element.91.refs_1_, f32[48,768]{1,0:T(8,128)} %convert_bitcast_fusion.refs_0_.refs_2_.rows_ref.refs_3_), custom_call_target="tpu_custom_call" | custom-call | flops 7864320 | bytes 78643200 | tf_op jit(solution)/shard_map/join/pallas_call | solution.py:296
  260.3 4.2 all-gather.18.cloned.1.call-done
  264.5 25.8 %experts_forward.3 = (bf16[8,256,768]{2,1,0:T(8,128)(2,1)}, bf16[8,256,1024]{2,1,0:T(8,128)(2,1)}, f32[1024,128]{1,0:T(8,128)}, f32[1024,128]{1,0:T(8,128)}, bf1...) custom-call(bf16[1024,768]{1,0:T(8,128)(2,1)} %bitcast.160, bf16[8,8,96,1536]{3,2,1,0:T(8,128)(2,1)} %bitcast.153, ...), custom_call_target="tpu_custom_call" | custom-call | flops 11274289152 | bytes 18874368 | tf_op jit(solution)/shard_map/experts_forward/pallas_call | solution.py:862
  290.8 12.1 %all-gather.10.cloned.1.call-done.g_ref = bf16[1024,768]{1,0:T(8,128)(2,1)} async-done(((bf16[256,768]{1,0:T(8,128)(2,1)}), bf16[1024,768]{1,0:T(8,128)(2,1)}) %all-gather.10.cloned.1.call-update) | async-done | bytes 1572880 | tf_op jit(solution)/shard_map/all_gather | solution.py:1255
  302.9 40.9 %experts_backward.2 = (bf16[4,8,96,1536]{3,2,1,0:T(8,128)(2,1)}, f32[1024,128]{1,0:T(8,128)}, bf16[1024,768]{1,0:T(8,128)(2,1)}, f32[768,128]{1,0:T(8,128)}, f32[128,128]{1,0:T(8,128)}) custom-call(bf16[1024,768]{1,0:T(8,128)(2,1)} %all-gather.10.cloned.1.call-done.g_ref, bf16[8,8,96,1536]{3,2,1,0:T(8,128)(2,1)} %bitcast.154, ...), custom_call_target="tpu_custom_call" | custom-call | flops 16106127360 | bytes 37748736 | tf_op jit(solution)/shard_map/experts_backward/pallas_call | solution.py:1077
  344.0 40.8 %join_back.3 = (bf16[32,32,768]{2,1,0:T(8,128)(2,1)}, f32[1,768]{1,0:T(1,128)}) custom-call(bf16[32,32,768]{2,1,0:T(8,128)(2,1)} %bitcast.116, bf16[32,32,768]{2,1,0:T(8,128)(2,1)} %get-tuple-element.94.refs_1_, bf16[32,32,768]{2,1,0:T(8,128)(2,1)} %bitcast.112, f32[48,768]{1,0:T(8,128)} %convert_bitcast_fusion.refs_0_.refs_2_.rows_ref.refs_3_), custom_call_target="tpu_custom_call" | custom-call | flops 7864320 | bytes 78643200 | tf_op jit(solution)/shard_map/join_back/pallas_call | solution.py:296
  384.8 19.7 %attend_backward.2 = (bf16[1024,768]{1,0:T(8,128)(2,1)}, bf16[768,768]{1,0:T(8,128)(2,1)}) custom-call(s32[1,2]{1,0:T(1,128)} %starts_ref.7, bf16[1024,768]{1,0:T(8,128)(2,1)} %bitcast.117, bf16[768,768]{1,0:T(8,128)(2,1)} %all-gather.16.cloned.1.call-done.w_ref, bf16[1024,768]{1,0:T(8,128)(2,1)} %bitcast.159, bf16[1024,576]{1,0:T(8,128)(2,1)} %get-tuple-element.104.qkv_ref, ...), custom_call_target="tpu_custom_call" | custom-call | flops 4429185024 | bytes 9437184 | tf_op jit(solution)/shard_map/attend_backward/pallas_call | solution.py:749
  404.6 41.6 %join_back.4 = (bf16[32,32,768]{2,1,0:T(8,128)(2,1)}, f32[1,768]{1,0:T(1,128)}) custom-call(bf16[32,32,768]{2,1,0:T(8,128)(2,1)} %bitcast.120, bf16[32,32,768]{2,1,0:T(8,128)(2,1)} %get-tuple-element.91.refs_1_, bf16[32,32,768]{2,1,0:T(8,128)(2,1)} %get-tuple-element.103.refs_2_, f32[48,768]{1,0:T(8,128)} %convert_bitcast_fusion.refs_0_.refs_2_.rows_ref.refs_3_), custom_call_target="tpu_custom_call" | custom-call | flops 7864320 | bytes 78643200 | tf_op jit(solution)/shard_map/join_back/pallas_call | solution.py:296
  446.2 50.1 %experts_backward.3 = (bf16[4,8,96,1536]{3,2,1,0:T(8,128)(2,1)}, f32[1024,128]{1,0:T(8,128)}, bf16[1024,768]{1,0:T(8,128)(2,1)}, f32[768,128]{1,0:T(8,128)}, f32[128,128]{1,0:T(8,128)}) custom-call(bf16[1024,768]{1,0:T(8,128)(2,1)} %bitcast.113, bf16[8,8,96,1536]{3,2,1,0:T(8,128)(2,1)} %bitcast.152, bf16[8,256,768]{2,1,0:T(8,128)(2,1)} %get-tuple-element.109.x_ref, ...), custom_call_target="tpu_custom_call" | custom-call | flops 16106127360 | bytes 37748736 | tf_op jit(solution)/shard_map/experts_backward/pallas_call | solution.py:1077
  500.1 49.9 %join_back.5 = (bf16[32,32,768]{2,1,0:T(8,128)(2,1)}, f32[1,768]{1,0:T(1,128)}) custom-call(bf16[32,32,768]{2,1,0:T(8,128)(2,1)} %bitcast.115, bf16[32,32,768]{2,1,0:T(8,128)(2,1)} %get-tuple-element.84.refs_1_, bf16[32,32,768]{2,1,0:T(8,128)(2,1)} %get-tuple-element.108.refs_2_, f32[48,768]{1,0:T(8,128)} %convert_bitcast_fusion.refs_0_.refs_2_.rows_ref.refs_3_), custom_call_target="tpu_custom_call" | custom-call | flops 7864320 | bytes 78643200 | tf_op jit(solution)/shard_map/join_back/pallas_call | solution.py:296
  550.0 19.5 %attend_backward.3 = (bf16[1024,768]{1,0:T(8,128)(2,1)}, bf16[768,768]{1,0:T(8,128)(2,1)}) custom-call(s32[1,2]{1,0:T(1,128)} %starts_ref.7, bf16[1024,768]{1,0:T(8,128)(2,1)} %bitcast.118, bf16[768,768]{1,0:T(8,128)(2,1)} %all-gather.12.cloned.1.call-done.w_ref, bf16[1024,768]{1,0:T(8,128)(2,1)} %get-tuple-element.119.a_ref, ...), custom_call_target="tpu_custom_call" | custom-call | flops 4429185024 | bytes 9437184 | tf_op jit(solution)/shard_map/attend_backward/pallas_call | solution.py:749
  569.5 36.6 %line_end.1 = (f32[2,128,768]{2,1,0:T(8,128)}, f32[1,768]{1,0:T(1,128)}, f32[96,768]{1,0:T(8,128)}) custom-call(bf16[4,2,128,768]{3,2,1,0:T(8,128)(2,1)} %bitcast.121, bf16[2,128,768]{2,1,0:T(8,128)(2,1)} %bitcast.110, bf16[4,2,128,768]{3,2,1,0:T(8,128)(2,1)} %bitcast.119, f32[48,768]{1,0:T(8,128)} %convert_bitcast_fusion.refs_0_.refs_2_.rows_ref.refs_3_, ...), custom_call_target="tpu_custom_call" | custom-call | flops 7864320 | bytes 78643200 | tf_op jit(solution)/shard_map/line_end/pallas_call | solution.py:617
  607.8 14.1 %closing.1 = (f32[2,24]{1,0:T(2,128)}, f32[2,24]{1,0:T(2,128)}, f32[12,2,24]{2,1,0:T(2,128)}, f32[12,2,12]{2,1,0:T(2,128)}, f32[2,2,24]{2,1,0:T(2,128)}, /*index...) custom-call(bf16[32,40,128]{2,1,0:T(8,128)(2,1)} %pad_maximum_fusion.2.refs_0_, ...), custom_call_target="tpu_custom_call" | custom-call | tf_op jit(solution)/shard_map/closing/pallas_call | solution.py:165
  621.9 8.1 %unpack.1 = (f32[2,8,96,2,512]{4,3,2,1,0:T(2,128)}, f32[2,8,96,512]{3,2,1,0:T(8,128)}) custom-call(bf16[8,96,1536]{2,1,0:T(8,128)(2,1)} %bitcast.102, bf16[8,96,1536]{2,1,0:T(8,128)(2,1)} %bitcast.101), custom_call_target="tpu_custom_call" | custom-call | tf_op jit(solution)/shard_map/unpack/pallas_call | solution.py:1148
  (132 shorter events, 29.3 us)
Async XLA Ops:
  7.2 70.8 %all-gather.12.cloned.1.call-start = ((), (), s32[]{:S(2)}) async-start(), calls=%async_computation.7 | async-start | bytes 1327104 | tf_op jit(solution)/shard_map/all_gather | solution.py:1227
  10.3 129.1 %all-gather.14.cloned.1.call-start = ((), (), s32[]{:S(2)}) async-start(), calls=%async_computation.8 | async-start | bytes 21233664 | tf_op jit(solution)/shard_map/all_gather | solution.py:1235
  22.1 182.3 %all-gather.16.cloned.1.call-start = ((), (), s32[]{:S(2)}) async-start(), calls=%async_computation.9 | async-start | bytes 1327104 | tf_op jit(solution)/shard_map/all_gather | solution.py:1227
  23.4 241.1 %all-gather.18.cloned.1.call-start = ((), (), s32[]{:S(2)}) async-start(), calls=%async_computation.10 | async-start | bytes 21233664 | tf_op jit(solution)/shard_map/all_gather | solution.py:1235
  27.3 46.3 %copy-start.10 = (s32[2,1024,2]{1,2,0:T(2,128)S(1)}, s32[2,1024,2]{1,2,0:T(2,128)}, u32[]{:S(2)}) copy-start(s32[2,1024,2]{1,2,0:T(2,128)} %param.17) | copy-start | bytes 49156
  27.3 275.6 %all-gather.10.cloned.1.call-start = ((), (), s32[]{:S(2)}) async-start(), calls=%async_computation.4 | async-start | bytes 1966080 | tf_op jit(solution)/shard_map/all_gather | solution.py:1255
  74.0 2.2 copy-start.7
  74.7 2.5 copy-start.2
  216.9 127.1 %reduce-scatter.9.cloned.1.call-start = ((), (), s32[]{:S(2)}) async-start(), calls=%async_computation.5 | async-start | bytes 1966080 | tf_op jit(solution)/shard_map/reduce_scatter | solution.py:1271
  218.0 42.3 %copy-start.3 = (s32[1024,128]{1,0:T(8,128)}, s32[1024,128]{1,0:T(8,128)S(1)}, u32[]{:S(2)}) copy-start(s32[1024,128]{1,0:T(8,128)S(1)} %fusion.5.pos_ref) | copy-start | bytes 1572868
  290.3 209.7 %reduce-scatter.13.cloned.1.call-start = ((), (), s32[]{:S(2)}) async-start(), calls=%async_computation.11 | async-start | bytes 11796480
  343.9 225.6 %reduce-scatter.11.cloned.1.call-start = ((), (), s32[]{:S(2)}) async-start(), calls=%async_computation.6 | async-start | bytes 1327104 | tf_op jit(solution)/shard_map/reduce_scatter | solution.py:1299
  404.6 217.4 %reduce-scatter.15.cloned.1.call-start = ((), (), s32[]{:S(2)}) async-start(), calls=%async_computation.12 | async-start | bytes 11796480
  496.3 1.9 copy-start.5
  569.5 36.6 %copy-start.15 = (f32[1,768]{1,0:T(1,128)S(1)}, f32[1,768]{1,0:T(1,128)}, u32[]{:S(2)}) copy-start(f32[1,768]{1,0:T(1,128)} %get-tuple-element.132) | copy-start | bytes 9220
  569.5 36.6 %copy-start.16 = (f32[1,768]{1,0:T(1,128)S(1)}, f32[1,768]{1,0:T(1,128)}, u32[]{:S(2)}) copy-start(f32[1,768]{1,0:T(1,128)} %get-tuple-element.130) | copy-start | bytes 9220
  569.5 36.6 %copy-start.17 = (f32[1,768]{1,0:T(1,128)S(1)}, f32[1,768]{1,0:T(1,128)}, u32[]{:S(2)}) copy-start(f32[1,768]{1,0:T(1,128)} %get-tuple-element.131) | copy-start | bytes 9220
  621.9 8.1 %copy-start = (f32[2,128,768]{2,1,0:T(8,128)S(1)}, f32[2,128,768]{2,1,0:T(8,128)}, u32[]{:S(2)}) copy-start(f32[2,128,768]{2,1,0:T(8,128)} %get-tuple-element.127) | copy-start | bytes 2359300
  630.0 2.3 copy-start.6
  630.0 3.0 copy-start.20
  630.1 3.6 copy-start.12
  630.1 4.1 copy-start.11
  630.1 4.7 copy-start.18
  630.1 5.3 copy-start.14
  (9 other events, 11.0 us)
Sparse Core Ops, SparseCore 0:
  10.4 26.6 all-gather.11
  39.6 98.6 all-gather.13
  140.1 23.9 all-gather.15
  165.8 98.5 all-gather.17
  265.9 37.0 all-gather.9
  305.1 34.2 reduce-scatter.8
  344.0 93.6 reduce-scatter.12
  441.0 36.7 reduce-scatter.10
  496.4 106.3 reduce-scatter.14

commit v8 on v7

--- a/solution.py
+++ b/solution.py
@@ -23,7 +23,7 @@
 AHEAD = 2
 PIECES = 32
 LAG = 4
-APART = 16000
+APART = 12000
 MIX_STEP = 16
 VMEM_LIMIT = 60 * 1024 * 1024
 

time: 647 us -> 648 us (level)
    pallas_call x6, Pallas kernels: 260 us -> 270 us  [join(): pl.pallas_call(functools.partial(join_kernel, back, gain_row, nt, pieces,...]
  transfers between devices with their start and end apart: 9 -> 9, of which waited for: 2 -> 1; matrix products, arithmetic and copies ran while one was open for 5% -> 5% of each run, Pallas kernels for 87% -> 88%
where the time goes in v8:
time: 648 us; the launch traced here: 644 us
  Pallas kernels  576 us (89%)
  local copies, waits for them, and re-layouts  28.6 us (4%)
  between operations  14.6 us (2%)
  waiting for transfers between devices  10.7 us (2%)
  other arithmetic  10.5 us (2%)
    pallas_call x6, Pallas kernels, join(): pl.pallas_call(functools.partial(join_kernel, back, gain_row, nt, pieces,...  270 us
    pallas_call x2, Pallas kernels, experts_backward(): pl.pallas_call(functools.partial(experts_back_kernel, cap, layer, at, con...  88.5 us
    pallas_call x2, Pallas kernels, line_exchange(): pl.pallas_call(functools.partial(line_kernel, kind, nt, chunks, lag, extr...  79.2 us
    pallas_call x2, Pallas kernels, experts_forward(): pl.pallas_call(functools.partial(experts_kernel, cap, layer, at, consts),...  51.9 us
    pallas_call x2, Pallas kernels, attend_backward(): pl.pallas_call(functools.partial(attend_back_kernel, heads, spans, PIC),...  39.5 us
    pallas_call x2, Pallas kernels, attend_forward(): pl.pallas_call(functools.partial(attend_kernel, heads, spans, PIC, raw),...  25.5 us
    pallas_call x1, Pallas kernels, closing(): pl.pallas_call(functools.partial(closing_kernel, ndp, inner, layers, cons...  14.1 us
  transfers between devices with their start and end apart: 9, of which 1 were waited for; matrix products, arithmetic and copies ran while one was open for 5% of the time, Pallas kernels for 88%

profile of v8, /device:TPU:0, one launch (start us, length us, event | category | flops | bytes accessed | tf_op | source)
XLA Modules:
  0.0 643.7 jit_solution(11567729898689438771)
XLA Ops:
  10.3 5.0 fusion.11
  15.3 2.8 reshape_squeeze.13
  18.1 2.4 slice_bitcast_fusion
  24.6 2.7 pad_maximum_fusion.1
  29.6 43.0 %line_start.1 = (bf16[4,2,128,768]{3,2,1,0:T(8,128)(2,1)}, bf16[32,24,128]{2,1,0:T(8,128)(2,1)}) custom-call(bf16[2,128,768]{2,1,0:T(8,128)(2,1)} %bitcast.109, bf16[24,128]{1,0:T(8,128)(2,1)} %pad.19.refs_1_), custom_call_target="tpu_custom_call" | custom-call | flops 7864320 | bytes 78643200 | tf_op jit(solution)/shard_map/line_start/pallas_call | solution.py:617
  77.9 13.2 %attend_forward.2 = (bf16[1024,576]{1,0:T(8,128)(2,1)}, bf16[1024,192]{1,0:T(8,128)(2,1)}, f32[1024,3]{1,0:T(8,128)}, bf16[1024,768]{1,0:T(8,128)(2,1)}, bf16[1024,768]{1,0:T(8,128)(2,1)}) custom-call(s32[1,2]{1,0:T(1,128)} %starts_ref.7, bf16[1024,768]{1,0:T(8,128)(2,1)} %bitcast.103, bf16[768,768]{1,0:T(8,128)(2,1)} %all-gather.12.cloned.1.call-done.w_ref, ...), custom_call_target="tpu_custom_call" | custom-call | flops 2013265920 | bytes 4718592 | tf_op jit(solution)/shard_map/attend_forward/pallas_call | solution.py:690
  91.1 48.2 %join.3 = (bf16[32,32,768]{2,1,0:T(8,128)(2,1)}, bf16[32,32,768]{2,1,0:T(8,128)(2,1)}) custom-call(bf16[32,32,768]{2,1,0:T(8,128)(2,1)} %bitcast.106, bf16[32,32,768]{2,1,0:T(8,128)(2,1)} %bitcast.104, f32[48,768]{1,0:T(8,128)} %convert_bitcast_fusion.refs_0_.refs_2_.rows_ref.refs_3_), custom_call_target="tpu_custom_call" | custom-call | flops 7864320 | bytes 78643200 | tf_op jit(solution)/shard_map/join/pallas_call | solution.py:296
  139.3 26.1 %experts_forward.2 = (bf16[8,256,768]{2,1,0:T(8,128)(2,1)}, bf16[8,256,1024]{2,1,0:T(8,128)(2,1)}, f32[1024,128]{1,0:T(8,128)}, f32[1024,128]{1,0:T(8,128)}, bf1...) custom-call(bf16[1024,768]{1,0:T(8,128)(2,1)} %bitcast.156, bf16[8,8,96,1536]{3,2,1,0:T(8,128)(2,1)} %bitcast.151, ...), custom_call_target="tpu_custom_call" | custom-call | flops 11274289152 | bytes 18874368 | tf_op jit(solution)/shard_map/experts_forward/pallas_call | solution.py:862
  165.4 41.7 %join.4 = (bf16[32,32,768]{2,1,0:T(8,128)(2,1)}, bf16[32,32,768]{2,1,0:T(8,128)(2,1)}) custom-call(bf16[32,32,768]{2,1,0:T(8,128)(2,1)} %bitcast.107, bf16[32,32,768]{2,1,0:T(8,128)(2,1)} %bitcast.108, f32[48,768]{1,0:T(8,128)} %convert_bitcast_fusion.refs_0_.refs_2_.rows_ref.refs_3_), custom_call_target="tpu_custom_call" | custom-call | flops 7864320 | bytes 78643200 | tf_op jit(solution)/shard_map/join/pallas_call | solution.py:296
  207.2 12.3 %attend_forward.3 = (bf16[1024,576]{1,0:T(8,128)(2,1)}, bf16[1024,192]{1,0:T(8,128)(2,1)}, f32[1024,3]{1,0:T(8,128)}, bf16[1024,768]{1,0:T(8,128)(2,1)}) custom-call(s32[1,2]{1,0:T(1,128)} %starts_ref.7, bf16[1024,768]{1,0:T(8,128)(2,1)} %bitcast.158, bf16[768,768]{1,0:T(8,128)(2,1)} %all-gather.16.cloned.1.call-done.w_ref), custom_call_target="tpu_custom_call" | custom-call | flops 2013265920 | bytes 4718592 | tf_op jit(solution)/shard_map/attend_forward/pallas_call | solution.py:690
  222.1 44.0 %join.5 = (bf16[32,32,768]{2,1,0:T(8,128)(2,1)}, bf16[32,32,768]{2,1,0:T(8,128)(2,1)}) custom-call(bf16[32,32,768]{2,1,0:T(8,128)(2,1)} %bitcast.105, bf16[32,32,768]{2,1,0:T(8,128)(2,1)} %get-tuple-element.91.refs_1_, f32[48,768]{1,0:T(8,128)} %convert_bitcast_fusion.refs_0_.refs_2_.rows_ref.refs_3_), custom_call_target="tpu_custom_call" | custom-call | flops 7864320 | bytes 78643200 | tf_op jit(solution)/shard_map/join/pallas_call | solution.py:296
  266.2 25.8 %experts_forward.3 = (bf16[8,256,768]{2,1,0:T(8,128)(2,1)}, bf16[8,256,1024]{2,1,0:T(8,128)(2,1)}, f32[1024,128]{1,0:T(8,128)}, f32[1024,128]{1,0:T(8,128)}, bf1...) custom-call(bf16[1024,768]{1,0:T(8,128)(2,1)} %bitcast.160, bf16[8,8,96,1536]{3,2,1,0:T(8,128)(2,1)} %bitcast.153, ...), custom_call_target="tpu_custom_call" | custom-call | flops 11274289152 | bytes 18874368 | tf_op jit(solution)/shard_map/experts_forward/pallas_call | solution.py:862
  292.5 10.5 %all-gather.10.cloned.1.call-done.g_ref = bf16[1024,768]{1,0:T(8,128)(2,1)} async-done(((bf16[256,768]{1,0:T(8,128)(2,1)}), bf16[1024,768]{1,0:T(8,128)(2,1)}) %all-gather.10.cloned.1.call-update) | async-done | bytes 1572880 | tf_op jit(solution)/shard_map/all_gather | solution.py:1255
  303.0 40.9 %experts_backward.2 = (bf16[4,8,96,1536]{3,2,1,0:T(8,128)(2,1)}, f32[1024,128]{1,0:T(8,128)}, bf16[1024,768]{1,0:T(8,128)(2,1)}, f32[768,128]{1,0:T(8,128)}, f32[128,128]{1,0:T(8,128)}) custom-call(bf16[1024,768]{1,0:T(8,128)(2,1)} %all-gather.10.cloned.1.call-done.g_ref, bf16[8,8,96,1536]{3,2,1,0:T(8,128)(2,1)} %bitcast.154, ...), custom_call_target="tpu_custom_call" | custom-call | flops 16106127360 | bytes 37748736 | tf_op jit(solution)/shard_map/experts_backward/pallas_call | solution.py:1077
  344.0 43.0 %join_back.3 = (bf16[32,32,768]{2,1,0:T(8,128)(2,1)}, f32[1,768]{1,0:T(1,128)}) custom-call(bf16[32,32,768]{2,1,0:T(8,128)(2,1)} %bitcast.116, bf16[32,32,768]{2,1,0:T(8,128)(2,1)} %get-tuple-element.94.refs_1_, bf16[32,32,768]{2,1,0:T(8,128)(2,1)} %bitcast.112, f32[48,768]{1,0:T(8,128)} %convert_bitcast_fusion.refs_0_.refs_2_.rows_ref.refs_3_), custom_call_target="tpu_custom_call" | custom-call | flops 7864320 | bytes 78643200 | tf_op jit(solution)/shard_map/join_back/pallas_call | solution.py:296
  387.0 20.0 %attend_backward.2 = (bf16[1024,768]{1,0:T(8,128)(2,1)}, bf16[768,768]{1,0:T(8,128)(2,1)}) custom-call(s32[1,2]{1,0:T(1,128)} %starts_ref.7, bf16[1024,768]{1,0:T(8,128)(2,1)} %bitcast.117, bf16[768,768]{1,0:T(8,128)(2,1)} %all-gather.16.cloned.1.call-done.w_ref, bf16[1024,768]{1,0:T(8,128)(2,1)} %bitcast.159, bf16[1024,576]{1,0:T(8,128)(2,1)} %get-tuple-element.104.qkv_ref, ...), custom_call_target="tpu_custom_call" | custom-call | flops 4429185024 | bytes 9437184 | tf_op jit(solution)/shard_map/attend_backward/pallas_call | solution.py:749
  407.1 43.0 %join_back.4 = (bf16[32,32,768]{2,1,0:T(8,128)(2,1)}, f32[1,768]{1,0:T(1,128)}) custom-call(bf16[32,32,768]{2,1,0:T(8,128)(2,1)} %bitcast.120, bf16[32,32,768]{2,1,0:T(8,128)(2,1)} %get-tuple-element.91.refs_1_, bf16[32,32,768]{2,1,0:T(8,128)(2,1)} %get-tuple-element.103.refs_2_, f32[48,768]{1,0:T(8,128)} %convert_bitcast_fusion.refs_0_.refs_2_.rows_ref.refs_3_), custom_call_target="tpu_custom_call" | custom-call | flops 7864320 | bytes 78643200 | tf_op jit(solution)/shard_map/join_back/pallas_call | solution.py:296
  450.1 47.6 %experts_backward.3 = (bf16[4,8,96,1536]{3,2,1,0:T(8,128)(2,1)}, f32[1024,128]{1,0:T(8,128)}, bf16[1024,768]{1,0:T(8,128)(2,1)}, f32[768,128]{1,0:T(8,128)}, f32[128,128]{1,0:T(8,128)}) custom-call(bf16[1024,768]{1,0:T(8,128)(2,1)} %bitcast.113, bf16[8,8,96,1536]{3,2,1,0:T(8,128)(2,1)} %bitcast.152, bf16[8,256,768]{2,1,0:T(8,128)(2,1)} %get-tuple-element.109.x_ref, ...), custom_call_target="tpu_custom_call" | custom-call | flops 16106127360 | bytes 37748736 | tf_op jit(solution)/shard_map/experts_backward/pallas_call | solution.py:1077
  499.6 2.0 convert_add_fusion
  501.6 49.7 %join_back.5 = (bf16[32,32,768]{2,1,0:T(8,128)(2,1)}, f32[1,768]{1,0:T(1,128)}) custom-call(bf16[32,32,768]{2,1,0:T(8,128)(2,1)} %bitcast.115, bf16[32,32,768]{2,1,0:T(8,128)(2,1)} %get-tuple-element.84.refs_1_, bf16[32,32,768]{2,1,0:T(8,128)(2,1)} %get-tuple-element.108.refs_2_, f32[48,768]{1,0:T(8,128)} %convert_bitcast_fusion.refs_0_.refs_2_.rows_ref.refs_3_), custom_call_target="tpu_custom_call" | custom-call | flops 7864320 | bytes 78643200 | tf_op jit(solution)/shard_map/join_back/pallas_call | solution.py:296
  551.2 19.5 %attend_backward.3 = (bf16[1024,768]{1,0:T(8,128)(2,1)}, bf16[768,768]{1,0:T(8,128)(2,1)}) custom-call(s32[1,2]{1,0:T(1,128)} %starts_ref.7, bf16[1024,768]{1,0:T(8,128)(2,1)} %bitcast.118, bf16[768,768]{1,0:T(8,128)(2,1)} %all-gather.12.cloned.1.call-done.w_ref, bf16[1024,768]{1,0:T(8,128)(2,1)} %get-tuple-element.119.a_ref, ...), custom_call_target="tpu_custom_call" | custom-call | flops 4429185024 | bytes 9437184 | tf_op jit(solution)/shard_map/attend_backward/pallas_call | solution.py:749
  570.8 36.3 %line_end.1 = (f32[2,128,768]{2,1,0:T(8,128)}, f32[1,768]{1,0:T(1,128)}, f32[96,768]{1,0:T(8,128)}) custom-call(bf16[4,2,128,768]{3,2,1,0:T(8,128)(2,1)} %bitcast.121, bf16[2,128,768]{2,1,0:T(8,128)(2,1)} %bitcast.110, bf16[4,2,128,768]{3,2,1,0:T(8,128)(2,1)} %bitcast.119, f32[48,768]{1,0:T(8,128)} %convert_bitcast_fusion.refs_0_.refs_2_.rows_ref.refs_3_, ...), custom_call_target="tpu_custom_call" | custom-call | flops 7864320 | bytes 78643200 | tf_op jit(solution)/shard_map/line_end/pallas_call | solution.py:617
  608.7 14.1 %closing.1 = (f32[2,24]{1,0:T(2,128)}, f32[2,24]{1,0:T(2,128)}, f32[12,2,24]{2,1,0:T(2,128)}, f32[12,2,12]{2,1,0:T(2,128)}, f32[2,2,24]{2,1,0:T(2,128)}, /*index...) custom-call(bf16[32,40,128]{2,1,0:T(8,128)(2,1)} %pad_maximum_fusion.2.refs_0_, ...), custom_call_target="tpu_custom_call" | custom-call | tf_op jit(solution)/shard_map/closing/pallas_call | solution.py:165
  622.9 8.1 %unpack.1 = (f32[2,8,96,2,512]{4,3,2,1,0:T(2,128)}, f32[2,8,96,512]{3,2,1,0:T(8,128)}) custom-call(bf16[8,96,1536]{2,1,0:T(8,128)(2,1)} %bitcast.102, bf16[8,96,1536]{2,1,0:T(8,128)(2,1)} %bitcast.101), custom_call_target="tpu_custom_call" | custom-call | tf_op jit(solution)/shard_map/unpack/pallas_call | solution.py:1148
  (132 shorter events, 27.4 us)
Async XLA Ops:
  7.2 70.8 %all-gather.12.cloned.1.call-start = ((), (), s32[]{:S(2)}) async-start(), calls=%async_computation.7 | async-start | bytes 1327104 | tf_op jit(solution)/shard_map/all_gather | solution.py:1227
  10.3 129.1 %all-gather.14.cloned.1.call-start = ((), (), s32[]{:S(2)}) async-start(), calls=%async_computation.8 | async-start | bytes 21233664 | tf_op jit(solution)/shard_map/all_gather | solution.py:1235
  22.1 185.0 %all-gather.16.cloned.1.call-start = ((), (), s32[]{:S(2)}) async-start(), calls=%async_computation.9 | async-start | bytes 1327104 | tf_op jit(solution)/shard_map/all_gather | solution.py:1227
  23.4 242.8 %all-gather.18.cloned.1.call-start = ((), (), s32[]{:S(2)}) async-start(), calls=%async_computation.10 | async-start | bytes 21233664 | tf_op jit(solution)/shard_map/all_gather | solution.py:1235
  27.3 46.3 %copy-start.10 = (s32[2,1024,2]{1,2,0:T(2,128)S(1)}, s32[2,1024,2]{1,2,0:T(2,128)}, u32[]{:S(2)}) copy-start(s32[2,1024,2]{1,2,0:T(2,128)} %param.17) | copy-start | bytes 49156
  27.3 275.7 %all-gather.10.cloned.1.call-start = ((), (), s32[]{:S(2)}) async-start(), calls=%async_computation.4 | async-start | bytes 1966080 | tf_op jit(solution)/shard_map/all_gather | solution.py:1255
  74.0 2.2 copy-start.7
  74.7 2.5 copy-start.2
  219.5 124.5 %reduce-scatter.9.cloned.1.call-start = ((), (), s32[]{:S(2)}) async-start(), calls=%async_computation.5 | async-start | bytes 1966080 | tf_op jit(solution)/shard_map/reduce_scatter | solution.py:1271
  220.6 45.5 %copy-start.3 = (s32[1024,128]{1,0:T(8,128)}, s32[1024,128]{1,0:T(8,128)S(1)}, u32[]{:S(2)}) copy-start(s32[1024,128]{1,0:T(8,128)S(1)} %fusion.5.pos_ref) | copy-start | bytes 1572868
  292.0 209.5 %reduce-scatter.13.cloned.1.call-start = ((), (), s32[]{:S(2)}) async-start(), calls=%async_computation.11 | async-start | bytes 11796480
  343.9 226.8 %reduce-scatter.11.cloned.1.call-start = ((), (), s32[]{:S(2)}) async-start(), calls=%async_computation.6 | async-start | bytes 1327104 | tf_op jit(solution)/shard_map/reduce_scatter | solution.py:1299
  407.0 215.9 %reduce-scatter.15.cloned.1.call-start = ((), (), s32[]{:S(2)}) async-start(), calls=%async_computation.12 | async-start | bytes 11796480
  497.7 1.9 copy-start.5
  570.8 36.3 %copy-start.15 = (f32[1,768]{1,0:T(1,128)S(1)}, f32[1,768]{1,0:T(1,128)}, u32[]{:S(2)}) copy-start(f32[1,768]{1,0:T(1,128)} %get-tuple-element.132) | copy-start | bytes 9220
  570.8 36.3 %copy-start.16 = (f32[1,768]{1,0:T(1,128)S(1)}, f32[1,768]{1,0:T(1,128)}, u32[]{:S(2)}) copy-start(f32[1,768]{1,0:T(1,128)} %get-tuple-element.130) | copy-start | bytes 9220
  570.8 36.3 %copy-start.17 = (f32[1,768]{1,0:T(1,128)S(1)}, f32[1,768]{1,0:T(1,128)}, u32[]{:S(2)}) copy-start(f32[1,768]{1,0:T(1,128)} %get-tuple-element.131) | copy-start | bytes 9220
  622.9 8.1 %copy-start = (f32[2,128,768]{2,1,0:T(8,128)S(1)}, f32[2,128,768]{2,1,0:T(8,128)}, u32[]{:S(2)}) copy-start(f32[2,128,768]{2,1,0:T(8,128)} %get-tuple-element.127) | copy-start | bytes 2359300
  631.0 2.3 copy-start.6
  631.0 3.0 copy-start.20
  631.0 3.6 copy-start.12
  631.0 4.1 copy-start.11
  631.1 4.7 copy-start.18
  631.1 5.3 copy-start.14
  (9 other events, 11.0 us)
Sparse Core Ops, SparseCore 0:
  10.4 26.6 all-gather.11
  39.6 98.6 all-gather.13
  140.1 23.9 all-gather.15
  165.8 98.5 all-gather.17
  265.9 37.0 all-gather.9
  305.1 34.2 reduce-scatter.8
  344.0 93.7 reduce-scatter.12
  441.0 36.7 reduce-scatter.10
  497.9 106.5 reduce-scatter.14
